TPU v7x, 32 devices: a whole 2x2x4 slice. The times are simulated.
32 devices in a mesh: dp: 8 (over y, x, core), mp: 4 (over z).
Axes of the slice: x: 2, y: 2, z: 4, core: 2. Of those that a mesh axis runs over, the one named last changes fastest.
Arguments:
- tokens: bfloat16 [2, 8704, 1024], P(None, ('dp', 'mp')), may hold values from -6 to 6
- seg_ids: int32 [2, 8704], P(None, 'dp'), may hold values from 0 to 1, as said below
- qkv_weight: bfloat16 [3, 1024, 1024], P(None, 'dp', 'mp'), may hold values from -0.25 to 0.25
- qv_bias: bfloat16 [2, 1024], P(None, ('mp', 'dp')), may hold values from -2 to 2
- out_weight: bfloat16 [1024, 1024], P(('mp', 'dp')), may hold values from -0.1875 to 0.1875
- up_weight: bfloat16 [1024, 4096], P('dp', 'mp'), may hold values from -0.1875 to 0.1875
- up_bias: bfloat16 [4096], P(('mp', 'dp')), may hold values from -3 to 3
- down_weight: bfloat16 [4096, 1024], P(('mp', 'dp')), may hold values from -0.09375 to 0.09375
- norm_gain: bfloat16 [4, 1024], P(None, 'dp'), may hold values from 0.099609375 to 1.8984375
- norm_bias: bfloat16 [4, 1024], P(None, 'dp'), may hold values from -2 to 2
- branch_bias: bfloat16 [2, 1024], P(None, 'dp'), may hold values from -3 to 3
- out_grad: bfloat16 [2, 8704, 1024], P(None, ('dp', 'mp')), may hold values from -6 to 6
Outputs:
- layer_out: bfloat16 [2, 8704, 1024], P(None, ('dp', 'mp'))
- input_grad: float32 [2, 8704, 1024], P(None, ('dp', 'mp'))
- qkv_grad: float32 [3, 1024, 1024], P(None, 'dp', 'mp')
- qv_bias_grad: float32 [2, 1024], P(None, ('mp', 'dp'))
- out_weight_grad: float32 [1024, 1024], P(('mp', 'dp'))
- up_weight_grad: float32 [1024, 4096], P('dp', 'mp')
- up_bias_grad: float32 [4096], P(('mp', 'dp'))
- down_weight_grad: float32 [4096, 1024], P(('mp', 'dp'))
- norm_gain_grad: float32 [4, 1024], P(None, 'dp')
- norm_bias_grad: float32 [4, 1024], P(None, 'dp')
- branch_bias_grad: float32 [2, 1024], P(None, 'dp')
Inputs may be any that keep to these rules, and one draw needn't show every extreme that they name: `seg_ids`: each packed row of 1088 tokens holds 1 items numbered 0 upward in order, each of 1024 image codes plus 5 to 64 caption tokens; the rest of the row is padding numbered 1.
All inputs are finite; a program needn't handle non-finite values.
Results may differ from a plain program's by a relative error of at most 0.019.
Values may be sent and summed in bfloat16 or wider, within the bound.
A program may use at most 192 MiB of HBM per device.

v0:
```python
import math

import jax
import jax.numpy as jnp
from jax import lax
from jax.sharding import PartitionSpec as P

HEAD_DIM = 64


ALPHA = 32.0
EPS = 1e-05


def normalize(value, gain, shift):
    mean = jnp.mean(value, axis=-1, keepdims=True)
    centred = value - mean
    variance = jnp.mean(centred * centred, axis=-1, keepdims=True)
    return centred * lax.rsqrt(variance + EPS) * gain + shift


def normalize_back(value, gain, grad):
    mean = jnp.mean(value, axis=-1, keepdims=True)
    centred = value - mean
    variance = jnp.mean(centred * centred, axis=-1, keepdims=True)
    inverse = lax.rsqrt(variance + EPS)
    unit = centred * inverse
    scaled = grad * gain
    grad_in = inverse * (
        scaled
        - jnp.mean(scaled, axis=-1, keepdims=True)
        - unit * jnp.mean(scaled * unit, axis=-1, keepdims=True)
    )
    return (grad_in, jnp.sum(grad * unit, axis=0), jnp.sum(grad, axis=0))


def gelu_exact(value):
    return jax.nn.gelu(value, approximate=False)


def block_mask(seg_row, start, block):
    query_pos = start + jnp.arange(block, dtype=jnp.int32)
    key_pos = jnp.arange(seg_row.shape[0], dtype=jnp.int32)
    seg_block = seg_row[start : start + block]
    return (seg_block[:, None] == seg_row[None, :]) & (key_pos[None, :] <= query_pos[:, None])


def attend_forward(queries, keys, values, seg_row):
    length = queries.shape[0]
    block = length // 4
    results = []
    sums = []
    for part_index in range(4):
        start = part_index * block
        q_block = queries[start : start + block]
        allowed = block_mask(seg_row, start, block)[None]
        scores = jnp.einsum("qhd,khd->hqk", q_block, keys, preferred_element_type=jnp.float32)
        masked = jnp.where(allowed, scores, -1e30)
        top = jnp.max(masked, axis=-1, keepdims=True)
        expo = jnp.exp(ALPHA * (masked - top))
        total = jnp.sum(expo, axis=-1, keepdims=True)
        probs = (expo / total).astype(jnp.bfloat16)
        results.append(
            jnp.einsum("hqk,khd->qhd", probs, values, preferred_element_type=jnp.float32)
        )
        sums.append(ALPHA * top + jnp.log(total))
    return (jnp.concatenate(results, axis=0), jnp.concatenate(sums, axis=1))


def attend_backward(queries, keys, values, seg_row, log_sums, grad_out):
    length = queries.shape[0]
    block = length // 4
    grad_queries = []
    grad_keys = jnp.zeros(keys.shape, jnp.float32)
    grad_values = jnp.zeros(values.shape, jnp.float32)
    for part_index in range(4):
        start = part_index * block
        q_block = queries[start : start + block]
        g_block = grad_out[start : start + block]
        allowed = block_mask(seg_row, start, block)[None]
        scores = jnp.einsum("qhd,khd->hqk", q_block, keys, preferred_element_type=jnp.float32)
        masked = jnp.where(allowed, scores, -1e30)
        probs_full = jnp.exp(ALPHA * masked - log_sums[:, start : start + block])
        probs = probs_full.astype(jnp.bfloat16)
        grad_probs = jnp.einsum("qhd,khd->hqk", g_block, values, preferred_element_type=jnp.float32)
        delta = jnp.sum(probs_full * grad_probs, axis=-1, keepdims=True)
        grad_scores = (ALPHA * probs_full * (grad_probs - delta)).astype(jnp.bfloat16)
        grad_queries.append(
            jnp.einsum("hqk,khd->qhd", grad_scores, keys, preferred_element_type=jnp.float32)
        )
        grad_keys = grad_keys + jnp.einsum(
            "hqk,qhd->khd", grad_scores, q_block, preferred_element_type=jnp.float32
        )
        grad_values = grad_values + jnp.einsum(
            "hqk,qhd->khd", probs, g_block, preferred_element_type=jnp.float32
        )
    return (jnp.concatenate(grad_queries, axis=0), grad_keys, grad_values)


def on_device(
    tokens,
    seg_ids,
    qkv_weight,
    qv_bias,
    out_weight,
    up_weight,
    up_bias,
    down_weight,
    norm_gain,
    norm_bias,
    branch_bias,
    out_grad,
):

    def fetch():
        return (
            lax.all_gather(qkv_weight, "dp", axis=1, tiled=True),
            lax.all_gather(qv_bias, "dp", axis=1, tiled=True),
            lax.all_gather(out_weight, "dp", axis=0, tiled=True),
            lax.all_gather(up_weight, "dp", axis=0, tiled=True),
            lax.all_gather(up_bias, "dp", axis=0, tiled=True),
            lax.all_gather(down_weight, "dp", axis=0, tiled=True),
            lax.all_gather(norm_gain, "dp", axis=1, tiled=True),
            lax.all_gather(norm_bias, "dp", axis=1, tiled=True),
            lax.all_gather(branch_bias, "dp", axis=1, tiled=True),
        )

    scale = 1.0 / (ALPHA * math.sqrt(HEAD_DIM))
    batches = tokens.shape[0]
    length = seg_ids.shape[1]
    share = length // lax.axis_size("mp")
    saved = []
    outputs = []
    for step in range(batches):
        weights = fetch()
        qkv, qv_b, w_out, w_up, b_up, w_down, gains, shifts, branch_b = weights
        gains = gains.astype(jnp.float32)
        shifts = shifts.astype(jnp.float32)
        branch_b = branch_b.astype(jnp.float32)
        qv_b = qv_b.astype(jnp.float32)
        x_rows = tokens[step].astype(jnp.float32)
        seg_row = seg_ids[step]
        normed = normalize(x_rows, gains[0], shifts[0]).astype(jnp.bfloat16)
        hidden_in = lax.all_gather(normed, "mp", axis=0, tiled=True)
        queries = (
            (jnp.dot(hidden_in, qkv[0], preferred_element_type=jnp.float32) + qv_b[0]) * scale
        ).astype(jnp.bfloat16)
        keys = jnp.dot(hidden_in, qkv[1], preferred_element_type=jnp.float32).astype(jnp.bfloat16)
        values = (jnp.dot(hidden_in, qkv[2], preferred_element_type=jnp.float32) + qv_b[1]).astype(
            jnp.bfloat16
        )
        heads = queries.shape[1] // HEAD_DIM
        q_heads = queries.reshape(length, heads, HEAD_DIM)
        k_heads = keys.reshape(length, heads, HEAD_DIM)
        v_heads = values.reshape(length, heads, HEAD_DIM)
        attended, log_sums = attend_forward(q_heads, k_heads, v_heads, seg_row)
        mixed = attended.reshape(length, heads * HEAD_DIM).astype(jnp.bfloat16)

        def out_term(start, count, mixed=mixed, w_out=w_out):
            return jnp.dot(mixed, w_out, preferred_element_type=jnp.float32)

        branch = (
            lax.psum_scatter(
                out_term(jnp.int32(0), lax.axis_size("mp") * share).astype(jnp.bfloat16),
                "mp",
                scatter_dimension=0,
                tiled=True,
            ).astype(jnp.float32)
            + branch_b[0]
        )
        middle = x_rows + normalize(branch, gains[1], shifts[1])
        normed_two = normalize(middle, gains[2], shifts[2]).astype(jnp.bfloat16)
        hidden_two = lax.all_gather(normed_two, "mp", axis=0, tiled=True)
        pre = jnp.dot(hidden_two, w_up, preferred_element_type=jnp.float32) + b_up.astype(
            jnp.float32
        )
        act = gelu_exact(pre).astype(jnp.bfloat16)

        def ffn_term(start, count, act=act, w_down=w_down):
            return jnp.dot(act, w_down, preferred_element_type=jnp.float32)

        ffn_out = (
            lax.psum_scatter(
                ffn_term(jnp.int32(0), lax.axis_size("mp") * share).astype(jnp.bfloat16),
                "mp",
                scatter_dimension=0,
                tiled=True,
            ).astype(jnp.float32)
            + branch_b[1]
        )
        outputs.append((middle + normalize(ffn_out, gains[3], shifts[3])).astype(jnp.bfloat16))
        saved.append(
            (
                x_rows,
                hidden_in,
                q_heads,
                k_heads,
                v_heads,
                log_sums,
                mixed,
                branch,
                middle,
                hidden_two,
                pre,
                act,
                ffn_out,
            )
        )
    grad_inputs = []
    totals = None
    for step in range(batches):
        weights = fetch()
        qkv, qv_b, w_out, w_up, b_up, w_down, gains, shifts, branch_b = weights
        gains = gains.astype(jnp.float32)
        (
            x_rows,
            hidden_in,
            q_heads,
            k_heads,
            v_heads,
            log_sums,
            mixed,
            branch,
            middle,
            hidden_two,
            pre,
            act,
            ffn_out,
        ) = saved[step]
        seg_row = seg_ids[step]
        heads = q_heads.shape[1]
        grad_y = out_grad[step].astype(jnp.float32)
        grad_f, dgain_three, dshift_three = normalize_back(ffn_out, gains[3], grad_y)
        grad_f = grad_f.astype(jnp.bfloat16)
        dbranch_one = jnp.sum(grad_f.astype(jnp.float32), axis=0)
        pull = jax.vjp(gelu_exact, pre)[1]
        grad_f_all = lax.all_gather(grad_f, "mp", axis=0, tiled=True)
        dw_down = jnp.einsum("tf,td->fd", act, grad_f_all, preferred_element_type=jnp.float32)
        grad_act = jnp.einsum("td,fd->tf", grad_f_all, w_down, preferred_element_type=jnp.float32)
        grad_pre = pull(grad_act)[0].astype(jnp.bfloat16)
        dup_bias = jnp.sum(grad_pre.astype(jnp.float32), axis=0)
        dw_up = jnp.einsum("td,tf->df", hidden_two, grad_pre, preferred_element_type=jnp.float32)

        def ffn_back(start, count, grad_pre=grad_pre, w_up=w_up):
            return jnp.einsum("tf,df->td", grad_pre, w_up, preferred_element_type=jnp.float32)

        grad_norm_two = lax.psum_scatter(
            ffn_back(jnp.int32(0), lax.axis_size("mp") * share).astype(jnp.bfloat16),
            "mp",
            scatter_dimension=0,
            tiled=True,
        ).astype(jnp.float32)
        back_two, dgain_two, dshift_two = normalize_back(middle, gains[2], grad_norm_two)
        grad_mid = grad_y + back_two
        grad_branch, dgain_one, dshift_one = normalize_back(branch, gains[1], grad_mid)
        grad_branch = grad_branch.astype(jnp.bfloat16)
        dbranch_zero = jnp.sum(grad_branch.astype(jnp.float32), axis=0)
        grad_branch_all = lax.all_gather(grad_branch, "mp", axis=0, tiled=True)
        dw_out = jnp.einsum("tc,td->cd", mixed, grad_branch_all, preferred_element_type=jnp.float32)
        grad_mixed = jnp.einsum(
            "td,cd->tc", grad_branch_all, w_out, preferred_element_type=jnp.float32
        ).astype(jnp.bfloat16)
        grad_q, grad_k, grad_v = attend_backward(
            q_heads,
            k_heads,
            v_heads,
            seg_row,
            log_sums,
            grad_mixed.reshape(length, heads, HEAD_DIM),
        )
        grad_q = grad_q.reshape(length, heads * HEAD_DIM).astype(jnp.bfloat16)
        grad_k = grad_k.reshape(length, heads * HEAD_DIM).astype(jnp.bfloat16)
        grad_v = grad_v.reshape(length, heads * HEAD_DIM).astype(jnp.bfloat16)
        dw_qkv = jnp.stack(
            [
                scale
                * jnp.einsum("td,tc->dc", hidden_in, grad_q, preferred_element_type=jnp.float32),
                jnp.einsum("td,tc->dc", hidden_in, grad_k, preferred_element_type=jnp.float32),
                jnp.einsum("td,tc->dc", hidden_in, grad_v, preferred_element_type=jnp.float32),
            ]
        )
        dqv_bias = jnp.stack(
            [
                scale * jnp.sum(grad_q.astype(jnp.float32), axis=0),
                jnp.sum(grad_v.astype(jnp.float32), axis=0),
            ]
        )

        def attn_back(start, count, grad_q=grad_q, grad_k=grad_k, grad_v=grad_v, qkv=qkv):
            term = scale * jnp.einsum(
                "tc,dc->td", grad_q, qkv[0], preferred_element_type=jnp.float32
            )
            term = term + jnp.einsum(
                "tc,dc->td", grad_k, qkv[1], preferred_element_type=jnp.float32
            )
            return term + jnp.einsum(
                "tc,dc->td", grad_v, qkv[2], preferred_element_type=jnp.float32
            )

        grad_norm_one = lax.psum_scatter(
            attn_back(jnp.int32(0), lax.axis_size("mp") * share).astype(jnp.bfloat16),
            "mp",
            scatter_dimension=0,
            tiled=True,
        ).astype(jnp.float32)
        back_one, dgain_zero, dshift_zero = normalize_back(x_rows, gains[0], grad_norm_one)
        grad_inputs.append(grad_mid + back_one)
        local = (
            dw_qkv,
            dqv_bias,
            dw_out,
            dw_up,
            dup_bias,
            dw_down,
            jnp.stack([dgain_zero, dgain_one, dgain_two, dgain_three]),
            jnp.stack([dshift_zero, dshift_one, dshift_two, dshift_three]),
            jnp.stack([dbranch_zero, dbranch_one]),
        )
        local = (
            lax.psum_scatter(local[0], "dp", scatter_dimension=1, tiled=True),
            lax.psum_scatter(local[1], "dp", scatter_dimension=1, tiled=True),
            lax.psum_scatter(local[2], "dp", scatter_dimension=0, tiled=True),
            lax.psum_scatter(local[3], "dp", scatter_dimension=0, tiled=True),
            lax.psum_scatter(local[4], "dp", scatter_dimension=0, tiled=True),
            lax.psum_scatter(local[5], "dp", scatter_dimension=0, tiled=True),
            lax.psum_scatter(local[6], "dp", scatter_dimension=1, tiled=True),
            lax.psum_scatter(local[7], "dp", scatter_dimension=1, tiled=True),
            lax.psum_scatter(local[8], "dp", scatter_dimension=1, tiled=True),
        )
        totals = (
            local if totals is None else tuple((left + right for left, right in zip(totals, local)))
        )
    vectors = lax.psum((totals[6], totals[7], totals[8]), "mp")
    return (
        jnp.stack(outputs),
        jnp.stack(grad_inputs),
        totals[0],
        totals[1],
        totals[2],
        totals[3],
        totals[4],
        totals[5],
        vectors[0],
        vectors[1],
        vectors[2],
    )


def solution(mesh):
    in_specs = (
        P(None, ("dp", "mp"), None),
        P(None, "dp"),
        P(None, "dp", "mp"),
        P(None, ("mp", "dp")),
        P(("mp", "dp"), None),
        P("dp", "mp"),
        P(("mp", "dp")),
        P(("mp", "dp"), None),
        P(None, "dp"),
        P(None, "dp"),
        P(None, "dp"),
        P(None, ("dp", "mp"), None),
    )
    out_specs = (
        P(None, ("dp", "mp"), None),
        P(None, ("dp", "mp"), None),
        P(None, "dp", "mp"),
        P(None, ("mp", "dp")),
        P(("mp", "dp"), None),
        P("dp", "mp"),
        P(("mp", "dp")),
        P(("mp", "dp"), None),
        P(None, "dp"),
        P(None, "dp"),
        P(None, "dp"),
    )
    return jax.shard_map(
        on_device, mesh=mesh, in_specs=in_specs, out_specs=out_specs, check_vma=False
    )
```

profile of v0, /device:TPU:1, one launch (start us, length us, event | category | flops | bytes accessed | tf_op | source)
XLA Modules:
  0.0 1328.2 jit_solution(9125537895247549174)
XLA Ops:
  8.0 10.3 all_gather.34
  18.3 8.7 all_gather.35
  34.4 7.9 all-gather
  42.5 10.7 all_gather.75
  57.1 31.1 %all-gather.24.cloned.1.call-done = bf16[1088,1024]{1,0:T(8,128)(2,1)} async-done(((bf16[272,1024]{1,0:T(8,128)(2,1)}), bf16[1088,1024]{1,0:T(8,128)(2,1)}) %all-gather.24.cloned.1.call-update) | async-done | bytes 2228240 | tf_op jit(solution)/shard_map/all_gather | solution.py:144
  101.3 36.2 %all-gather.14.cloned.1.call-done = bf16[1088,1024]{1,0:T(8,128)(2,1)} async-done(((bf16[272,1024]{1,0:T(8,128)(2,1)}), bf16[1088,1024]{1,0:T(8,128)(2,1)}) %all-gather.14.cloned.1.call-update) | async-done | bytes 2228240 | tf_op jit(solution)/shard_map/all_gather | solution.py:144
  208.0 9.4 all_gather.76
  217.4 12.8 reduce-scatter.25.cloned.1.call-done
  231.4 46.3 %reduce-scatter.29.cloned.1.call-done = bf16[272,1024]{1,0:T(8,128)(2,1)} async-done(((bf16[1088,1024]{1,0:T(8,128)(2,1)}), bf16[272,1024]{1,0:T(8,128)(2,1)}) %reduce-scatter.29.cloned.1.call-update) | async-done | bytes 557072 | tf_op jit(solution)/shard_map/reduce_scatter | solution.py:163
  285.8 9.4 all-gather.1
  295.2 12.2 all-gather.20.cloned.1.call-done
  307.5 50.0 %all-gather.18.cloned.1.call-done = bf16[1088,1024]{1,0:T(8,128)(2,1)} async-done(((bf16[272,1024]{1,0:T(8,128)(2,1)}), bf16[1088,1024]{1,0:T(8,128)(2,1)}) %all-gather.18.cloned.1.call-update) | async-done | bytes 2228240 | tf_op jit(solution)/shard_map/all_gather | solution.py:173
  357.5 15.7 %multiply_convert_fusion.9 = (bf16[1088,1024]{1,0:T(8,128)(2,1)}, f32[1088,1024]{1,0:T(8,128)}, f32[1088,1024]{1,0:T(8,128)}) fusion(f32[1024]{0:T(1024)S(1)} %bitcast.598, bf16[1088,1024]{1,0:T(8,128)(2,1)} %all-gather.18.cloned.1.call-done, bf16[1024,1024]{1,0:T(8,128)(2,1)} %all-gather.20.cloned.1.call-done), kind=kOutput, calls=%fused_computation.77 | convolution fusion | flops 2355232768 | bytes 15470592 | tf_op jit(solution)/shard_map/dot_general | solution.py:174
  373.2 13.4 %all-gather.22.cloned.1.call-done = bf16[1024,1024]{1,0:T(8,128)(2,1)} async-done(((bf16[128,1024]{1,0:T(8,128)(2,1)}), bf16[1024,1024]{1,0:T(8,128)(2,1)}) %all-gather.22.cloned.1.call-update) | async-done | bytes 2097168 | tf_op jit(solution)/shard_map/all_gather | solution.py:122
  386.6 6.2 convolution_convert_fusion.4
  393.1 43.0 %all-gather.26.cloned.1.call-done = bf16[1088,1024]{1,0:T(8,128)(2,1)} async-done(((bf16[272,1024]{1,0:T(8,128)(2,1)}), bf16[1088,1024]{1,0:T(8,128)(2,1)}) %all-gather.26.cloned.1.call-update) | async-done | bytes 2228240 | tf_op jit(solution)/shard_map/all_gather | solution.py:173
  436.1 15.5 %multiply_convert_fusion.8 = (bf16[1088,1024]{1,0:T(8,128)(2,1)S(1)}, f32[1088,1024]{1,0:T(8,128)}, f32[1088,1024]{1,0:T(8,128)}) fusion(f32[1024]{0:T(1024)S(1)} %bitcast.599, bf16[1088,1024]{1,0:T(8,128)(2,1)} %all-gather.26.cloned.1.call-done, bf16[1024,1024]{1,0:T(8,128)(2,1)} %all-gather.20.cloned.1.call-done), kind=kOutput, calls=%fused_computation.64 | convolution fusion | flops 2355232768 | bytes 15470592 | tf_op jit(solution)/shard_map/dot_general | solution.py:174
  453.0 3.9 convolution_convert_fusion.2
  456.9 26.0 %reduce-scatter.27.cloned.1.call-done = bf16[272,1024]{1,0:T(8,128)(2,1)} async-done(((bf16[1088,1024]{1,0:T(8,128)(2,1)}), bf16[272,1024]{1,0:T(8,128)(2,1)}) %reduce-scatter.27.cloned.1.call-update) | async-done | bytes 557072 | tf_op jit(solution)/shard_map/reduce_scatter | solution.py:183
  484.2 46.5 %reduce-scatter.31.cloned.1.call-done = bf16[272,1024]{1,0:T(8,128)(2,1)} async-done(((bf16[1088,1024]{1,0:T(8,128)(2,1)}), bf16[272,1024]{1,0:T(8,128)(2,1)}) %reduce-scatter.31.cloned.1.call-update) | async-done | bytes 557072 | tf_op jit(solution)/shard_map/reduce_scatter | solution.py:183
  540.5 46.8 %all-gather.28.cloned.1.call-done = bf16[1088,1024]{1,0:T(8,128)(2,1)} async-done(((bf16[272,1024]{1,0:T(8,128)(2,1)}), bf16[1088,1024]{1,0:T(8,128)(2,1)}) %all-gather.28.cloned.1.call-update) | async-done | bytes 2228240 | tf_op jit(solution)/shard_map/all_gather | solution.py:237
  587.4 9.4 convert_reduce_fusion.1
  598.1 3.9 convolution_convert_fusion.1
  602.1 34.0 %all-gather.32.cloned.1.call-done = bf16[1088,1024]{1,0:T(8,128)(2,1)} async-done(((bf16[272,1024]{1,0:T(8,128)(2,1)}), bf16[1088,1024]{1,0:T(8,128)(2,1)}) %all-gather.32.cloned.1.call-update) | async-done | bytes 2228240 | tf_op jit(solution)/shard_map/all_gather | solution.py:237
  636.1 9.4 convert_reduce_fusion
  646.8 3.9 convolution_convert_fusion
  651.0 32.0 %reduce-scatter.33.cloned.1.call-done = bf16[272,1024]{1,0:T(8,128)(2,1)} async-done(((bf16[1088,1024]{1,0:T(8,128)(2,1)}), bf16[272,1024]{1,0:T(8,128)(2,1)}) %reduce-scatter.33.cloned.1.call-update) | async-done | bytes 557072 | tf_op jit(solution)/shard_map/reduce_scatter | solution.py:247
  683.0 47.6 %reduce-scatter.37.cloned.1.call-done = bf16[272,1024]{1,0:T(8,128)(2,1)} async-done(((bf16[1088,1024]{1,0:T(8,128)(2,1)}), bf16[272,1024]{1,0:T(8,128)(2,1)}) %reduce-scatter.37.cloned.1.call-update) | async-done | bytes 557072 | tf_op jit(solution)/shard_map/reduce_scatter | solution.py:247
  730.6 5.0 fusion.168
  742.0 47.0 %all-gather.30.cloned.1.call-done = bf16[1088,1024]{1,0:T(8,128)(2,1)} async-done(((bf16[272,1024]{1,0:T(8,128)(2,1)}), bf16[1088,1024]{1,0:T(8,128)(2,1)}) %all-gather.30.cloned.1.call-update) | async-done | bytes 2228240 | tf_op jit(solution)/shard_map/all_gather | solution.py:258
  791.7 4.1 multiply_reduce_fusion.7
  801.9 35.8 %all-gather.34.cloned.1.call-done = bf16[1088,1024]{1,0:T(8,128)(2,1)} async-done(((bf16[272,1024]{1,0:T(8,128)(2,1)}), bf16[1088,1024]{1,0:T(8,128)(2,1)}) %all-gather.34.cloned.1.call-update) | async-done | bytes 2228240 | tf_op jit(solution)/shard_map/all_gather | solution.py:258
  847.3 4.1 multiply_reduce_fusion.6
  880.3 4.3 multiply_reduce_fusion
  923.7 7.3 fusion.232
  936.0 35.8 %reduce-scatter.39.cloned.1.call-done = bf16[272,1024]{1,0:T(8,128)(2,1)} async-done(((bf16[1088,1024]{1,0:T(8,128)(2,1)}), bf16[272,1024]{1,0:T(8,128)(2,1)}) %reduce-scatter.39.cloned.1.call-update) | async-done | bytes 557072 | tf_op jit(solution)/shard_map/reduce_scatter | solution.py:300
  976.7 8.4 convolution_add_fusion.22
  985.2 5.5 fusion.231
  990.7 4.5 convolution_add_fusion.23
  1013.5 12.0 all-reduce
  1029.3 16.0 %reduce-scatter.49.cloned.1.call-done = f32[32,2]{1,0:T(8,128)} async-done(((f32[256,2]{1,0:T(8,128)}), f32[32,2]{1,0:T(8,128)}) %reduce-scatter.49.cloned.1.call-update) | async-done | bytes 272
  1050.4 32.2 %reduce-scatter.51.cloned.1.call-done = f32[128,4]{1,0:T(8,128)} async-done(((f32[1024,4]{1,0:T(8,128)}), f32[128,4]{1,0:T(8,128)}) %reduce-scatter.51.cloned.1.call-update) | async-done | bytes 2064
  1083.4 36.7 %reduce-scatter.53.cloned.1.call-done = f32[128,4]{1,0:T(8,128)} async-done(((f32[1024,4]{1,0:T(8,128)}), f32[128,4]{1,0:T(8,128)}) %reduce-scatter.53.cloned.1.call-update) | async-done | bytes 2064
  1121.0 10.4 all-reduce.1
  1131.4 44.3 %reduce-scatter.47.cloned.1.call-done = f32[128,1024]{1,0:T(8,128)} async-done(((f32[1024,1024]{1,0:T(8,128)}), f32[128,1024]{1,0:T(8,128)}) %reduce-scatter.47.cloned.1.call-update) | async-done | bytes 524304 | tf_op jit(solution)/shard_map/reduce_scatter | solution.py:325
  1175.7 55.7 %reduce-scatter.45.cloned.1.call-done = f32[128,1024]{1,0:T(8,128)} async-done(((f32[1024,1024]{1,0:T(8,128)}), f32[128,1024]{1,0:T(8,128)}) %reduce-scatter.45.cloned.1.call-update) | async-done | bytes 524304 | tf_op jit(solution)/shard_map/reduce_scatter | solution.py:323
  1231.4 39.5 %reduce-scatter.43.cloned.1.call-done = f32[32,1024]{1,0:T(8,128)} async-done(((f32[256,1024]{1,0:T(8,128)}), f32[32,1024]{1,0:T(8,128)}) %reduce-scatter.43.cloned.1.call-update) | async-done | bytes 131088 | tf_op jit(solution)/shard_map/reduce_scatter | solution.py:322
  1270.9 50.2 %reduce-scatter.41.cloned.1.call-done = f32[3,128,256]{2,1,0:T(8,128)} async-done(((f32[3,1024,256]{2,1,0:T(8,128)}), f32[3,128,256]{2,1,0:T(8,128)}) %reduce-scatter.41.cloned.1.call-update) | async-done | bytes 393232 | tf_op jit(solution)/shard_map/reduce_scatter | solution.py:320
  (663 shorter events, 248.9 us)
Async XLA Ops:
  7.2 49.9 %all-gather.16.cloned.1.call-start = ((), (), s32[]{:S(2)}) async-start(), calls=%async_computation.17 | async-start | bytes 1769472 | tf_op jit(solution)/shard_map/all_gather | solution.py:117
  7.9 80.3 %all-gather.24.cloned.1.call-start = ((), (), s32[]{:S(2)}) async-start(), calls=%async_computation.23 | async-start | bytes 2785280 | tf_op jit(solution)/shard_map/all_gather | solution.py:144
  33.6 104.0 %all-gather.14.cloned.1.call-start = ((), (), s32[]{:S(2)}) async-start(), calls=%async_computation.16 | async-start | bytes 2785280 | tf_op jit(solution)/shard_map/all_gather | solution.py:144
  34.3 195.9 %reduce-scatter.25.cloned.1.call-start = ((), (), s32[]{:S(2)}) async-start(), calls=%async_computation.18 | async-start | bytes 2785280 | tf_op jit(solution)/shard_map/reduce_scatter | solution.py:163
  92.8 101.6 %copy-start.8 = (bf16[1088,256]{0,1:T(8,128)(2,1)}, bf16[1088,256]{0,1:T(8,128)(2,1)S(1)}, u32[]{:S(2)}) copy-start(bf16[1088,256]{0,1:T(8,128)(2,1)S(1)} %copy.138) | copy-start | bytes 1671172
  150.3 51.3 %copy-start.20 = (bf16[1088,256]{0,1:T(8,128)(2,1)}, bf16[1088,256]{0,1:T(8,128)(2,1)S(1)}, u32[]{:S(2)}) copy-start(bf16[1088,256]{0,1:T(8,128)(2,1)S(1)} %copy.136) | copy-start | bytes 1671172
  185.3 92.4 %reduce-scatter.29.cloned.1.call-start = ((), (), s32[]{:S(2)}) async-start(), calls=%async_computation.24 | async-start | bytes 2785280 | tf_op jit(solution)/shard_map/reduce_scatter | solution.py:163
  207.3 73.5 %copy-start.93 = (f32[1,1024]{1,0:T(1,128)S(1)}, f32[1,1024]{1,0:T(1,128)}, u32[]{:S(2)}) copy-start(f32[1,1024]{1,0:T(1,128)} %get-tuple-element.129) | copy-start | bytes 12292
  207.3 73.5 %copy-start.147 = (f32[1,1024]{1,0:T(1,128)S(1)}, f32[1,1024]{1,0:T(1,128)}, u32[]{:S(2)}) copy-start(f32[1,1024]{1,0:T(1,128)} %get-tuple-element.133) | copy-start | bytes 12292
  207.3 100.1 %all-gather.20.cloned.1.call-start = ((), (), s32[]{:S(2)}) async-start(), calls=%async_computation.20 | async-start | bytes 2359296 | tf_op jit(solution)/shard_map/all_gather | solution.py:120
  207.9 149.6 %all-gather.18.cloned.1.call-start = ((), (), s32[]{:S(2)}) async-start(), calls=%async_computation.19 | async-start | bytes 2785280 | tf_op jit(solution)/shard_map/all_gather | solution.py:173
  285.0 101.7 %all-gather.22.cloned.1.call-start = ((), (), s32[]{:S(2)}) async-start(), calls=%async_computation.21 | async-start | bytes 2359296 | tf_op jit(solution)/shard_map/all_gather | solution.py:122
  285.7 150.4 %all-gather.26.cloned.1.call-start = ((), (), s32[]{:S(2)}) async-start(), calls=%async_computation.25 | async-start | bytes 2785280 | tf_op jit(solution)/shard_map/all_gather | solution.py:173
  295.2 187.8 %reduce-scatter.27.cloned.1.call-start = ((), (), s32[]{:S(2)}) async-start(), calls=%async_computation.22 | async-start | bytes 2785280 | tf_op jit(solution)/shard_map/reduce_scatter | solution.py:183
  392.8 137.9 %reduce-scatter.31.cloned.1.call-start = ((), (), s32[]{:S(2)}) async-start(), calls=%async_computation.26 | async-start | bytes 2785280 | tf_op jit(solution)/shard_map/reduce_scatter | solution.py:183
  456.8 77.0 %copy-start.18 = (bf16[2,272,1024]{2,1,0:T(8,128)(2,1)S(1)}, bf16[2,272,1024]{2,1,0:T(8,128)(2,1)}, u32[]{:S(2)}) copy-start(bf16[2,272,1024]{2,1,0:T(8,128)(2,1)} %param.23) | copy-start | bytes 3342340
  456.8 77.0 %copy-start.92 = (f32[1,1024]{1,0:T(1,128)S(1)}, f32[1,1024]{1,0:T(1,128)}, u32[]{:S(2)}) copy-start(f32[1,1024]{1,0:T(1,128)} %get-tuple-element.127) | copy-start | bytes 12292
  456.9 130.5 %all-gather.28.cloned.1.call-start = ((), (), s32[]{:S(2)}) async-start(), calls=%async_computation.27 | async-start | bytes 2785280 | tf_op jit(solution)/shard_map/all_gather | solution.py:237
  539.3 96.8 %all-gather.32.cloned.1.call-start = ((), (), s32[]{:S(2)}) async-start(), calls=%async_computation.31 | async-start | bytes 2785280 | tf_op jit(solution)/shard_map/all_gather | solution.py:237
  540.1 142.9 %reduce-scatter.33.cloned.1.call-start = ((), (), s32[]{:S(2)}) async-start(), calls=%async_computation.28 | async-start | bytes 2785280 | tf_op jit(solution)/shard_map/reduce_scatter | solution.py:247
  602.0 128.6 %reduce-scatter.37.cloned.1.call-start = ((), (), s32[]{:S(2)}) async-start(), calls=%async_computation.32 | async-start | bytes 2785280 | tf_op jit(solution)/shard_map/reduce_scatter | solution.py:247
  646.8 83.8 %copy-start.146 = (f32[1,1024]{1,0:T(1,128)S(1)}, f32[1,1024]{1,0:T(1,128)}, u32[]{:S(2)}) copy-start(f32[1,1024]{1,0:T(1,128)} %get-tuple-element.131) | copy-start | bytes 12292
  650.7 138.3 %all-gather.30.cloned.1.call-start = ((), (), s32[]{:S(2)}) async-start(), calls=%async_computation.29 | async-start | bytes 2785280 | tf_op jit(solution)/shard_map/all_gather | solution.py:258
  738.6 50.5 %copy-start.38 = (bf16[256,1024]{1,0:T(8,128)(2,1)S(1)}, bf16[256,1024]{1,0:T(8,128)(2,1)}, u32[]{:S(2)}) copy-start(bf16[256,1024]{1,0:T(8,128)(2,1)} %all_gather.75) | copy-start | bytes 1572868
  741.0 96.6 %all-gather.34.cloned.1.call-start = ((), (), s32[]{:S(2)}) async-start(), calls=%async_computation.33 | async-start | bytes 2785280 | tf_op jit(solution)/shard_map/all_gather | solution.py:258
  741.9 194.2 %reduce-scatter.35.cloned.1.call-start = ((), (), s32[]{:S(2)}) async-start(), calls=%async_computation.30 | async-start | bytes 2785280 | tf_op jit(solution)/shard_map/reduce_scatter | solution.py:300
  742.0 49.7 %copy-start.23 = (bf16[1088,256]{0,1:T(8,128)(2,1)S(1)}, bf16[1088,256]{0,1:T(8,128)(2,1)}, u32[]{:S(2)}) copy-start(bf16[1088,256]{0,1:T(8,128)(2,1)} %copy-done.22) | copy-start | bytes 1671172
  879.2 92.6 %reduce-scatter.39.cloned.1.call-start = ((), (), s32[]{:S(2)}) async-start(), calls=%async_computation.34 | async-start | bytes 2785280 | tf_op jit(solution)/shard_map/reduce_scatter | solution.py:300
  922.1 106.3 %reduce-scatter.55.cloned.1.call-start = ((), (), s32[]{:S(2)}) async-start(), calls=%async_computation.42 | async-start | bytes 589824
  932.0 39.8 %copy-start.109 = (f32[272]{0:T(512)S(1)}, f32[272]{0:T(512)}, u32[]{:S(2)}) copy-start(f32[272]{0:T(512)} %copy-done.108) | copy-start | bytes 3268
  932.0 39.8 %copy-start.112 = (f32[272]{0:T(512)S(1)}, f32[272]{0:T(512)}, u32[]{:S(2)}) copy-start(f32[272]{0:T(512)} %copy-done.111) | copy-start | bytes 3268
  932.1 113.2 %reduce-scatter.49.cloned.1.call-start = ((), (), s32[]{:S(2)}) async-start(), calls=%async_computation.39 | async-start | bytes 147456
  933.0 41.3 %copy-start.131 = (f32[1024]{0:T(1024)S(1)}, f32[1024]{0:T(1024)}, u32[]{:S(2)}) copy-start(f32[1024]{0:T(1024)} %get-tuple-element.17) | copy-start | bytes 12292
  933.0 41.3 %copy-start.132 = (f32[1024]{0:T(1024)S(1)}, f32[1024]{0:T(1024)}, u32[]{:S(2)}) copy-start(f32[1024]{0:T(1024)} %get-tuple-element.28) | copy-start | bytes 12292
  933.0 41.3 %copy-start.135 = (f32[1024]{0:T(1024)S(1)}, f32[1024]{0:T(1024)}, u32[]{:S(2)}) copy-start(f32[1024]{0:T(1024)} %get-tuple-element.15) | copy-start | bytes 12292
  933.0 41.3 %copy-start.136 = (f32[1024]{0:T(1024)S(1)}, f32[1024]{0:T(1024)}, u32[]{:S(2)}) copy-start(f32[1024]{0:T(1024)} %get-tuple-element.64) | copy-start | bytes 12292
  933.0 41.3 %copy-start.142 = (f32[1024]{0:T(1024)S(1)}, f32[1024]{0:T(1024)}, u32[]{:S(2)}) copy-start(f32[1024]{0:T(1024)} %get-tuple-element.25) | copy-start | bytes 12292
  933.0 41.3 %copy-start.143 = (f32[1024]{0:T(1024)S(1)}, f32[1024]{0:T(1024)}, u32[]{:S(2)}) copy-start(f32[1024]{0:T(1024)} %get-tuple-element.124) | copy-start | bytes 12292
  934.4 41.0 %copy-start.133 = (f32[1024]{0:T(1024)S(1)}, f32[1024]{0:T(1024)}, u32[]{:S(2)}) copy-start(f32[1024]{0:T(1024)} %get-tuple-element.38) | copy-start | bytes 12292
  934.4 41.0 %copy-start.134 = (f32[1024]{0:T(1024)S(1)}, f32[1024]{0:T(1024)}, u32[]{:S(2)}) copy-start(f32[1024]{0:T(1024)} %get-tuple-element.61) | copy-start | bytes 12292
  934.4 41.0 %copy-start.140 = (f32[1024]{0:T(1024)S(1)}, f32[1024]{0:T(1024)}, u32[]{:S(2)}) copy-start(f32[1024]{0:T(1024)} %get-tuple-element.50) | copy-start | bytes 12292
  934.5 41.0 %copy-start.141 = (f32[1024]{0:T(1024)S(1)}, f32[1024]{0:T(1024)}, u32[]{:S(2)}) copy-start(f32[1024]{0:T(1024)} %get-tuple-element.121) | copy-start | bytes 12292
  936.0 146.6 %reduce-scatter.51.cloned.1.call-start = ((), (), s32[]{:S(2)}) async-start(), calls=%async_computation.40 | async-start | bytes 589824
  975.4 144.7 %reduce-scatter.53.cloned.1.call-start = ((), (), s32[]{:S(2)}) async-start(), calls=%async_computation.41 | async-start | bytes 589824
  976.6 199.1 %reduce-scatter.47.cloned.1.call-start = ((), (), s32[]{:S(2)}) async-start(), calls=%async_computation.38 | async-start | bytes 4718592 | tf_op jit(solution)/shard_map/reduce_scatter | solution.py:325
  985.1 246.3 %reduce-scatter.45.cloned.1.call-start = ((), (), s32[]{:S(2)}) async-start(), calls=%async_computation.37 | async-start | bytes 4718592 | tf_op jit(solution)/shard_map/reduce_scatter | solution.py:323
  995.3 275.6 %reduce-scatter.43.cloned.1.call-start = ((), (), s32[]{:S(2)}) async-start(), calls=%async_computation.36 | async-start | bytes 1179648 | tf_op jit(solution)/shard_map/reduce_scatter | solution.py:322
  1000.8 320.3 %reduce-scatter.41.cloned.1.call-start = ((), (), s32[]{:S(2)}) async-start(), calls=%async_computation.35 | async-start | bytes 3538944 | tf_op jit(solution)/shard_map/reduce_scatter | solution.py:320
  (170 other events, 967.1 us)
Sparse Core Ops, SparseCore 0:
  9.9 28.2 all-gather.15
  40.3 47.8 all-gather.23
  90.4 47.1 all-gather.13
  185.4 44.6 reduce-scatter.24
  232.3 45.4 reduce-scatter.28
  279.5 27.9 all-gather.19
  309.6 47.8 all-gather.17
  359.4 27.1 all-gather.21
  388.2 47.8 all-gather.25
  438.2 44.6 reduce-scatter.26
  485.3 45.4 reduce-scatter.30
  539.5 47.8 all-gather.27
  588.9 47.1 all-gather.31
  638.3 44.6 reduce-scatter.32
  685.2 45.4 reduce-scatter.36
  741.1 47.8 all-gather.29
  790.4 47.1 all-gather.33
  879.4 44.6 reduce-scatter.34
  926.4 45.4 reduce-scatter.38
  975.3 33.2 reduce-scatter.54
  1011.9 33.3 reduce-scatter.48
  1048.4 34.1 reduce-scatter.50
  1085.9 34.1 reduce-scatter.52
  1123.9 51.7 reduce-scatter.46
  1180.0 51.3 reduce-scatter.44
  1235.0 35.8 reduce-scatter.42
  1274.7 46.3 reduce-scatter.40
where the time goes:
time: 1330 us
  waiting for transfers between devices  875 us (66%)
  matrix products  222 us (17%)
  blocking collectives  78.9 us (6%)
  other arithmetic  69 us (5%)
  local copies, waits for them, and re-layouts  62.5 us (5%)
  between operations  18.1 us (1%)
    all_gather x2, waiting for transfers between devices, on_device(): hidden_two = lax.all_gather(normed_two, 'mp', axis=0, tiled=True)  93.1 us
    unnamed x31, waiting for transfers between devices  88.5 us
    all_gather x2, waiting for transfers between devices, on_device(): grad_branch_all = lax.all_gather(grad_branch, 'mp', axis=0, tiled=True)  82.8 us
    all_gather x2, waiting for transfers between devices, on_device(): grad_f_all = lax.all_gather(grad_f, 'mp', axis=0, tiled=True)  80.9 us
    reduce_scatter x2, waiting for transfers between devices, on_device(): lax.psum_scatter(ffn_back(jnp.int32(0), lax.axis_size('mp') * share).asty...  79.6 us
    reduce_scatter x2, waiting for transfers between devices, on_device(): lax.psum_scatter(ffn_term(jnp.int32(0), lax.axis_size('mp') * share).asty...  72.5 us
    all_gather x2, waiting for transfers between devices, on_device(): hidden_in = lax.all_gather(normed, 'mp', axis=0, tiled=True)  67.3 us
    reduce_scatter x2, waiting for transfers between devices, on_device(): lax.psum_scatter(out_term(jnp.int32(0), lax.axis_size('mp') * share).asty...  59.1 us
  transfers between devices with their start and end apart: 27, of which 24 were waited for; matrix products, arithmetic and copies ran while one was open for 17% of the time, Pallas kernels for 0%

commit v1 on v0

v1 whole, which is shorter than its diff:
```python
import functools
import math

import jax
import jax.numpy as jnp
from jax import lax
from jax.experimental import pallas as pl
from jax.experimental.pallas import tpu as pltpu
from jax.sharding import PartitionSpec as P

HEAD_DIM = 64
CAPTION = 64
ALPHA = 32.0
EPS = 1e-05
SCALE = 1.0 / (ALPHA * math.sqrt(HEAD_DIM))
NEG = -1e30
BF = jnp.bfloat16
F32 = jnp.float32


def stats(value):
    mean = jnp.mean(value, axis=-1, keepdims=True)
    centred = value - mean
    inverse = lax.rsqrt(jnp.mean(centred * centred, axis=-1, keepdims=True) + EPS)
    return centred * inverse, inverse


def norm_back(unit, inverse, gain, grad):
    scaled = grad * gain
    grad_in = inverse * (
        scaled
        - jnp.mean(scaled, axis=-1, keepdims=True)
        - unit * jnp.mean(scaled * unit, axis=-1, keepdims=True)
    )
    return grad_in, jnp.sum(grad * unit, axis=0), jnp.sum(grad, axis=0)


def gelu_both(value):
    cdf = 0.5 * (1.0 + lax.erf(value * (1.0 / math.sqrt(2.0))))
    pdf = jnp.exp(-0.5 * value * value) * (1.0 / math.sqrt(2.0 * math.pi))
    return (value * cdf).astype(BF), (cdf + value * pdf).astype(BF)


def dot_nt(a, b):
    return lax.dot_general(a, b, (((1,), (1,)), ((), ())), preferred_element_type=F32)


def dot_tn(a, b):
    return lax.dot_general(a, b, (((0,), (0,)), ((), ())), preferred_element_type=F32)


def dot_nn(a, b):
    return lax.dot_general(a, b, (((1,), (0,)), ((), ())), preferred_element_type=F32)


def row_blocks(length):
    body = length - CAPTION
    cuts = list(range(0, body, 256)) + [body, length]
    return list(zip(cuts[:-1], cuts[1:]))


def masks(start, stop, length, seg_c, seg_r):
    rows = stop - start
    if stop < length:
        causal = lax.broadcasted_iota(jnp.int32, (rows, rows), 0) >= lax.broadcasted_iota(
            jnp.int32, (rows, rows), 1
        )
        return causal, None
    own = lax.broadcasted_iota(jnp.int32, (rows, rows), 0) >= lax.broadcasted_iota(
        jnp.int32, (rows, rows), 1
    )
    same = seg_c[:, 0:1] == seg_r[0:1, start:stop]
    before = seg_c[:, 0:1] == seg_r[0:1, 0:start]
    return own & same, before


def attend_fwd_kernel(q_ref, k_ref, v_ref, segc_ref, segr_ref, o_ref, lse_ref):
    length = q_ref.shape[0]
    lane = lax.broadcasted_iota(jnp.int32, (1, 128), 1)
    for start, stop in row_blocks(length):
        own, before = masks(start, stop, length, segc_ref[...], segr_ref[...])
        outs = []
        lses = []
        for head in range(2):
            q = jnp.where((lane >= 64) == (head == 1), q_ref[start:stop, :], jnp.zeros((), BF))
            s2 = jnp.where(own, dot_nt(q, k_ref[start:stop, :]), NEG)
            top = jnp.max(s2, axis=-1, keepdims=True)
            if start:
                s1 = dot_nt(q, k_ref[0:start, :])
                if before is not None:
                    s1 = jnp.where(before, s1, NEG)
                top = jnp.maximum(top, jnp.max(s1, axis=-1, keepdims=True))
            e2 = jnp.exp(ALPHA * (s2 - top))
            total = jnp.sum(e2, axis=-1, keepdims=True)
            acc = dot_nn(e2.astype(BF), v_ref[start:stop, :])
            if start:
                e1 = jnp.exp(ALPHA * (s1 - top))
                total = total + jnp.sum(e1, axis=-1, keepdims=True)
                acc = acc + dot_nn(e1.astype(BF), v_ref[0:start, :])
            outs.append(acc / total)
            lses.append(ALPHA * top + jnp.log(total))
        o_ref[start:stop, :] = jnp.where(lane < 64, outs[0], outs[1]).astype(BF)
        lse_ref[start:stop, :] = jnp.where(lane < 64, lses[0], lses[1])


def attend_bwd_kernel(
    q_ref, k_ref, v_ref, do_ref, lse_ref, segc_ref, segr_ref, d_ref, dk_ref, dv_ref
):
    length = q_ref.shape[0]
    pair = pl.program_id(0)
    pairs = d_ref.shape[1] // 384
    lane = lax.broadcasted_iota(jnp.int32, (1, 128), 1)
    dk_ref[...] = jnp.zeros_like(dk_ref)
    dv_ref[...] = jnp.zeros_like(dv_ref)
    zero = jnp.zeros((), BF)
    for start, stop in row_blocks(length):
        own, before = masks(start, stop, length, segc_ref[...], segr_ref[...])
        dqs = []
        for head in range(2):
            mine = (lane >= 64) == (head == 1)
            q = jnp.where(mine, q_ref[start:stop, :], zero)
            do = jnp.where(mine, do_ref[start:stop, :], zero)
            lse = lse_ref[start:stop, head * 64 : head * 64 + 1]
            p2 = jnp.where(own, jnp.exp(ALPHA * dot_nt(q, k_ref[start:stop, :]) - lse), 0.0)
            g2 = dot_nt(do, v_ref[start:stop, :])
            delta = jnp.sum(p2 * g2, axis=-1, keepdims=True)
            if start:
                p1 = jnp.exp(ALPHA * dot_nt(q, k_ref[0:start, :]) - lse)
                if before is not None:
                    p1 = jnp.where(before, p1, 0.0)
                g1 = dot_nt(do, v_ref[0:start, :])
                delta = delta + jnp.sum(p1 * g1, axis=-1, keepdims=True)
            ds2 = (ALPHA * p2 * (g2 - delta)).astype(BF)
            dq = dot_nn(ds2, k_ref[start:stop, :])
            dk_ref[start:stop, :] += dot_tn(ds2, q)
            dv_ref[start:stop, :] += dot_tn(p2.astype(BF), do)
            if start:
                ds1 = (ALPHA * p1 * (g1 - delta)).astype(BF)
                dq = dq + dot_nn(ds1, k_ref[0:start, :])
                dk_ref[0:start, :] += dot_tn(ds1, q)
                dv_ref[0:start, :] += dot_tn(p1.astype(BF), do)
            dqs.append(dq)
        merged = jnp.where(lane < 64, dqs[0], dqs[1]) * SCALE
        d_ref[start:stop, pl.ds(pl.multiple_of(pair * 128, 128), 128)] = merged.astype(BF)
    d_ref[:, pl.ds(pl.multiple_of((pairs + pair) * 128, 128), 128)] = dk_ref[...].astype(BF)
    d_ref[:, pl.ds(pl.multiple_of((2 * pairs + pair) * 128, 128), 128)] = dv_ref[...].astype(BF)


def attend_forward(qkv, seg_c, seg_r):
    length, width = qkv.shape
    pairs = width // 384
    col = lambda base: pl.BlockSpec((length, 128), lambda j, base=base: (0, base + j))
    whole = lambda a: pl.BlockSpec(a.shape, lambda j: (0, 0))
    return pl.pallas_call(
        attend_fwd_kernel,
        grid=(pairs,),
        in_specs=[col(0), col(pairs), col(2 * pairs), whole(seg_c), whole(seg_r)],
        out_specs=[col(0), col(0)],
        out_shape=[
            jax.ShapeDtypeStruct((length, 128 * pairs), BF),
            jax.ShapeDtypeStruct((length, 128 * pairs), F32),
        ],
        compiler_params=pltpu.CompilerParams(vmem_limit_bytes=40 << 20),
        cost_estimate=pl.CostEstimate(
            flops=8 * pairs * length * length * 128,
            bytes_accessed=10 * length * 128 * pairs,
            transcendentals=pairs * length * length,
        ),
    )(qkv, qkv, qkv, seg_c, seg_r)


def attend_backward(qkv, grad_o, lse, seg_c, seg_r):
    length, width = qkv.shape
    pairs = width // 384
    col = lambda base: pl.BlockSpec((length, 128), lambda j, base=base: (0, base + j))
    whole = lambda a: pl.BlockSpec(a.shape, lambda j: (0, 0))
    return pl.pallas_call(
        attend_bwd_kernel,
        grid=(pairs,),
        in_specs=[
            col(0),
            col(pairs),
            col(2 * pairs),
            col(0),
            col(0),
            whole(seg_c),
            whole(seg_r),
        ],
        out_specs=pl.BlockSpec((length, width), lambda j: (0, 0)),
        out_shape=jax.ShapeDtypeStruct((length, width), BF),
        scratch_shapes=[pltpu.VMEM((length, 128), F32), pltpu.VMEM((length, 128), F32)],
        compiler_params=pltpu.CompilerParams(vmem_limit_bytes=48 << 20),
        cost_estimate=pl.CostEstimate(
            flops=20 * pairs * length * length * 128,
            bytes_accessed=18 * length * 128 * pairs,
            transcendentals=pairs * length * length,
        ),
    )(qkv, qkv, qkv, grad_o, lse, seg_c, seg_r)


def build(n_dp, n_mp):
    groups = n_dp // 2
    bits = [1 << b for b in range(groups.bit_length() - 1)]
    orders = (bits, bits[::-1])

    def flat(dp, mp):
        return dp * n_mp + mp

    token_out = []
    token_in = []
    for k in range(2):
        pairs_out = []
        for dp in range(n_dp):
            for z in range(n_mp):
                m = (k + z) % 2
                dest = flat(2 * (dp // 2) + z // 2, 2 * m + dp % 2)
                pairs_out.append((flat(dp, z), dest))
        token_out.append(pairs_out)
        token_in.append([(b, a) for a, b in pairs_out])
    weight_out = []
    weight_in = []
    for k in range(n_mp):
        pairs_out = []
        for dp in range(n_dp):
            for z in range(n_mp):
                s = 2 * (z % 2) + dp % 2
                pairs_out.append((flat(dp, z), flat(2 * (dp // 2) + z // 2, s ^ k)))
        weight_out.append(pairs_out)
        weight_in.append([(b, a) for a, b in pairs_out])
    both = ("dp", "mp")

    def swap(value):
        return lax.ppermute(value, "dp", [(i, i ^ 1) for i in range(n_dp)])

    def hop(value, bit):
        return lax.ppermute(value, "dp", [(i, i ^ (2 * bit)) for i in range(n_dp)])

    def on_device(
        tokens,
        seg_ids,
        qkv_weight,
        qv_bias,
        out_weight,
        up_weight,
        up_bias,
        down_weight,
        norm_gain,
        norm_bias,
        branch_bias,
        out_grad,
    ):
        dp = lax.axis_index("dp")
        z = lax.axis_index("mp")
        core = dp % 2
        group = dp // 2
        length = seg_ids.shape[1]
        half = length // 2
        quarter = length // n_mp
        width = tokens.shape[2]

        def pick2(flag, first, second):
            return jnp.where(flag == 0, first, second)

        def to_rows(value):
            got = []
            for k in range(2):
                mine = lax.dynamic_index_in_dim(value, (k + z) % 2, 0, keepdims=False)
                got.append(lax.ppermute(mine, both, token_out[k]))
            m = z // 2
            stack = jnp.stack(got)
            return jnp.concatenate(
                [
                    lax.dynamic_index_in_dim(stack, m, 0, keepdims=False),
                    lax.dynamic_index_in_dim(stack, 1 - m, 0, keepdims=False),
                ]
            )

        def from_rows(value):
            parts = value.reshape(2, quarter, width)
            m = z // 2
            got = []
            for k in range(2):
                mine = lax.dynamic_index_in_dim(parts, (m + k) % 2, 0, keepdims=False)
                got.append(lax.ppermute(mine, both, token_in[k]))
            first = pick2(z % 2, got[0], got[1])
            second = pick2(z % 2, got[1], got[0])
            return first, second

        def gather(block):
            rows, columns = block.shape
            got = [lax.ppermute(block, both, weight_out[k]) for k in range(n_mp)]
            local = jnp.zeros((n_mp, rows, columns), block.dtype)
            for k in range(n_mp):
                local = lax.dynamic_update_slice(local, got[k][None], (z ^ k, 0, 0))
            local = local.reshape(2, 1, 2 * rows, columns)
            result = []
            for i in range(2):
                pieces = [(0, local[i])]
                for bit in orders[i]:
                    pieces = pieces + [(rel ^ bit, hop(piece, bit)) for rel, piece in pieces]
                full = jnp.zeros((groups, 2 * rows, columns), block.dtype)
                for rel, piece in pieces:
                    full = lax.dynamic_update_slice(full, piece, (group ^ rel, 0, 0))
                result.append(full.reshape(n_dp * rows, columns))
            return result

        def scatter(grads):
            kept = []
            for i in range(2):
                total, columns = grads[i].shape
                rows = total // n_dp
                full = grads[i].astype(BF).reshape(groups, 2 * rows, columns)
                pieces = {
                    rel: lax.dynamic_index_in_dim(full, group ^ rel, 0, keepdims=False)
                    for rel in range(groups)
                }
                for bit in orders[i][::-1]:
                    keep = [rel for rel in pieces if not rel & bit]
                    pieces = {
                        rel: (
                            pieces[rel].astype(F32) + hop(pieces[rel ^ bit], bit).astype(F32)
                        ).astype(BF)
                        for rel in keep
                    }
                kept.append(pieces[0].reshape(2, rows, columns))
            local = jnp.concatenate(kept)
            summed = None
            for k in range(n_mp):
                mine = lax.dynamic_index_in_dim(local, z ^ k, 0, keepdims=False)
                got = lax.ppermute(mine, both, weight_in[k]).astype(F32)
                summed = got if summed is None else summed + got
            return summed

        def share(mine):
            other = swap(mine)
            return jnp.concatenate([pick2(core, mine, other), pick2(core, other, mine)])

        def reduce_half(partial):
            theirs = lax.dynamic_slice_in_dim(partial, (1 - core) * half, half, 0)
            ours = lax.dynamic_slice_in_dim(partial, core * half, half, 0)
            return ours.astype(F32) + swap(theirs.astype(BF)).astype(F32)

        x = to_rows(tokens).astype(F32)
        grad_y = to_rows(out_grad).astype(F32)

        per_qv = qv_bias.shape[1]
        slim = width // n_dp
        rows = [
            jnp.pad(value, ((0, 0), (0, slim_up - value.shape[1])))
            for slim_up in [max(slim, 2 * per_qv, up_bias.shape[0])]
            for value in (
                qv_bias.reshape(1, -1),
                up_bias.reshape(1, -1),
                norm_gain,
                norm_bias,
                branch_bias,
            )
        ]
        small = jnp.concatenate(rows, axis=0)
        every = lax.all_gather(small, both, axis=0)
        every = every.reshape(n_dp, n_mp, *small.shape).astype(F32)
        wide = every[:, 0, :, :slim].transpose(1, 0, 2).reshape(small.shape[0], width)
        gains = wide[2:6]
        shifts = wide[6:10]
        branch_b = wide[10:12]
        served = lax.dynamic_slice_in_dim(every, 2 * core, 2, 1)
        qv_b = served[:, :, 0, : 2 * per_qv].reshape(n_dp, 2, 2, per_qv)
        qv_b = qv_b.transpose(1, 2, 0, 3).reshape(2, 2, n_dp * per_qv)
        up_b = served[:, :, 1, : up_bias.shape[0]].transpose(1, 0, 2).reshape(2, -1)

        seg_other = swap(seg_ids)
        seg_own = pick2((core + z) % 2, seg_ids, seg_other)
        seg_row = lax.dynamic_index_in_dim(seg_own, z // 2, 0, keepdims=False)
        seg_r = jnp.broadcast_to(seg_row[None, :], (8, length))
        seg_c = jnp.broadcast_to(seg_row[length - CAPTION :, None], (CAPTION, 128))

        block_qkv = qkv_weight.transpose(1, 0, 2).reshape(qkv_weight.shape[1], -1)
        w_qkv = gather(block_qkv)
        n_out = out_weight.shape[0]
        w_out = gather(out_weight)
        w_up = gather(up_weight)
        w_down = gather(down_weight)

        unit0, inv0 = stats(x)
        h1 = share((unit0 * gains[0] + shifts[0]).astype(BF))
        cols = w_qkv[0].shape[1] // 3
        qkvs = []
        attended = []
        log_sums = []
        partial = None
        for i in range(2):
            bias = jnp.concatenate([qv_b[i, 0], jnp.zeros((cols,), F32), qv_b[i, 1]])
            factor = jnp.concatenate([jnp.full((cols,), SCALE, F32), jnp.ones((2 * cols,), F32)])
            qkv = ((dot_nn(h1, w_qkv[i]) + bias) * factor).astype(BF)
            o, lse = attend_forward(qkv, seg_c, seg_r)
            qkvs.append(qkv)
            attended.append(o)
            log_sums.append(lse)
            term = dot_nn(o, w_out[i])
            partial = term if partial is None else partial + term
        branch = reduce_half(partial) + branch_b[0]
        unit1, inv1 = stats(branch)
        middle = x + unit1 * gains[1] + shifts[1]
        unit2, inv2 = stats(middle)
        h2 = share((unit2 * gains[2] + shifts[2]).astype(BF))
        acts = []
        slopes = []
        partial = None
        for i in range(2):
            act, slope = gelu_both(dot_nn(h2, w_up[i]) + up_b[i])
            acts.append(act)
            slopes.append(slope)
            term = dot_nn(act, w_down[i])
            partial = term if partial is None else partial + term
        ffn_out = reduce_half(partial) + branch_b[1]
        unit3, inv3 = stats(ffn_out)
        out_rows = (middle + unit3 * gains[3] + shifts[3]).astype(BF)
        layer_out = jnp.stack(from_rows(out_rows))

        grad_f, dgain3, dshift3 = norm_back(unit3, inv3, gains[3], grad_y)
        grad_f = grad_f.astype(BF)
        dbranch1 = jnp.sum(grad_f.astype(F32), axis=0)
        grad_f_all = share(grad_f)
        dw_down = []
        dw_up = []
        dup = []
        partial = None
        for i in range(2):
            dw_down.append(dot_tn(acts[i], grad_f_all))
            grad_pre = (dot_nt(grad_f_all, w_down[i]) * slopes[i].astype(F32)).astype(BF)
            dup.append(jnp.sum(grad_pre.astype(F32), axis=0))
            dw_up.append(dot_tn(h2, grad_pre))
            term = dot_nt(grad_pre, w_up[i])
            partial = term if partial is None else partial + term
        down_grad = scatter(dw_down)
        up_grad = scatter(dw_up)
        grad_h2 = reduce_half(partial)
        back2, dgain2, dshift2 = norm_back(unit2, inv2, gains[2], grad_h2)
        grad_mid = grad_y + back2
        grad_a, dgain1, dshift1 = norm_back(unit1, inv1, gains[1], grad_mid)
        grad_a = grad_a.astype(BF)
        dbranch0 = jnp.sum(grad_a.astype(F32), axis=0)
        grad_a_all = share(grad_a)
        dw_out = []
        dw_qkv = []
        dqv = []
        partial = None
        for i in range(2):
            dw_out.append(dot_tn(attended[i], grad_a_all))
            grad_o = dot_nt(grad_a_all, w_out[i]).astype(BF)
            grad_qkv = attend_backward(qkvs[i], grad_o, log_sums[i], seg_c, seg_r)
            sums = jnp.sum(grad_qkv.astype(F32), axis=0)
            dqv.append(jnp.stack([sums[:cols], sums[2 * cols :]]))
            dw_qkv.append(dot_tn(h1, grad_qkv))
            term = dot_nt(grad_qkv, w_qkv[i])
            partial = term if partial is None else partial + term
        out_grad_w = scatter(dw_out)
        qkv_grad = scatter(dw_qkv)
        grad_h1 = reduce_half(partial)
        back0, dgain0, dshift0 = norm_back(unit0, inv0, gains[0], grad_h1)
        input_grad = jnp.stack(from_rows((grad_mid + back0).astype(BF))).astype(F32)
        qkv_grad = qkv_grad.reshape(qkv_weight.shape[1], 3, cols).transpose(1, 0, 2)

        n_ff = up_bias.shape[0] * n_dp * n_mp
        placed_up = lax.dynamic_update_slice(
            jnp.zeros((n_ff,), F32), jnp.concatenate(dup), (core * (n_ff // 2),)
        )
        placed_qv = lax.dynamic_update_slice(
            jnp.zeros((2, width), F32), jnp.concatenate(dqv, axis=1), (0, core * (width // 2))
        )
        vectors = jnp.concatenate(
            [
                jnp.stack(
                    [
                        dgain0,
                        dgain1,
                        dgain2,
                        dgain3,
                        dshift0,
                        dshift1,
                        dshift2,
                        dshift3,
                        dbranch0,
                        dbranch1,
                    ]
                ),
                placed_qv,
                placed_up.reshape(-1, width),
            ]
        )
        vectors = lax.psum(vectors, both)
        mine = lax.dynamic_slice_in_dim(vectors[:10], dp * slim, slim, 1)
        where_qv = (z * n_dp + dp) * per_qv
        qv_grad = lax.dynamic_slice_in_dim(vectors[10:12], where_qv, per_qv, 1)
        up_bias_grad = lax.dynamic_slice_in_dim(
            vectors[12:].reshape(-1), (z * n_dp + dp) * up_bias.shape[0], up_bias.shape[0], 0
        )
        return (
            layer_out,
            input_grad,
            qkv_grad,
            qv_grad,
            out_grad_w,
            up_grad,
            up_bias_grad,
            down_grad,
            mine[0:4],
            mine[4:8],
            mine[8:10],
        )

    return on_device


def solution(mesh):
    n_dp, n_mp = mesh.shape["dp"], mesh.shape["mp"]
    in_specs = (
        P(None, ("dp", "mp"), None),
        P(None, "dp"),
        P(None, "dp", "mp"),
        P(None, ("mp", "dp")),
        P(("mp", "dp"), None),
        P("dp", "mp"),
        P(("mp", "dp")),
        P(("mp", "dp"), None),
        P(None, "dp"),
        P(None, "dp"),
        P(None, "dp"),
        P(None, ("dp", "mp"), None),
    )
    out_specs = (
        P(None, ("dp", "mp"), None),
        P(None, ("dp", "mp"), None),
        P(None, "dp", "mp"),
        P(None, ("mp", "dp")),
        P(("mp", "dp"), None),
        P("dp", "mp"),
        P(("mp", "dp")),
        P(("mp", "dp"), None),
        P(None, "dp"),
        P(None, "dp"),
        P(None, "dp"),
    )
    return jax.shard_map(
        build(n_dp, n_mp), mesh=mesh, in_specs=in_specs, out_specs=out_specs, check_vma=False
    )
```

time: 1330 us -> 788 us (0.59)
  waiting for transfers between devices: 875 us -> 319 us
  starting transfers between devices: 2.55 us -> 172 us
  matrix products: 222 us -> 65.2 us
  Pallas kernels: 0 us -> 47.3 us
  local copies, waits for them, and re-layouts: 62.5 us -> 44.8 us
  blocking collectives: 78.9 us -> 61.5 us
  other arithmetic: 69 us -> 51.7 us
    reduce_scatter x12 -> x0, waiting for transfers between devices: 437 us -> none  [the longest x2 79.6 us: on_device(): lax.psum_scatter(ffn_back(jnp.int32(0), lax.axis_size('mp') * share).asty...]
    all_gather x11 -> x0, waiting for transfers between devices: 350 us -> none  [the longest x2 93.1 us: on_device(): hidden_two = lax.all_gather(normed_two, 'mp', axis=0, tiled=True)]
    ppermute x0 -> x97, waiting for transfers between devices: none -> 207 us  [the longest x48 104 us: hop(): return lax.ppermute(value, 'dp', [(i, i ^ 2 * bit) for i in range(n_dp)])]
    ppermute x0 -> x97, starting transfers between devices: none -> 171 us  [the longest x16 53.8 us: gather(): got = [lax.ppermute(block, both, weight_out[k]) for k in range(n_mp)]]
    dot_general x84 -> x24, matrix products: 222 us -> 65.2 us  [the longest x8 23.8 us: dot_nt(): lax.dot_general(a, b, (((1,), (1,)), ((), ())), preferred_element_type=F32)]
    psum x0 -> x1, waiting for transfers between devices: none -> 112 us  [on_device(): vectors = lax.psum(vectors, both)]
    unnamed x31 -> x1, waiting for transfers between devices: 88.5 us -> 0.02 us
    pallas_call x0 -> x4, Pallas kernels: none -> 47.3 us  [the longest x2 29.8 us: attend_backward(): pl.pallas_call(attend_bwd_kernel, grid=(pairs,), in_specs=[col(0), col(pa...]
  transfers between devices with their start and end apart: 27 -> 98, of which waited for: 24 -> 33; matrix products, arithmetic and copies ran while one was open for 17% -> 12% of each run, Pallas kernels for 0% -> 2%
where the time goes in v1:
time: 788 us; the launch traced here: 778 us
  waiting for transfers between devices  319 us (40%)
  starting transfers between devices  172 us (22%)
  matrix products  65.2 us (8%)
  blocking collectives  61.5 us (8%)
  other arithmetic  51.7 us (7%)
  Pallas kernels  47.3 us (6%)
  local copies, waits for them, and re-layouts  44.8 us (6%)
  between operations  17.2 us (2%)
    psum x1, waiting for transfers between devices, on_device(): vectors = lax.psum(vectors, both)  112 us
    ppermute x48, waiting for transfers between devices, hop(): return lax.ppermute(value, 'dp', [(i, i ^ 2 * bit) for i in range(n_dp)])  104 us
    all_gather x1, blocking collectives, on_device(): every = lax.all_gather(small, both, axis=0)  61.5 us
    ppermute x16, starting transfers between devices, gather(): got = [lax.ppermute(block, both, weight_out[k]) for k in range(n_mp)]  53.8 us
    ppermute x16, starting transfers between devices, scatter(): got = lax.ppermute(mine, both, weight_in[k]).astype(F32)  45.3 us
    ppermute x4, waiting for transfers between devices, to_rows(): got.append(lax.ppermute(mine, both, token_out[k]))  43.8 us
    ppermute x48, starting transfers between devices, hop(): return lax.ppermute(value, 'dp', [(i, i ^ 2 * bit) for i in range(n_dp)])  32.7 us
    pallas_call x2, Pallas kernels, attend_backward(): pl.pallas_call(attend_bwd_kernel, grid=(pairs,), in_specs=[col(0), col(pa...  29.8 us
  transfers between devices with their start and end apart: 98, of which 33 were waited for; matrix products, arithmetic and copies ran while one was open for 12% of the time, Pallas kernels for 2%

profile of v1, /device:TPU:1, one launch (start us, length us, event | category | flops | bytes accessed | tf_op | source)
XLA Modules:
  0.0 777.9 jit_solution(750549089098234851)
XLA Ops:
  8.3 4.6 collective-permute-start.3
  22.0 61.5 %all-gather.1 = bf16[32,12,128]{2,1,0:T(8,128)(2,1)S(1)} all-gather(bf16[1,12,128]{2,1,0:T(8,128)(2,1)S(1)} %bitcast.439), channel_id=2, replica_groups=mesh['dp'=8,'mp'=4] {'dp','mp'}, dimensions={0}, use_global_device_ids=true | all-gather | bytes 101376 | tf_op jit(solution)/shard_map/all_gather | solution.py:360
  86.2 5.2 collective-permute-start.12
  100.1 4.9 collective-permute-done.21
  113.7 6.4 collective-permute-start.34
  120.5 3.5 collective-permute-start.26
  125.7 7.3 collective-permute-start.28
  136.7 13.2 %collective-permute-start.29 = (bf16[128,1024]{1,0:T(8,128)(2,1)S(1)}, bf16[128,1024]{1,0:T(8,128)(2,1)S(1)}, u32[]{:S(2)}, u32[]{:S(2)}) collective-permute-start(bf16[128,1024]{1,0:T(8,128)(2,1)S(1)} %copy-done.70), channel_id=1, source_target_pairs={{0,3},{1,1},{2,7},{3,5},{4,2},{5,0},{6,6},{7,4},{8,11},{9,9},{10,1... | collective-permute-start | bytes 786440 | tf_op jit(solution)/shard_map/ppermute | solution.py:291
  156.9 7.9 %collective-permute-done.27 = bf16[128,1024]{1,0:T(8,128)(2,1)} collective-permute-done((bf16[128,1024]{1,0:T(8,128)(2,1)}, bf16[128,1024]{1,0:T(8,128)(2,1)}, u32[]{:S(2)}, u32[]{:S(2)}) %collective-permute-start.27) | collective-permute-done | bytes 262176 | tf_op jit(solution)/shard_map/ppermute | solution.py:291
  168.0 20.3 %collective-permute-done = bf16[272,1024]{1,0:T(8,128)(2,1)S(1)} collective-permute-done((bf16[272,1024]{1,0:T(8,128)(2,1)S(1)}, bf16[272,1024]{1,0:T(8,128)(2,1)S(1)}, u32[]{:S(2)}, u32[]{:S(2)}) %collective-permute-start) | collective-permute-done | bytes 557088 | tf_op jit(solution)/shard_map/ppermute | solution.py:268
  192.3 4.2 collective-permute-done.18
  196.9 8.0 %collective-permute-done.8 = bf16[1,256,768]{2,1,0:T(8,128)(2,1)S(1)} collective-permute-done((bf16[1,256,768]{2,1,0:T(8,128)(2,1)S(1)}, bf16[1,256,768]{2,1,0:T(8,128)(2,1)S(1)}, u32[]{:S(2)}, u32[]{:S(2)}) %collective-permute-start.8) | collective-permute-done | bytes 393248 | tf_op jit(solution)/shard_map/ppermute | solution.py:236
  205.5 7.9 %collective-permute-done.9 = bf16[1,256,768]{2,1,0:T(8,128)(2,1)S(1)} collective-permute-done((bf16[1,256,768]{2,1,0:T(8,128)(2,1)S(1)}, bf16[1,256,768]{2,1,0:T(8,128)(2,1)S(1)}, u32[]{:S(2)}, u32[]{:S(2)}) %collective-permute-start.9) | collective-permute-done | bytes 393248 | tf_op jit(solution)/shard_map/ppermute | solution.py:236
  218.6 8.7 %shard_map.203 = (bf16[1088,256]{1,0:T(8,128)(2,1)S(1)}, f32[1088,256]{1,0:T(8,128)S(1)}) custom-call(bf16[1088,768]{1,0:T(8,128)(2,1)S(1)} %fusion.14.q_ref.k_ref.v_ref, bf16[1088,768]{1,0:T(8,128)(2,1)S(1)} %fusion.14.q_ref.k_ref.v_ref, bf16[1088,768]{1,0:T(8,128)(2,1)S(1)} %fusion.14.q_ref.k_ref.v_ref, s32[64,128]{1,0:T(8,128)S(1)} %broadcast_in_dim.100.segc_ref, ...), custom_call_target="tpu_custom_call" | custom-call | flops 2424307712 | bytes 2785280 | tf_op jit(solution)/shard_map/pallas_call | solution.py:154
  228.2 8.9 %shard_map.204 = (bf16[1088,256]{1,0:T(8,128)(2,1)S(1)}, f32[1088,256]{1,0:T(8,128)S(1)}) custom-call(bf16[1088,768]{1,0:T(8,128)(2,1)S(1)} %fusion.15.q_ref.k_ref.v_ref, bf16[1088,768]{1,0:T(8,128)(2,1)S(1)} %fusion.15.q_ref.k_ref.v_ref, bf16[1088,768]{1,0:T(8,128)(2,1)S(1)} %fusion.15.q_ref.k_ref.v_ref, s32[64,128]{1,0:T(8,128)S(1)} %broadcast_in_dim.100.segc_ref, ...), custom_call_target="tpu_custom_call" | custom-call | flops 2424307712 | bytes 2785280 | tf_op jit(solution)/shard_map/pallas_call | solution.py:154
  248.4 5.6 collective-permute-done.43
  257.5 9.0 %collective-permute-done.37 = bf16[1,256,1024]{2,1,0:T(8,128)(2,1)S(1)} collective-permute-done((bf16[1,256,1024]{2,1,0:T(8,128)(2,1)S(1)}, bf16[1,256,1024]{2,1,0:T(8,128)(2,1)S(1)}, u32[]{:S(2)}, u32[]{:S(2)}) %collective-permute-start.37) | collective-permute-done | bytes 524320 | tf_op jit(solution)/shard_map/ppermute | solution.py:236
  267.8 8.7 %collective-permute-done.32 = bf16[1,256,1024]{2,1,0:T(8,128)(2,1)S(1)} collective-permute-done((bf16[1,256,1024]{2,1,0:T(8,128)(2,1)S(1)}, bf16[1,256,1024]{2,1,0:T(8,128)(2,1)S(1)}, u32[]{:S(2)}, u32[]{:S(2)}) %collective-permute-start.32) | collective-permute-done | bytes 524320 | tf_op jit(solution)/shard_map/ppermute | solution.py:236
  277.8 11.2 %collective-permute-done.45 = bf16[1,256,1024]{2,1,0:T(8,128)(2,1)S(1)} collective-permute-done((bf16[1,256,1024]{2,1,0:T(8,128)(2,1)S(1)}, bf16[1,256,1024]{2,1,0:T(8,128)(2,1)S(1)}, u32[]{:S(2)}, u32[]{:S(2)}) %collective-permute-start.45) | collective-permute-done | bytes 524320 | tf_op jit(solution)/shard_map/ppermute | solution.py:236
  289.9 5.8 multiply_convert_fusion.1
  295.7 5.8 multiply_convert_fusion
  310.5 3.8 collective-permute-start.49
  314.3 3.8 collective-permute-start.50
  318.1 23.5 %collective-permute-done.49 = bf16[272,1024]{1,0:T(8,128)(2,1)S(1)} collective-permute-done((bf16[272,1024]{1,0:T(8,128)(2,1)}, bf16[272,1024]{1,0:T(8,128)(2,1)S(1)}, u32[]{:S(2)}, u32[]{:S(2)}) %collective-permute-start.49) | collective-permute-done | bytes 557088 | tf_op jit(solution)/shard_map/ppermute | solution.py:268
  352.6 3.8 collective-permute-start.47
  357.1 9.3 %collective-permute-done.47 = bf16[272,1024]{1,0:T(8,128)(2,1)} collective-permute-done((bf16[272,1024]{1,0:T(8,128)(2,1)}, bf16[272,1024]{1,0:T(8,128)(2,1)}, u32[]{:S(2)}, u32[]{:S(2)}) %collective-permute-start.47) | collective-permute-done | bytes 557088 | tf_op jit(solution)/shard_map/ppermute | solution.py:284
  366.4 10.1 %collective-permute-done.48 = bf16[272,1024]{1,0:T(8,128)(2,1)} collective-permute-done((bf16[272,1024]{1,0:T(8,128)(2,1)}, bf16[272,1024]{1,0:T(8,128)(2,1)}, u32[]{:S(2)}, u32[]{:S(2)}) %collective-permute-start.48) | collective-permute-done | bytes 557088 | tf_op jit(solution)/shard_map/ppermute | solution.py:284
  387.9 5.6 convert_reduce_fusion
  406.8 5.6 convert_reduce_fusion.1
  412.4 3.6 convolution_convert_fusion.5
  430.5 6.9 collective-permute-start.52
  441.6 7.4 collective-permute-done.92
  454.6 10.3 %collective-permute-start.93 = (bf16[128,1024]{1,0:T(8,128)(2,1)S(1)}, bf16[128,1024]{1,0:T(8,128)(2,1)S(1)}, u32[]{:S(2)}, u32[]{:S(2)}) collective-permute-start(bf16[128,1024]{1,0:T(8,128)(2,1)S(1)} %get-tuple-element.120), channel_id=1, source_target_pairs={{0,0},{2,1},{4,2},{6,3},{1,4},{3,5},{5,6},{7,7},{8,8},{10,9},{12,1... | collective-permute-start | bytes 786440 | tf_op jit(solution)/shard_map/ppermute | solution.py:330
  471.1 6.9 collective-permute-start.53
  478.3 3.7 collective-permute-start.95
  484.6 4.5 collective-permute-start.83
  493.8 3.5 collective-permute-start.86
  501.0 6.9 collective-permute-done.85
  507.9 8.5 %collective-permute-done.86 = bf16[128,1024]{1,0:T(8,128)(2,1)S(1)} collective-permute-done((bf16[128,1024]{1,0:T(8,128)(2,1)S(1)}, bf16[128,1024]{1,0:T(8,128)(2,1)S(1)}, u32[]{:S(2)}, u32[]{:S(2)}) %collective-permute-start.86) | collective-permute-done | bytes 262176 | tf_op jit(solution)/shard_map/ppermute | solution.py:330
  522.4 14.7 %shard_map.206 = bf16[1088,768]{1,0:T(8,128)(2,1)S(1)} custom-call(bf16[1088,768]{1,0:T(8,128)(2,1)S(1)} %copy-done.1, bf16[1088,768]{1,0:T(8,128)(2,1)S(1)} %copy-done.1, bf16[1088,768]{1,0:T(8,128)(2,1)S(1)} %copy-done.1, bf16[1088,256]{1,0:T(8,128)(2,1)S(1)} %convolution_convert_fusion.do_ref, f32[1088,256]{1,0:T(8,128)S(1)} %copy-done.5, ...), custom_call_target="tpu_custom_call" | custom-call | flops 6060769280 | bytes 5013504 | tf_op jit(solution)/shard_map/pallas_call | solution.py:177
  537.4 4.0 fusion.116
  543.7 15.2 %shard_map.205 = bf16[1088,768]{1,0:T(8,128)(2,1)S(1)} custom-call(bf16[1088,768]{1,0:T(8,128)(2,1)S(1)} %fusion.14.q_ref.k_ref.v_ref, bf16[1088,768]{1,0:T(8,128)(2,1)S(1)} %fusion.14.q_ref.k_ref.v_ref, bf16[1088,768]{1,0:T(8,128)(2,1)S(1)} %fusion.14.q_ref.k_ref.v_ref, bf16[1088,256]{1,0:T(8,128)(2,1)S(1)} %convolution_convert_fusion.1.do_ref, ...), custom_call_target="tpu_custom_call" | custom-call | flops 6060769280 | bytes 5013504 | tf_op jit(solution)/shard_map/pallas_call | solution.py:177
  576.2 14.8 %collective-permute-done.69 = bf16[64,1024]{1,0:T(8,128)(2,1)S(1)} collective-permute-done((bf16[64,1024]{1,0:T(8,128)(2,1)S(1)}, bf16[64,1024]{1,0:T(8,128)(2,1)S(1)}, u32[]{:S(2)}, u32[]{:S(2)}) %collective-permute-start.69) | collective-permute-done | bytes 131104 | tf_op jit(solution)/shard_map/ppermute | solution.py:236
  608.6 5.7 collective-permute-done.62
  614.8 7.0 collective-permute-done.57
  632.4 4.9 fusion.32
  643.8 4.5 collective-permute-start.55
  651.7 111.9 %all-reduce.3.cloned.1.call-done = f32[16,1024]{1,0:T(8,128)} async-done(((f32[16,1024]{1,0:T(8,128)}), f32[16,1024]{1,0:T(8,128)}) %all-reduce.3.cloned.1.call-update) | async-done | bytes 65552 | tf_op jit(solution)/shard_map/psum | solution.py:491
  (539 shorter events, 231.9 us)
Async XLA Ops:
  7.2 756.4 %all-reduce.3.cloned.1.call-start = ((), (), s32[]{:S(2)}) async-start(), calls=%async_computation | async-start | bytes 131072 | tf_op jit(solution)/shard_map/psum | solution.py:491
  8.3 105.3 %collective-permute-start.3 = (bf16[128,768]{0,1:T(8,128)(2,1)S(1)}, bf16[128,768]{0,1:T(8,128)(2,1)S(1)}, u32[]{:S(2)}, u32[]{:S(2)}) collective-permute-start(bf16[128,768]{0,1:T(8,128)(2,1)S(1)} %bitcast.403), channel_id=1, source_target_pairs={{0,0},{1,2},{2,4},{3,6},{4,1},{5,3},{6,5},{7,7},{8,8},{9,10},{10,1... | collective-permute-start | bytes 589832 | tf_op jit(solution)/shard_map/ppermute | solution.py:291
  12.9 107.3 %collective-permute-start.4 = (bf16[128,768]{0,1:T(8,128)(2,1)S(1)}, bf16[128,768]{0,1:T(8,128)(2,1)S(1)}, u32[]{:S(2)}, u32[]{:S(2)}) collective-permute-start(bf16[128,768]{0,1:T(8,128)(2,1)S(1)} %bitcast.404), channel_id=1, source_target_pairs={{0,1},{1,3},{2,5},{3,7},{4,0},{5,2},{6,4},{7,6},{8,9},{9,11},{10,1... | collective-permute-start | bytes 589832 | tf_op jit(solution)/shard_map/ppermute | solution.py:291
  13.0 107.5 %collective-permute-start.5 = (bf16[128,768]{0,1:T(8,128)(2,1)S(1)}, bf16[128,768]{0,1:T(8,128)(2,1)S(1)}, u32[]{:S(2)}, u32[]{:S(2)}) collective-permute-start(bf16[128,768]{0,1:T(8,128)(2,1)S(1)} %bitcast.405), channel_id=1, source_target_pairs={{0,2},{1,0},{2,6},{3,4},{4,3},{5,1},{6,7},{7,5},{8,10},{9,8},{10,1... | collective-permute-start | bytes 589832 | tf_op jit(solution)/shard_map/ppermute | solution.py:291
  15.1 71.1 %collective-permute-start.10 = (s32[2,1088]{1,0:T(2,128)}, s32[2,1088]{1,0:T(2,128)S(1)}, u32[]{:S(2)}, u32[]{:S(2)}) collective-permute-start(s32[2,1088]{1,0:T(2,128)} %param.13), channel_id=1, source_target_pairs={{0,4},{4,0},{8,12},{12,8},{16,20},{20,16},{24,28},{28,24},{1,5},{5... | collective-permute-start | bytes 26120 | tf_op jit(solution)/shard_map/ppermute | solution.py:233
  17.2 74.3 %collective-permute-start.11 = (bf16[32,1024]{1,0:T(8,128)(2,1)}, bf16[32,1024]{1,0:T(8,128)(2,1)S(1)}, u32[]{:S(2)}, u32[]{:S(2)}) collective-permute-start(bf16[32,1024]{1,0:T(8,128)(2,1)} %param.16), channel_id=1, source_target_pairs={{0,0},{1,2},{2,4},{3,6},{4,1},{5,3},{6,5},{7,7},{8,8},{9,10},{10,1... | collective-permute-start | bytes 196616 | tf_op jit(solution)/shard_map/ppermute | solution.py:291
  113.7 23.1 %collective-permute-start.34 = (bf16[128,1024]{1,0:T(8,128)(2,1)}, bf16[128,1024]{1,0:T(8,128)(2,1)}, u32[]{:S(2)}, u32[]{:S(2)}) collective-permute-start(bf16[128,1024]{1,0:T(8,128)(2,1)} %param.19), channel_id=1, source_target_pairs={{0,1},{1,3},{2,5},{3,7},{4,0},{5,2},{6,4},{7,6},{8,9},{9,11},{10,1... | collective-permute-start | bytes 786440 | tf_op jit(solution)/shard_map/ppermute | solution.py:291
  120.3 30.6 %collective-permute-start.35 = (bf16[128,1024]{1,0:T(8,128)(2,1)}, bf16[128,1024]{1,0:T(8,128)(2,1)}, u32[]{:S(2)}, u32[]{:S(2)}) collective-permute-start(bf16[128,1024]{1,0:T(8,128)(2,1)} %param.19), channel_id=1, source_target_pairs={{0,2},{1,0},{2,6},{3,4},{4,3},{5,1},{6,7},{7,5},{8,10},{9,8},{10,1... | collective-permute-start | bytes 786440 | tf_op jit(solution)/shard_map/ppermute | solution.py:291
  120.5 33.3 %collective-permute-start.26 = (bf16[128,1024]{1,0:T(8,128)(2,1)}, bf16[128,1024]{1,0:T(8,128)(2,1)}, u32[]{:S(2)}, u32[]{:S(2)}) collective-permute-start(bf16[128,1024]{1,0:T(8,128)(2,1)} %param.17), channel_id=1, source_target_pairs={{0,0},{1,2},{2,4},{3,6},{4,1},{5,3},{6,5},{7,7},{8,8},{9,10},{10,1... | collective-permute-start | bytes 786440 | tf_op jit(solution)/shard_map/ppermute | solution.py:291
  124.2 40.5 %collective-permute-start.27 = (bf16[128,1024]{1,0:T(8,128)(2,1)}, bf16[128,1024]{1,0:T(8,128)(2,1)}, u32[]{:S(2)}, u32[]{:S(2)}) collective-permute-start(bf16[128,1024]{1,0:T(8,128)(2,1)} %param.17), channel_id=1, source_target_pairs={{0,1},{1,3},{2,5},{3,7},{4,0},{5,2},{6,4},{7,6},{8,9},{9,11},{10,1... | collective-permute-start | bytes 786440 | tf_op jit(solution)/shard_map/ppermute | solution.py:291
  125.7 39.9 %collective-permute-start.28 = (bf16[128,1024]{1,0:T(8,128)(2,1)S(1)}, bf16[128,1024]{1,0:T(8,128)(2,1)S(1)}, u32[]{:S(2)}, u32[]{:S(2)}) collective-permute-start(bf16[128,1024]{1,0:T(8,128)(2,1)S(1)} %copy-done.70), channel_id=1, source_target_pairs={{0,2},{1,0},{2,6},{3,4},{4,3},{5,1},{6,7},{7,5},{8,10},{9,8},{10,1... | collective-permute-start | bytes 786440 | tf_op jit(solution)/shard_map/ppermute | solution.py:291
  136.7 29.4 %collective-permute-start.29 = (bf16[128,1024]{1,0:T(8,128)(2,1)S(1)}, bf16[128,1024]{1,0:T(8,128)(2,1)S(1)}, u32[]{:S(2)}, u32[]{:S(2)}) collective-permute-start(bf16[128,1024]{1,0:T(8,128)(2,1)S(1)} %copy-done.70), channel_id=1, source_target_pairs={{0,3},{1,1},{2,7},{3,5},{4,2},{5,0},{6,6},{7,4},{8,11},{9,9},{10,1... | collective-permute-start | bytes 786440 | tf_op jit(solution)/shard_map/ppermute | solution.py:291
  153.8 34.5 %collective-permute-start = (bf16[272,1024]{1,0:T(8,128)(2,1)S(1)}, bf16[272,1024]{1,0:T(8,128)(2,1)S(1)}, u32[]{:S(2)}, u32[]{:S(2)}) collective-permute-start(bf16[272,1024]{1,0:T(8,128)(2,1)S(1)} %copy-done.56), channel_id=1, source_target_pairs={{0,0},{1,2},{2,4},{3,6},{4,1},{5,3},{6,5},{7,7},{8,8},{9,10},{10,1... | collective-permute-start | bytes 1671176 | tf_op jit(solution)/shard_map/ppermute | solution.py:268
  164.7 23.8 %collective-permute-start.1 = (bf16[272,1024]{1,0:T(8,128)(2,1)S(1)}, bf16[272,1024]{1,0:T(8,128)(2,1)S(1)}, u32[]{:S(2)}, u32[]{:S(2)}) collective-permute-start(bf16[272,1024]{1,0:T(8,128)(2,1)S(1)} %get-tuple-element.118), channel_id=1, source_target_pairs={{0,2},{1,0},{2,6},{3,4},{4,3},{5,1},{6,7},{7,5},{8,10},{9,8},{10,1... | collective-permute-start | bytes 1671176 | tf_op jit(solution)/shard_map/ppermute | solution.py:268
  165.7 24.6 %collective-permute-start.23 = (bf16[1,64,1024]{2,1,0:T(8,128)(2,1)S(1)}, bf16[1,64,1024]{2,1,0:T(8,128)(2,1)S(1)}, u32[]{:S(2)}, u32[]{:S(2)}) collective-permute-start(bf16[1,64,1024]{2,1,0:T(8,128)(2,1)S(1)} %collective-permute-done.21), channel_id=1, source_target_pairs={{0,8},{4,12},{8,0},{12,4},{16,24},{20,28},{24,16},{28,20},{1,9},{5... | collective-permute-start | bytes 393224 | tf_op jit(solution)/shard_map/ppermute | solution.py:236
  166.2 25.6 %collective-permute-start.17 = (bf16[1,64,1024]{2,1,0:T(8,128)(2,1)S(1)}, bf16[1,64,1024]{2,1,0:T(8,128)(2,1)S(1)}, u32[]{:S(2)}, u32[]{:S(2)}) collective-permute-start(bf16[1,64,1024]{2,1,0:T(8,128)(2,1)S(1)} %copy-done.61), channel_id=1, source_target_pairs={{0,16},{4,20},{8,24},{12,28},{16,0},{20,4},{24,8},{28,12},{1,17},{... | collective-permute-start | bytes 393224 | tf_op jit(solution)/shard_map/ppermute | solution.py:236
  166.5 25.6 %collective-permute-start.7 = (bf16[1,256,768]{2,1,0:T(8,128)(2,1)S(1)}, bf16[1,256,768]{2,1,0:T(8,128)(2,1)S(1)}, u32[]{:S(2)}, u32[]{:S(2)}) collective-permute-start(bf16[1,256,768]{2,1,0:T(8,128)(2,1)S(1)} %bitcast.383), channel_id=1, source_target_pairs={{0,8},{4,12},{8,0},{12,4},{16,24},{20,28},{24,16},{28,20},{1,9},{5... | collective-permute-start | bytes 1179656 | tf_op jit(solution)/shard_map/ppermute | solution.py:236
  190.1 23.8 %collective-permute-start.2 = (bf16[544,1024]{1,0:T(8,128)(2,1)S(1)}, bf16[544,1024]{1,0:T(8,128)(2,1)S(1)}, u32[]{:S(2)}, u32[]{:S(2)}) collective-permute-start(bf16[544,1024]{1,0:T(8,128)(2,1)S(1)} %fusion.26), channel_id=1, source_target_pairs={{0,4},{4,0},{8,12},{12,8},{16,20},{20,16},{24,28},{28,24},{1,5},{5... | collective-permute-start | bytes 3342344 | tf_op jit(solution)/shard_map/ppermute | solution.py:233
  204.9 36.0 %collective-permute-start.30 = (bf16[1,256,1024]{2,1,0:T(8,128)(2,1)S(1)}, bf16[1,256,1024]{2,1,0:T(8,128)(2,1)S(1)}, u32[]{:S(2)}, u32[]{:S(2)}) collective-permute-start(bf16[1,256,1024]{2,1,0:T(8,128)(2,1)S(1)} %bitcast.357), channel_id=1, source_target_pairs={{0,8},{4,12},{8,0},{12,4},{16,24},{20,28},{24,16},{28,20},{1,9},{5... | collective-permute-start | bytes 1572872 | tf_op jit(solution)/shard_map/ppermute | solution.py:236
  205.3 37.2 %collective-permute-start.31 = (bf16[1,256,1024]{2,1,0:T(8,128)(2,1)S(1)}, bf16[1,256,1024]{2,1,0:T(8,128)(2,1)S(1)}, u32[]{:S(2)}, u32[]{:S(2)}) collective-permute-start(bf16[1,256,1024]{2,1,0:T(8,128)(2,1)S(1)} %bitcast.358), channel_id=1, source_target_pairs={{0,16},{4,20},{8,24},{12,28},{16,0},{20,4},{24,8},{28,12},{1,17},{... | collective-permute-start | bytes 1572872 | tf_op jit(solution)/shard_map/ppermute | solution.py:236
  213.3 30.4 %collective-permute-start.40 = (bf16[1,256,1024]{2,1,0:T(8,128)(2,1)S(1)}, bf16[1,256,1024]{2,1,0:T(8,128)(2,1)S(1)}, u32[]{:S(2)}, u32[]{:S(2)}) collective-permute-start(bf16[1,256,1024]{2,1,0:T(8,128)(2,1)S(1)} %bitcast.354), channel_id=1, source_target_pairs={{0,16},{4,20},{8,24},{12,28},{16,0},{20,4},{24,8},{28,12},{1,17},{... | collective-permute-start | bytes 1572872 | tf_op jit(solution)/shard_map/ppermute | solution.py:236
  213.4 33.5 %collective-permute-start.41 = (bf16[1,256,1024]{2,1,0:T(8,128)(2,1)S(1)}, bf16[1,256,1024]{2,1,0:T(8,128)(2,1)S(1)}, u32[]{:S(2)}, u32[]{:S(2)}) collective-permute-start(bf16[1,256,1024]{2,1,0:T(8,128)(2,1)S(1)} %bitcast.355), channel_id=1, source_target_pairs={{0,8},{4,12},{8,0},{12,4},{16,24},{20,28},{24,16},{28,20},{1,9},{5... | collective-permute-start | bytes 1572872 | tf_op jit(solution)/shard_map/ppermute | solution.py:236
  243.7 22.8 %collective-permute-start.37 = (bf16[1,256,1024]{2,1,0:T(8,128)(2,1)S(1)}, bf16[1,256,1024]{2,1,0:T(8,128)(2,1)S(1)}, u32[]{:S(2)}, u32[]{:S(2)}) collective-permute-start(bf16[1,256,1024]{2,1,0:T(8,128)(2,1)S(1)} %bitcast.361), channel_id=1, source_target_pairs={{0,8},{4,12},{8,0},{12,4},{16,24},{20,28},{24,16},{28,20},{1,9},{5... | collective-permute-start | bytes 1572872 | tf_op jit(solution)/shard_map/ppermute | solution.py:236
  244.2 23.4 %collective-permute-start.38 = (bf16[1,256,1024]{2,1,0:T(8,128)(2,1)S(1)}, bf16[1,256,1024]{2,1,0:T(8,128)(2,1)S(1)}, u32[]{:S(2)}, u32[]{:S(2)}) collective-permute-start(bf16[1,256,1024]{2,1,0:T(8,128)(2,1)S(1)} %bitcast.362), channel_id=1, source_target_pairs={{0,16},{4,20},{8,24},{12,28},{16,0},{20,4},{24,8},{28,12},{1,17},{... | collective-permute-start | bytes 1572872 | tf_op jit(solution)/shard_map/ppermute | solution.py:236
  246.9 29.6 %collective-permute-start.32 = (bf16[1,256,1024]{2,1,0:T(8,128)(2,1)S(1)}, bf16[1,256,1024]{2,1,0:T(8,128)(2,1)S(1)}, u32[]{:S(2)}, u32[]{:S(2)}) collective-permute-start(bf16[1,256,1024]{2,1,0:T(8,128)(2,1)S(1)} %collective-permute-done.30), channel_id=1, source_target_pairs={{0,16},{4,20},{8,24},{12,28},{16,0},{20,4},{24,8},{28,12},{1,17},{... | collective-permute-start | bytes 1572872 | tf_op jit(solution)/shard_map/ppermute | solution.py:236
  254.0 35.1 %collective-permute-start.25 = (bf16[544,1024]{1,0:T(8,128)(2,1)S(1)}, bf16[544,1024]{1,0:T(8,128)(2,1)S(1)}, u32[]{:S(2)}, u32[]{:S(2)}) collective-permute-start(bf16[544,1024]{1,0:T(8,128)(2,1)S(1)} %add_convert_fusion.1), channel_id=1, source_target_pairs={{0,4},{4,0},{8,12},{12,8},{16,20},{20,16},{24,28},{28,24},{1,5},{5... | collective-permute-start | bytes 3342344 | tf_op jit(solution)/shard_map/ppermute | solution.py:233
  307.8 36.2 %collective-permute-start.46 = (bf16[544,1024]{1,0:T(8,128)(2,1)}, bf16[544,1024]{1,0:T(8,128)(2,1)}, u32[]{:S(2)}, u32[]{:S(2)}) collective-permute-start(bf16[544,1024]{1,0:T(8,128)(2,1)} %dynamic-slice_convert_fusion.2), channel_id=1, source_target_pairs={{0,4},{4,0},{8,12},{12,8},{16,20},{20,16},{24,28},{28,24},{1,5},{5... | collective-permute-start | bytes 3342344 | tf_op jit(solution)/shard_map/ppermute | solution.py:233
  310.5 31.1 %collective-permute-start.49 = (bf16[272,1024]{1,0:T(8,128)(2,1)}, bf16[272,1024]{1,0:T(8,128)(2,1)S(1)}, u32[]{:S(2)}, u32[]{:S(2)}) collective-permute-start(bf16[272,1024]{1,0:T(8,128)(2,1)} %get-tuple-element.111), channel_id=1, source_target_pairs={{0,0},{1,2},{2,4},{3,6},{4,1},{5,3},{6,5},{7,7},{8,8},{9,10},{10,1... | collective-permute-start | bytes 1671176 | tf_op jit(solution)/shard_map/ppermute | solution.py:268
  314.3 27.3 %collective-permute-start.50 = (bf16[272,1024]{1,0:T(8,128)(2,1)}, bf16[272,1024]{1,0:T(8,128)(2,1)}, u32[]{:S(2)}, u32[]{:S(2)}) collective-permute-start(bf16[272,1024]{1,0:T(8,128)(2,1)} %get-tuple-element.110), channel_id=1, source_target_pairs={{0,2},{1,0},{2,6},{3,4},{4,3},{5,1},{6,7},{7,5},{8,10},{9,8},{10,1... | collective-permute-start | bytes 1671176 | tf_op jit(solution)/shard_map/ppermute | solution.py:268
  351.5 27.4 %collective-permute-start.51 = (bf16[544,1024]{1,0:T(8,128)(2,1)}, bf16[544,1024]{1,0:T(8,128)(2,1)}, u32[]{:S(2)}, u32[]{:S(2)}) collective-permute-start(bf16[544,1024]{1,0:T(8,128)(2,1)} %get-tuple-element.69), channel_id=1, source_target_pairs={{0,4},{4,0},{8,12},{12,8},{16,20},{20,16},{24,28},{28,24},{1,5},{5... | collective-permute-start | bytes 3342344 | tf_op jit(solution)/shard_map/ppermute | solution.py:233
  400.3 23.9 %collective-permute-start.91 = (bf16[256,1024]{1,0:T(8,128)(2,1)}, bf16[256,1024]{1,0:T(8,128)(2,1)}, u32[]{:S(2)}, u32[]{:S(2)}) collective-permute-start(bf16[256,1024]{1,0:T(8,128)(2,1)} %get-tuple-element.93), channel_id=1, source_target_pairs={{0,8},{4,12},{8,0},{12,4},{16,24},{20,28},{24,16},{28,20},{1,9},{5... | collective-permute-start | bytes 1572872 | tf_op jit(solution)/shard_map/ppermute | solution.py:236
  401.7 39.8 %collective-permute-start.90 = (bf16[256,1024]{1,0:T(8,128)(2,1)}, bf16[256,1024]{1,0:T(8,128)(2,1)}, u32[]{:S(2)}, u32[]{:S(2)}) collective-permute-start(bf16[256,1024]{1,0:T(8,128)(2,1)} %get-tuple-element.92), channel_id=1, source_target_pairs={{0,8},{4,12},{8,0},{12,4},{16,24},{20,28},{24,16},{28,20},{1,9},{5... | collective-permute-start | bytes 1572872 | tf_op jit(solution)/shard_map/ppermute | solution.py:236
  402.8 24.3 %collective-permute-start.88 = (bf16[256,1024]{1,0:T(8,128)(2,1)}, bf16[256,1024]{1,0:T(8,128)(2,1)}, u32[]{:S(2)}, u32[]{:S(2)}) collective-permute-start(bf16[256,1024]{1,0:T(8,128)(2,1)} %get-tuple-element.95), channel_id=1, source_target_pairs={{0,16},{4,20},{8,24},{12,28},{16,0},{20,4},{24,8},{28,12},{1,17},{... | collective-permute-start | bytes 1572872 | tf_op jit(solution)/shard_map/ppermute | solution.py:236
  405.4 25.1 %collective-permute-start.81 = (bf16[256,1024]{1,0:T(8,128)(2,1)}, bf16[256,1024]{1,0:T(8,128)(2,1)}, u32[]{:S(2)}, u32[]{:S(2)}) collective-permute-start(bf16[256,1024]{1,0:T(8,128)(2,1)} %get-tuple-element.97), channel_id=1, source_target_pairs={{0,8},{4,12},{8,0},{12,4},{16,24},{20,28},{24,16},{28,20},{1,9},{5... | collective-permute-start | bytes 1572872 | tf_op jit(solution)/shard_map/ppermute | solution.py:236
  424.2 28.3 %collective-permute-start.87 = (bf16[256,1024]{1,0:T(8,128)(2,1)}, bf16[256,1024]{1,0:T(8,128)(2,1)S(1)}, u32[]{:S(2)}, u32[]{:S(2)}) collective-permute-start(bf16[256,1024]{1,0:T(8,128)(2,1)} %get-tuple-element.94), channel_id=1, source_target_pairs={{0,16},{4,20},{8,24},{12,28},{16,0},{20,4},{24,8},{28,12},{1,17},{... | collective-permute-start | bytes 1572872 | tf_op jit(solution)/shard_map/ppermute | solution.py:236
  430.5 24.1 %collective-permute-start.52 = (bf16[544,1024]{1,0:T(8,128)(2,1)}, bf16[544,1024]{1,0:T(8,128)(2,1)S(1)}, u32[]{:S(2)}, u32[]{:S(2)}) collective-permute-start(bf16[544,1024]{1,0:T(8,128)(2,1)} %dynamic-slice_convert_fusion.1), channel_id=1, source_target_pairs={{0,4},{4,0},{8,12},{12,8},{16,20},{20,16},{24,28},{28,24},{1,5},{5... | collective-permute-start | bytes 3342344 | tf_op jit(solution)/shard_map/ppermute | solution.py:233
  441.6 29.3 %collective-permute-start.80 = (bf16[256,1024]{1,0:T(8,128)(2,1)S(1)}, bf16[256,1024]{1,0:T(8,128)(2,1)S(1)}, u32[]{:S(2)}, u32[]{:S(2)}) collective-permute-start(bf16[256,1024]{1,0:T(8,128)(2,1)S(1)} %copy-done.59), channel_id=1, source_target_pairs={{0,8},{4,12},{8,0},{12,4},{16,24},{20,28},{24,16},{28,20},{1,9},{5... | collective-permute-start | bytes 1572872 | tf_op jit(solution)/shard_map/ppermute | solution.py:236
  449.0 29.3 %collective-permute-start.77 = (bf16[256,1024]{1,0:T(8,128)(2,1)S(1)}, bf16[256,1024]{1,0:T(8,128)(2,1)S(1)}, u32[]{:S(2)}, u32[]{:S(2)}) collective-permute-start(bf16[256,1024]{1,0:T(8,128)(2,1)S(1)} %copy-done.58), channel_id=1, source_target_pairs={{0,16},{4,20},{8,24},{12,28},{16,0},{20,4},{24,8},{28,12},{1,17},{... | collective-permute-start | bytes 1572872 | tf_op jit(solution)/shard_map/ppermute | solution.py:236
  452.6 29.4 %collective-permute-start.79 = (bf16[256,1024]{1,0:T(8,128)(2,1)S(1)}, bf16[256,1024]{1,0:T(8,128)(2,1)S(1)}, u32[]{:S(2)}, u32[]{:S(2)}) collective-permute-start(bf16[256,1024]{1,0:T(8,128)(2,1)S(1)} %fusion.46), channel_id=1, source_target_pairs={{0,8},{4,12},{8,0},{12,4},{16,24},{20,28},{24,16},{28,20},{1,9},{5... | collective-permute-start | bytes 1572872 | tf_op jit(solution)/shard_map/ppermute | solution.py:236
  454.6 30.0 %collective-permute-start.93 = (bf16[128,1024]{1,0:T(8,128)(2,1)S(1)}, bf16[128,1024]{1,0:T(8,128)(2,1)S(1)}, u32[]{:S(2)}, u32[]{:S(2)}) collective-permute-start(bf16[128,1024]{1,0:T(8,128)(2,1)S(1)} %get-tuple-element.120), channel_id=1, source_target_pairs={{0,0},{2,1},{4,2},{6,3},{1,4},{3,5},{5,6},{7,7},{8,8},{10,9},{12,1... | collective-permute-start | bytes 786440 | tf_op jit(solution)/shard_map/ppermute | solution.py:330
  471.1 46.3 %collective-permute-start.53 = (bf16[544,1024]{1,0:T(8,128)(2,1)S(1)}, bf16[544,1024]{1,0:T(8,128)(2,1)S(1)}, u32[]{:S(2)}, u32[]{:S(2)}) collective-permute-start(bf16[544,1024]{1,0:T(8,128)(2,1)S(1)} %get-tuple-element.71), channel_id=1, source_target_pairs={{0,4},{4,0},{8,12},{12,8},{16,20},{20,16},{24,28},{28,24},{1,5},{5... | collective-permute-start | bytes 3342344 | tf_op jit(solution)/shard_map/ppermute | solution.py:233
  568.0 64.4 %collective-permute-start.54 = (bf16[544,1024]{1,0:T(8,128)(2,1)}, bf16[544,1024]{1,0:T(8,128)(2,1)}, u32[]{:S(2)}, u32[]{:S(2)}) collective-permute-start(bf16[544,1024]{1,0:T(8,128)(2,1)} %dynamic-slice_convert_fusion), channel_id=1, source_target_pairs={{0,4},{4,0},{8,12},{12,8},{16,20},{20,16},{24,28},{28,24},{1,5},{5... | collective-permute-start | bytes 3342344 | tf_op jit(solution)/shard_map/ppermute | solution.py:233
  569.1 25.4 %collective-permute-start.61 = (bf16[256,768]{1,0:T(8,128)(2,1)S(1)}, bf16[256,768]{1,0:T(8,128)(2,1)S(1)}, u32[]{:S(2)}, u32[]{:S(2)}) collective-permute-start(bf16[256,768]{1,0:T(8,128)(2,1)S(1)} %get-tuple-element.101), channel_id=1, source_target_pairs={{0,8},{4,12},{8,0},{12,4},{16,24},{20,28},{24,16},{28,20},{1,9},{5... | collective-permute-start | bytes 1179656 | tf_op jit(solution)/shard_map/ppermute | solution.py:236
  570.0 38.6 %collective-permute-start.60 = (bf16[256,768]{1,0:T(8,128)(2,1)S(1)}, bf16[256,768]{1,0:T(8,128)(2,1)S(1)}, u32[]{:S(2)}, u32[]{:S(2)}) collective-permute-start(bf16[256,768]{1,0:T(8,128)(2,1)S(1)} %get-tuple-element.100), channel_id=1, source_target_pairs={{0,8},{4,12},{8,0},{12,4},{16,24},{20,28},{24,16},{28,20},{1,9},{5... | collective-permute-start | bytes 1179656 | tf_op jit(solution)/shard_map/ppermute | solution.py:236
  575.5 27.7 %collective-permute-start.58 = (bf16[256,768]{1,0:T(8,128)(2,1)S(1)}, bf16[256,768]{1,0:T(8,128)(2,1)S(1)}, u32[]{:S(2)}, u32[]{:S(2)}) collective-permute-start(bf16[256,768]{1,0:T(8,128)(2,1)S(1)} %get-tuple-element.103), channel_id=1, source_target_pairs={{0,16},{4,20},{8,24},{12,28},{16,0},{20,4},{24,8},{28,12},{1,17},{... | collective-permute-start | bytes 1179656 | tf_op jit(solution)/shard_map/ppermute | solution.py:236
  624.2 24.2 %collective-permute-start.63 = (bf16[128,768]{0,1:T(8,128)(2,1)}, bf16[128,768]{0,1:T(8,128)(2,1)}, u32[]{:S(2)}, u32[]{:S(2)}) collective-permute-start(bf16[128,768]{0,1:T(8,128)(2,1)} %get-tuple-element.132), channel_id=1, source_target_pairs={{0,0},{2,1},{4,2},{6,3},{1,4},{3,5},{5,6},{7,7},{8,8},{10,9},{12,1... | collective-permute-start | bytes 589832 | tf_op jit(solution)/shard_map/ppermute | solution.py:330
  643.8 125.2 %collective-permute-start.55 = (bf16[272,1024]{1,0:T(8,128)(2,1)S(1)}, bf16[272,1024]{1,0:T(8,128)(2,1)S(1)}, u32[]{:S(2)}, u32[]{:S(2)}) collective-permute-start(bf16[272,1024]{1,0:T(8,128)(2,1)S(1)} %get-tuple-element.106), channel_id=1, source_target_pairs={{0,0},{2,1},{4,2},{6,3},{1,4},{3,5},{5,6},{7,7},{8,8},{10,9},{12,1... | collective-permute-start | bytes 1671176 | tf_op jit(solution)/shard_map/ppermute | solution.py:284
  648.4 120.7 %collective-permute-start.56 = (bf16[272,1024]{1,0:T(8,128)(2,1)S(1)}, bf16[272,1024]{1,0:T(8,128)(2,1)S(1)}, u32[]{:S(2)}, u32[]{:S(2)}) collective-permute-start(bf16[272,1024]{1,0:T(8,128)(2,1)S(1)} %get-tuple-element.107), channel_id=1, source_target_pairs={{2,0},{0,1},{6,2},{4,3},{3,4},{1,5},{7,6},{5,7},{10,8},{8,9},{14,1... | collective-permute-start | bytes 1671176 | tf_op jit(solution)/shard_map/ppermute | solution.py:284
  (133 other events, 1783.5 us)
Sparse Core Ops, SparseCore 0:
  640.1 123.4 all-reduce.2

commit v2 on v1

--- a/solution.py
+++ b/solution.py
@@ -198,6 +198,251 @@
     )(qkv, qkv, qkv, grad_o, lse, seg_c, seg_r)
 
 
+MESH = pl.DeviceIdType.MESH
+
+
+def plan_hops(groups, which):
+    bits = [1 << b for b in range(groups.bit_length() - 1)]
+    if len(bits) == 2 and which:
+        bits = bits[::-1]
+    known = [0]
+    steps = []
+    for bit in bits:
+        steps.append((bit, list(known)))
+        known = known + [rel ^ bit for rel in known]
+    return steps
+
+
+class Links:
+    def __init__(self, n_dp, n_mp, send_sems):
+        self.n_dp, self.n_mp = n_dp, n_mp
+        self.dp = lax.axis_index("dp")
+        self.z = lax.axis_index("mp")
+        self.core = lax.rem(self.dp, 2)
+        self.group = self.dp // 2
+        self.send_sems = send_sems
+        self.used = 0
+        self.open = []
+
+    def barrier(self):
+        sem = pltpu.get_barrier_semaphore()
+        count = 0
+        for cc in range(2):
+            for zz in range(self.n_mp):
+
+                @pl.when(jnp.logical_or(cc != self.core, zz != self.z))
+                def _(cc=cc, zz=zz):
+                    pl.semaphore_signal(
+                        sem, inc=1, device_id=(2 * self.group + cc, zz), device_id_type=MESH
+                    )
+
+                count += 1
+        bit = 1
+        while bit < self.n_dp // 2:
+            pl.semaphore_signal(
+                sem, inc=1, device_id=(self.dp ^ (2 * bit), self.z), device_id_type=MESH
+            )
+            count += 1
+            bit *= 2
+        pl.semaphore_wait(sem, count - 1)
+
+    def send(self, src, dst, recv_sem, dp, z):
+        copy = pltpu.make_async_remote_copy(
+            src_ref=src,
+            dst_ref=dst,
+            send_sem=self.send_sems.at[self.used],
+            recv_sem=recv_sem,
+            device_id=(dp, z),
+            device_id_type=MESH,
+        )
+        copy.start()
+        self.used += 1
+        self.open.append((None, copy))
+
+    def send_or_keep(self, src, dst, recv_sem, dp, z):
+        own = jnp.logical_and(dp == self.dp, z == self.z)
+        copy = pltpu.make_async_remote_copy(
+            src_ref=src,
+            dst_ref=dst,
+            send_sem=self.send_sems.at[self.used],
+            recv_sem=recv_sem,
+            device_id=(dp, z),
+            device_id_type=MESH,
+        )
+        here = pltpu.make_async_copy(src, dst, recv_sem)
+
+        @pl.when(jnp.logical_not(own))
+        def _():
+            copy.start()
+
+        @pl.when(own)
+        def _():
+            here.start()
+
+        self.used += 1
+        self.open.append((own, copy))
+
+    def arrived(self, src, dst, recv_sem):
+        pltpu.make_async_remote_copy(
+            src_ref=src,
+            dst_ref=dst,
+            send_sem=self.send_sems.at[0],
+            recv_sem=recv_sem,
+            device_id=(self.dp ^ 1, self.z),
+            device_id_type=MESH,
+        ).wait_recv()
+
+    def finish(self):
+        for own, copy in self.open:
+            if own is None:
+                copy.wait_send()
+            else:
+
+                @pl.when(jnp.logical_not(own))
+                def _(copy=copy):
+                    copy.wait_send()
+
+        self.open = []
+
+
+def rows_at(index, rows):
+    return pl.ds(pl.multiple_of(index * rows, rows), rows)
+
+
+class Gather:
+    def __init__(self, links, src, dst, col_sems, hop_sems):
+        self.links, self.src, self.dst = links, src, dst
+        self.rows = src.shape[0]
+        self.col_sems, self.hop_sems = col_sems, hop_sems
+        self.groups = links.n_dp // 2
+
+    def column(self):
+        k = self.links
+        i = lax.rem(k.z, 2)
+        for zz in range(k.n_mp):
+            k.send_or_keep(
+                self.src,
+                self.dst.at[i, rows_at(k.dp, self.rows), :],
+                self.col_sems.at[i, k.core],
+                2 * k.group + k.z // 2,
+                zz,
+            )
+
+    def piece(self, i, group):
+        return self.dst.at[i, rows_at(group, 2 * self.rows), :]
+
+    def column_wait(self, i):
+        for c in range(2):
+            self.links.arrived(
+                self.src,
+                self.dst.at[i, rows_at(2 * self.links.group + c, self.rows), :],
+                self.col_sems.at[i, c],
+            )
+
+    def hop(self, i, rel, bit):
+        k = self.links
+        piece = self.piece(i, k.group ^ rel)
+        k.send(piece, piece, self.hop_sems.at[i, rel ^ bit], k.dp ^ (2 * bit), k.z)
+
+    def hop_wait(self, i, rel):
+        piece = self.piece(i, self.links.group ^ rel)
+        self.links.arrived(piece, piece, self.hop_sems.at[i, rel])
+
+    def first(self):
+        for i in range(2):
+            self.column_wait(i)
+            for bit, _ in plan_hops(self.groups, i):
+                self.hop(i, 0, bit)
+
+    def second(self):
+        steps = [plan_hops(self.groups, i) for i in range(2)]
+        self.waited = [set(), set()]
+        for level in range(1, len(steps[0])):
+            for i in range(2):
+                bit, known = steps[i][level]
+                for rel in known[1:]:
+                    if rel not in self.waited[i]:
+                        self.hop_wait(i, rel)
+                        self.waited[i].add(rel)
+                    self.hop(i, rel, bit)
+
+    def last(self):
+        for i in range(2):
+            for rel in range(1, self.groups):
+                if rel not in self.waited[i]:
+                    self.hop_wait(i, rel)
+
+
+def exchange_tokens(links, src, dst, sems):
+    quarter = src.shape[1]
+    for m in range(2):
+        links.send_or_keep(
+            src.at[m],
+            dst.at[rows_at(lax.rem(links.z, 2), quarter), :],
+            sems.at[lax.rem(links.z, 2)],
+            2 * links.group + links.z // 2,
+            2 * m + links.core,
+        )
+
+
+def exchange_tokens_wait(links, src, dst, sems):
+    quarter = src.shape[1]
+    for s in range(2):
+        links.arrived(src.at[0], dst.at[pl.ds(s * quarter, quarter), :], sems.at[s])
+
+
+def gather_kernel(n_dp, n_mp, *refs):
+    tokens, grads = refs[0:2]
+    blocks = refs[2:7]
+    x_out, g_out = refs[7:9]
+    fulls = refs[9:14]
+    send_sems, col_sems, hop_sems, tok_sems = refs[14:18]
+    links = Links(n_dp, n_mp, send_sems)
+    links.barrier()
+    ways = [
+        Gather(links, blocks[a], fulls[a], col_sems.at[a], hop_sems.at[a]) for a in range(5)
+    ]
+    ways[0].column()
+    ways[1].column()
+    exchange_tokens(links, tokens, x_out, tok_sems.at[0])
+    for way in ways[2:]:
+        way.column()
+    exchange_tokens(links, grads, g_out, tok_sems.at[1])
+    ways[0].first()
+    for a in range(1, 5):
+        ways[a].first()
+        ways[a - 1].second()
+    ways[4].second()
+    exchange_tokens_wait(links, tokens, x_out, tok_sems.at[0])
+    exchange_tokens_wait(links, grads, g_out, tok_sems.at[1])
+    for way in ways:
+        way.last()
+    links.finish()
+
+
+def gather_all(n_dp, n_mp, tokens, grads, blocks):
+    groups = n_dp // 2
+    hops = groups - 1
+    any_spec = pl.BlockSpec(memory_space=pl.ANY)
+    half = (2 * tokens.shape[1], tokens.shape[2])
+    shapes = [jax.ShapeDtypeStruct(half, tokens.dtype)] * 2 + [
+        jax.ShapeDtypeStruct((2, n_dp * b.shape[0], b.shape[1]), b.dtype) for b in blocks
+    ]
+    return pl.pallas_call(
+        functools.partial(gather_kernel, n_dp, n_mp),
+        in_specs=[any_spec] * 7,
+        out_specs=[any_spec] * 7,
+        out_shape=shapes,
+        scratch_shapes=[
+            pltpu.SemaphoreType.DMA((4 + 5 * (n_mp + 2 * hops),)),
+            pltpu.SemaphoreType.DMA((5, 2, 2)),
+            pltpu.SemaphoreType.DMA((5, 2, groups)),
+            pltpu.SemaphoreType.DMA((2, 2)),
+        ],
+        compiler_params=pltpu.CompilerParams(collective_id=0, has_side_effects=True),
+    )(tokens, grads, *blocks)
+
+
 def build(n_dp, n_mp):
     groups = n_dp // 2
     bits = [1 << b for b in range(groups.bit_length() - 1)]
@@ -340,9 +585,6 @@
             ours = lax.dynamic_slice_in_dim(partial, core * half, half, 0)
             return ours.astype(F32) + swap(theirs.astype(BF)).astype(F32)
 
-        x = to_rows(tokens).astype(F32)
-        grad_y = to_rows(out_grad).astype(F32)
-
         per_qv = qv_bias.shape[1]
         slim = width // n_dp
         rows = [
@@ -357,29 +599,32 @@
             )
         ]
         small = jnp.concatenate(rows, axis=0)
-        every = lax.all_gather(small, both, axis=0)
-        every = every.reshape(n_dp, n_mp, *small.shape).astype(F32)
-        wide = every[:, 0, :, :slim].transpose(1, 0, 2).reshape(small.shape[0], width)
+        small = jnp.pad(small, ((0, 16 - small.shape[0]), (0, 0)))
+        small = jnp.pad(small, ((0, 0), (0, max(0, 128 - small.shape[1]))))
+        block_qkv = qkv_weight.transpose(1, 0, 2).reshape(qkv_weight.shape[1], -1)
+        x, grad_y, every, w_qkv, w_out, w_up, w_down = gather_all(
+            n_dp,
+            n_mp,
+            tokens,
+            out_grad,
+            [small, block_qkv, out_weight, up_weight, down_weight],
+        )
+        x = x.astype(F32)
+        grad_y = grad_y.astype(F32)
+        every = every.reshape(2, n_dp, *small.shape).astype(F32)
+        wide = every[0, :, :, :slim].transpose(1, 0, 2).reshape(small.shape[0], width)
         gains = wide[2:6]
         shifts = wide[6:10]
         branch_b = wide[10:12]
-        served = lax.dynamic_slice_in_dim(every, 2 * core, 2, 1)
-        qv_b = served[:, :, 0, : 2 * per_qv].reshape(n_dp, 2, 2, per_qv)
-        qv_b = qv_b.transpose(1, 2, 0, 3).reshape(2, 2, n_dp * per_qv)
-        up_b = served[:, :, 1, : up_bias.shape[0]].transpose(1, 0, 2).reshape(2, -1)
+        qv_b = every[:, :, 0, : 2 * per_qv].reshape(2, n_dp, 2, per_qv)
+        qv_b = qv_b.transpose(0, 2, 1, 3).reshape(2, 2, n_dp * per_qv)
+        up_b = every[:, :, 1, : up_bias.shape[0]].reshape(2, -1)
 
         seg_other = swap(seg_ids)
         seg_own = pick2((core + z) % 2, seg_ids, seg_other)
         seg_row = lax.dynamic_index_in_dim(seg_own, z // 2, 0, keepdims=False)
         seg_r = jnp.broadcast_to(seg_row[None, :], (8, length))
         seg_c = jnp.broadcast_to(seg_row[length - CAPTION :, None], (CAPTION, 128))
-
-        block_qkv = qkv_weight.transpose(1, 0, 2).reshape(qkv_weight.shape[1], -1)
-        w_qkv = gather(block_qkv)
-        n_out = out_weight.shape[0]
-        w_out = gather(out_weight)
-        w_up = gather(up_weight)
-        w_down = gather(down_weight)
 
         unit0, inv0 = stats(x)
         h1 = share((unit0 * gains[0] + shifts[0]).astype(BF))

time: 788 us -> 666 us (0.85)
  Pallas kernels: 47.3 us -> 180 us
  waiting for transfers between devices: 319 us -> 201 us
  starting transfers between devices: 172 us -> 101 us
  blocking collectives: 61.5 us -> 0 us
    pallas_call x0 -> x1, Pallas kernels: none -> 132 us  [gather_all(): pl.pallas_call(functools.partial(gather_kernel, n_dp, n_mp), in_specs=[an...]
    ppermute x48 -> x24, waiting for transfers between devices: 104 us -> 39 us  [hop(): return lax.ppermute(value, 'dp', [(i, i ^ 2 * bit) for i in range(n_dp)])]
    ppermute x20 -> x0, starting transfers between devices: 63.3 us -> none  [the longest x16 53.8 us: gather(): got = [lax.ppermute(block, both, weight_out[k]) for k in range(n_mp)]]
    all_gather x1 -> x0, blocking collectives: 61.5 us -> none  [on_device(): every = lax.all_gather(small, both, axis=0)]
    ppermute x20 -> x0, waiting for transfers between devices: 59.6 us -> none  [the longest x4 43.8 us: to_rows(): got.append(lax.ppermute(mine, both, token_out[k]))]
    ppermute x48 -> x24, starting transfers between devices: 32.7 us -> 18.1 us  [hop(): return lax.ppermute(value, 'dp', [(i, i ^ 2 * bit) for i in range(n_dp)])]
    ppermute x9, waiting for transfers between devices: 0.02 us -> 9.76 us  [swap(): return lax.ppermute(value, 'dp', [(i, i ^ 1) for i in range(n_dp)])]
  transfers between devices with their start and end apart: 98 -> 54, of which waited for: 33 -> 19; matrix products, arithmetic and copies ran while one was open for 12% -> 10% of each run, Pallas kernels for 2% -> 0%
where the time goes in v2:
time: 666 us; the launch traced here: 659 us
  waiting for transfers between devices  201 us (30%)
  Pallas kernels  180 us (27%)
  starting transfers between devices  101 us (15%)
  matrix products  68.1 us (10%)
  other arithmetic  54.6 us (8%)
  local copies, waits for them, and re-layouts  38.5 us (6%)
  between operations  16.1 us (2%)
    pallas_call x1, Pallas kernels, gather_all(): pl.pallas_call(functools.partial(gather_kernel, n_dp, n_mp), in_specs=[an...  132 us
    psum x1, waiting for transfers between devices, on_device(): vectors = lax.psum(vectors, both)  113 us
    ppermute x16, starting transfers between devices, scatter(): got = lax.ppermute(mine, both, weight_in[k]).astype(F32)  50.6 us
    ppermute x24, waiting for transfers between devices, hop(): return lax.ppermute(value, 'dp', [(i, i ^ 2 * bit) for i in range(n_dp)])  39 us
    pallas_call x2, Pallas kernels, attend_backward(): pl.pallas_call(attend_bwd_kernel, grid=(pairs,), in_specs=[col(0), col(pa...  29.8 us
    dot_general x8, matrix products, dot_nn(): lax.dot_general(a, b, (((1,), (0,)), ((), ())), preferred_element_type=F32)  25.9 us
    dot_general x8, matrix products, dot_nt(): lax.dot_general(a, b, (((1,), (1,)), ((), ())), preferred_element_type=F32)  22.6 us
    ppermute x16, waiting for transfers between devices, scatter(): got = lax.ppermute(mine, both, weight_in[k]).astype(F32)  20.5 us
  transfers between devices with their start and end apart: 54, of which 19 were waited for; matrix products, arithmetic and copies ran while one was open for 10% of the time, Pallas kernels for 0%

profile of v2, /device:TPU:1, one launch (start us, length us, event | category | flops | bytes accessed | tf_op | source)
XLA Modules:
  0.0 659.3 jit_solution(6807013235020924695)
XLA Ops:
  12.7 132.2 %shard_map.203 = (bf16[544,1024]{1,0:T(8,128)(2,1)}, bf16[544,1024]{1,0:T(8,128)(2,1)}, bf16[2,128,128]{2,1,0:T(8,128)(2,1)}, bf16[2,1024,768]{2,1,0:T(8,128)(2,...) custom-call(bf16[2,272,1024]{2,1,0:T(8,128)(2,1)} %refs_0_.1, ...), custom_call_target="tpu_custom_call" | custom-call | tf_op jit(solution)/shard_map/pallas_call | solution.py:431
  158.4 8.7 %shard_map.205 = (bf16[1088,256]{1,0:T(8,128)(2,1)S(1)}, f32[1088,256]{1,0:T(8,128)S(1)}) custom-call(bf16[1088,768]{1,0:T(8,128)(2,1)S(1)} %fusion.15.q_ref.k_ref.v_ref, bf16[1088,768]{1,0:T(8,128)(2,1)S(1)} %fusion.15.q_ref.k_ref.v_ref, bf16[1088,768]{1,0:T(8,128)(2,1)S(1)} %fusion.15.q_ref.k_ref.v_ref, s32[64,128]{1,0:T(8,128)S(1)} %broadcast_in_dim.13.segc_ref, ...), custom_call_target="tpu_custom_call" | custom-call | flops 2424307712 | bytes 2785280 | tf_op jit(solution)/shard_map/pallas_call | solution.py:154
  168.1 9.0 %shard_map.204 = (bf16[1088,256]{1,0:T(8,128)(2,1)S(1)}, f32[1088,256]{1,0:T(8,128)S(1)}) custom-call(bf16[1088,768]{1,0:T(8,128)(2,1)S(1)} %fusion.14.q_ref.k_ref.v_ref, bf16[1088,768]{1,0:T(8,128)(2,1)S(1)} %fusion.14.q_ref.k_ref.v_ref, bf16[1088,768]{1,0:T(8,128)(2,1)S(1)} %fusion.14.q_ref.k_ref.v_ref, s32[64,128]{1,0:T(8,128)S(1)} %broadcast_in_dim.13.segc_ref, ...), custom_call_target="tpu_custom_call" | custom-call | flops 2424307712 | bytes 2785280 | tf_op jit(solution)/shard_map/pallas_call | solution.py:154
  178.1 2.8 convolution_add_fusion
  181.0 2.8 dynamic-slice_convert_fusion.3
  184.2 2.7 collective-permute-done.2
  196.6 5.6 multiply_convert_fusion
  202.2 5.8 multiply_convert_fusion.1
  210.5 4.6 convolution_add_fusion.3
  215.1 2.8 dynamic-slice_convert_fusion.2
  218.3 2.7 collective-permute-done.4
  230.3 10.5 %collective-permute-start.5 = (bf16[272,1024]{1,0:T(8,128)(2,1)}, bf16[272,1024]{1,0:T(8,128)(2,1)S(1)}, u32[]{:S(2)}, u32[]{:S(2)}) collective-permute-start(bf16[272,1024]{1,0:T(8,128)(2,1)} %get-tuple-element.113), channel_id=1, source_target_pairs={{0,0},{2,1},{4,2},{6,3},{1,4},{3,5},{5,6},{7,7},{8,8},{10,9},{12,1... | collective-permute-start | bytes 1671176 | tf_op jit(solution)/shard_map/ppermute | solution.py:529
  242.1 11.0 %collective-permute-done.5 = bf16[272,1024]{1,0:T(8,128)(2,1)S(1)} collective-permute-done((bf16[272,1024]{1,0:T(8,128)(2,1)}, bf16[272,1024]{1,0:T(8,128)(2,1)S(1)}, u32[]{:S(2)}, u32[]{:S(2)}) %collective-permute-start.5) | collective-permute-done | bytes 557088 | tf_op jit(solution)/shard_map/ppermute | solution.py:529
  253.1 7.9 %collective-permute-done.6 = bf16[272,1024]{1,0:T(8,128)(2,1)} collective-permute-done((bf16[272,1024]{1,0:T(8,128)(2,1)}, bf16[272,1024]{1,0:T(8,128)(2,1)}, u32[]{:S(2)}, u32[]{:S(2)}) %collective-permute-start.6) | collective-permute-done | bytes 557088 | tf_op jit(solution)/shard_map/ppermute | solution.py:529
  265.5 3.3 convolution_convert_fusion.2
  268.9 3.2 convolution_convert_fusion.3
  272.1 5.0 convert_reduce_fusion.1
  277.2 3.1 convolution_convert_fusion.5
  286.8 5.0 convert_reduce_fusion
  291.9 3.6 convolution_convert_fusion.4
  310.1 3.8 collective-permute-done.37
  313.9 7.2 %collective-permute-start.8 = (bf16[544,1024]{1,0:T(8,128)(2,1)}, bf16[544,1024]{1,0:T(8,128)(2,1)S(1)}, u32[]{:S(2)}, u32[]{:S(2)}) collective-permute-start(bf16[544,1024]{1,0:T(8,128)(2,1)} %dynamic-slice_convert_fusion.1), channel_id=1, source_target_pairs={{0,4},{4,0},{8,12},{12,8},{16,20},{20,16},{24,28},{28,24},{1,5},{5... | collective-permute-start | bytes 3342344 | tf_op jit(solution)/shard_map/ppermute | solution.py:478
  325.3 4.6 collective-permute-done.48
  336.2 11.7 %collective-permute-start.49 = (bf16[128,1024]{1,0:T(8,128)(2,1)S(1)}, bf16[128,1024]{1,0:T(8,128)(2,1)S(1)}, u32[]{:S(2)}, u32[]{:S(2)}) collective-permute-start(bf16[128,1024]{1,0:T(8,128)(2,1)S(1)} %get-tuple-element.115), channel_id=1, source_target_pairs={{0,0},{2,1},{4,2},{6,3},{1,4},{3,5},{5,6},{7,7},{8,8},{10,9},{12,1... | collective-permute-start | bytes 786440 | tf_op jit(solution)/shard_map/ppermute | solution.py:575
  353.9 5.6 collective-permute-start.9
  359.7 3.1 collective-permute-start.51
  365.4 4.5 collective-permute-start.39
  370.5 2.7 collective-permute-start.41
  374.6 5.7 collective-permute-start.42
  381.2 4.1 collective-permute-done.40
  385.3 3.4 collective-permute-done.41
  388.7 8.8 %collective-permute-done.42 = bf16[128,1024]{1,0:T(8,128)(2,1)S(1)} collective-permute-done((bf16[128,1024]{1,0:T(8,128)(2,1)S(1)}, bf16[128,1024]{1,0:T(8,128)(2,1)S(1)}, u32[]{:S(2)}, u32[]{:S(2)}) %collective-permute-start.42) | collective-permute-done | bytes 262176 | tf_op jit(solution)/shard_map/ppermute | solution.py:575
  403.4 14.7 %shard_map.206 = bf16[1088,768]{1,0:T(8,128)(2,1)S(1)} custom-call(bf16[1088,768]{1,0:T(8,128)(2,1)S(1)} %copy-done.1, bf16[1088,768]{1,0:T(8,128)(2,1)S(1)} %copy-done.1, bf16[1088,768]{1,0:T(8,128)(2,1)S(1)} %copy-done.1, bf16[1088,256]{1,0:T(8,128)(2,1)S(1)} %convolution_convert_fusion.1.do_ref, f32[1088,256]{1,0:T(8,128)S(1)} %copy-done.5, ...), custom_call_target="tpu_custom_call" | custom-call | flops 6060769280 | bytes 5013504 | tf_op jit(solution)/shard_map/pallas_call | solution.py:177
  418.4 4.0 fusion.60
  422.5 15.1 %shard_map.207 = bf16[1088,768]{1,0:T(8,128)(2,1)S(1)} custom-call(bf16[1088,768]{1,0:T(8,128)(2,1)S(1)} %fusion.15.q_ref.k_ref.v_ref, bf16[1088,768]{1,0:T(8,128)(2,1)S(1)} %fusion.15.q_ref.k_ref.v_ref, bf16[1088,768]{1,0:T(8,128)(2,1)S(1)} %fusion.15.q_ref.k_ref.v_ref, bf16[1088,256]{1,0:T(8,128)(2,1)S(1)} %convolution_convert_fusion.do_ref, ...), custom_call_target="tpu_custom_call" | custom-call | flops 6060769280 | bytes 5013504 | tf_op jit(solution)/shard_map/pallas_call | solution.py:177
  452.1 2.6 collective-permute-done.28
  456.4 14.3 %collective-permute-done.25 = bf16[64,1024]{1,0:T(8,128)(2,1)S(1)} collective-permute-done((bf16[64,1024]{1,0:T(8,128)(2,1)S(1)}, bf16[64,1024]{1,0:T(8,128)(2,1)S(1)}, u32[]{:S(2)}, u32[]{:S(2)}) %collective-permute-start.25) | collective-permute-done | bytes 131104 | tf_op jit(solution)/shard_map/ppermute | solution.py:481
  470.9 4.2 collective-permute-start.29
  475.1 3.0 collective-permute-start.30
  478.3 3.2 collective-permute-start.31
  485.2 2.7 collective-permute-done.32
  489.8 4.9 collective-permute-done.18
  495.1 7.0 %collective-permute-done.13 = bf16[256,768]{1,0:T(8,128)(2,1)S(1)} collective-permute-done((bf16[256,768]{1,0:T(8,128)(2,1)S(1)}, bf16[256,768]{1,0:T(8,128)(2,1)S(1)}, u32[]{:S(2)}, u32[]{:S(2)}) %collective-permute-start.13) | collective-permute-done | bytes 393248 | tf_op jit(solution)/shard_map/ppermute | solution.py:481
  504.5 2.9 collective-permute-start.19
  512.7 4.8 fusion.32
  517.5 2.7 concatenate.52
  524.1 4.5 collective-permute-start.11
  532.0 113.1 %all-reduce.4.cloned.1.call-done = f32[16,1024]{1,0:T(8,128)} async-done(((f32[16,1024]{1,0:T(8,128)}), f32[16,1024]{1,0:T(8,128)}) %all-reduce.4.cloned.1.call-update) | async-done | bytes 65552 | tf_op jit(solution)/shard_map/psum | solution.py:736
  (342 shorter events, 141.9 us)
Async XLA Ops:
  7.2 637.8 %all-reduce.4.cloned.1.call-start = ((), (), s32[]{:S(2)}) async-start(), calls=%async_computation | async-start | bytes 131072 | tf_op jit(solution)/shard_map/psum | solution.py:736
  228.9 34.3 %collective-permute-start.7 = (bf16[544,1024]{1,0:T(8,128)(2,1)}, bf16[544,1024]{1,0:T(8,128)(2,1)}, u32[]{:S(2)}, u32[]{:S(2)}) collective-permute-start(bf16[544,1024]{1,0:T(8,128)(2,1)} %get-tuple-element.72), channel_id=1, source_target_pairs={{0,4},{4,0},{8,12},{12,8},{16,20},{20,16},{24,28},{28,24},{1,5},{5... | collective-permute-start | bytes 3342344 | tf_op jit(solution)/shard_map/ppermute | solution.py:478
  230.3 22.8 %collective-permute-start.5 = (bf16[272,1024]{1,0:T(8,128)(2,1)}, bf16[272,1024]{1,0:T(8,128)(2,1)S(1)}, u32[]{:S(2)}, u32[]{:S(2)}) collective-permute-start(bf16[272,1024]{1,0:T(8,128)(2,1)} %get-tuple-element.113), channel_id=1, source_target_pairs={{0,0},{2,1},{4,2},{6,3},{1,4},{3,5},{5,6},{7,7},{8,8},{10,9},{12,1... | collective-permute-start | bytes 1671176 | tf_op jit(solution)/shard_map/ppermute | solution.py:529
  240.8 20.2 %collective-permute-start.6 = (bf16[272,1024]{1,0:T(8,128)(2,1)}, bf16[272,1024]{1,0:T(8,128)(2,1)}, u32[]{:S(2)}, u32[]{:S(2)}) collective-permute-start(bf16[272,1024]{1,0:T(8,128)(2,1)} %get-tuple-element.114), channel_id=1, source_target_pairs={{2,0},{0,1},{6,2},{4,3},{3,4},{1,5},{7,6},{5,7},{10,8},{8,9},{14,1... | collective-permute-start | bytes 1671176 | tf_op jit(solution)/shard_map/ppermute | solution.py:529
  284.0 21.6 %collective-permute-start.47 = (bf16[256,1024]{1,0:T(8,128)(2,1)}, bf16[256,1024]{1,0:T(8,128)(2,1)}, u32[]{:S(2)}, u32[]{:S(2)}) collective-permute-start(bf16[256,1024]{1,0:T(8,128)(2,1)} %get-tuple-element.96), channel_id=1, source_target_pairs={{0,8},{4,12},{8,0},{12,4},{16,24},{20,28},{24,16},{28,20},{1,9},{5... | collective-permute-start | bytes 1572872 | tf_op jit(solution)/shard_map/ppermute | solution.py:481
  284.3 39.8 %collective-permute-start.46 = (bf16[256,1024]{1,0:T(8,128)(2,1)}, bf16[256,1024]{1,0:T(8,128)(2,1)S(1)}, u32[]{:S(2)}, u32[]{:S(2)}) collective-permute-start(bf16[256,1024]{1,0:T(8,128)(2,1)} %get-tuple-element.95), channel_id=1, source_target_pairs={{0,8},{4,12},{8,0},{12,4},{16,24},{20,28},{24,16},{28,20},{1,9},{5... | collective-permute-start | bytes 1572872 | tf_op jit(solution)/shard_map/ppermute | solution.py:481
  286.5 21.7 %collective-permute-start.44 = (bf16[256,1024]{1,0:T(8,128)(2,1)}, bf16[256,1024]{1,0:T(8,128)(2,1)}, u32[]{:S(2)}, u32[]{:S(2)}) collective-permute-start(bf16[256,1024]{1,0:T(8,128)(2,1)} %get-tuple-element.98), channel_id=1, source_target_pairs={{0,16},{4,20},{8,24},{12,28},{16,0},{20,4},{24,8},{28,12},{1,17},{... | collective-permute-start | bytes 1572872 | tf_op jit(solution)/shard_map/ppermute | solution.py:481
  296.6 17.3 %collective-permute-start.37 = (bf16[256,1024]{1,0:T(8,128)(2,1)}, bf16[256,1024]{1,0:T(8,128)(2,1)}, u32[]{:S(2)}, u32[]{:S(2)}) collective-permute-start(bf16[256,1024]{1,0:T(8,128)(2,1)} %get-tuple-element.100), channel_id=1, source_target_pairs={{0,8},{4,12},{8,0},{12,4},{16,24},{20,28},{24,16},{28,20},{1,9},{5... | collective-permute-start | bytes 1572872 | tf_op jit(solution)/shard_map/ppermute | solution.py:481
  298.7 22.4 %collective-permute-start.34 = (bf16[256,1024]{1,0:T(8,128)(2,1)}, bf16[256,1024]{1,0:T(8,128)(2,1)}, u32[]{:S(2)}, u32[]{:S(2)}) collective-permute-start(bf16[256,1024]{1,0:T(8,128)(2,1)} %get-tuple-element.102), channel_id=1, source_target_pairs={{0,16},{4,20},{8,24},{12,28},{16,0},{20,4},{24,8},{28,12},{1,17},{... | collective-permute-start | bytes 1572872 | tf_op jit(solution)/shard_map/ppermute | solution.py:481
  305.6 26.6 %collective-permute-start.43 = (bf16[256,1024]{1,0:T(8,128)(2,1)}, bf16[256,1024]{1,0:T(8,128)(2,1)S(1)}, u32[]{:S(2)}, u32[]{:S(2)}) collective-permute-start(bf16[256,1024]{1,0:T(8,128)(2,1)} %get-tuple-element.97), channel_id=1, source_target_pairs={{0,16},{4,20},{8,24},{12,28},{16,0},{20,4},{24,8},{28,12},{1,17},{... | collective-permute-start | bytes 1572872 | tf_op jit(solution)/shard_map/ppermute | solution.py:481
  308.3 21.7 %collective-permute-start.48 = (bf16[256,1024]{1,0:T(8,128)(2,1)S(1)}, bf16[256,1024]{1,0:T(8,128)(2,1)S(1)}, u32[]{:S(2)}, u32[]{:S(2)}) collective-permute-start(bf16[256,1024]{1,0:T(8,128)(2,1)S(1)} %fusion.67), channel_id=1, source_target_pairs={{0,16},{4,20},{8,24},{12,28},{16,0},{20,4},{24,8},{28,12},{1,17},{... | collective-permute-start | bytes 1572872 | tf_op jit(solution)/shard_map/ppermute | solution.py:481
  313.9 22.3 %collective-permute-start.8 = (bf16[544,1024]{1,0:T(8,128)(2,1)}, bf16[544,1024]{1,0:T(8,128)(2,1)S(1)}, u32[]{:S(2)}, u32[]{:S(2)}) collective-permute-start(bf16[544,1024]{1,0:T(8,128)(2,1)} %dynamic-slice_convert_fusion.1), channel_id=1, source_target_pairs={{0,4},{4,0},{8,12},{12,8},{16,20},{20,16},{24,28},{28,24},{1,5},{5... | collective-permute-start | bytes 3342344 | tf_op jit(solution)/shard_map/ppermute | solution.py:478
  321.1 13.4 %collective-permute-start.45 = (bf16[256,1024]{1,0:T(8,128)(2,1)S(1)}, bf16[256,1024]{1,0:T(8,128)(2,1)S(1)}, u32[]{:S(2)}, u32[]{:S(2)}) collective-permute-start(bf16[256,1024]{1,0:T(8,128)(2,1)S(1)} %fusion.69), channel_id=1, source_target_pairs={{0,8},{4,12},{8,0},{12,4},{16,24},{20,28},{24,16},{28,20},{1,9},{5... | collective-permute-start | bytes 1572872 | tf_op jit(solution)/shard_map/ppermute | solution.py:481
  324.2 29.7 %collective-permute-start.36 = (bf16[256,1024]{1,0:T(8,128)(2,1)S(1)}, bf16[256,1024]{1,0:T(8,128)(2,1)S(1)}, u32[]{:S(2)}, u32[]{:S(2)}) collective-permute-start(bf16[256,1024]{1,0:T(8,128)(2,1)S(1)} %copy-done.39), channel_id=1, source_target_pairs={{0,8},{4,12},{8,0},{12,4},{16,24},{20,28},{24,16},{28,20},{1,9},{5... | collective-permute-start | bytes 1572872 | tf_op jit(solution)/shard_map/ppermute | solution.py:481
  329.9 29.8 %collective-permute-start.33 = (bf16[256,1024]{1,0:T(8,128)(2,1)S(1)}, bf16[256,1024]{1,0:T(8,128)(2,1)S(1)}, u32[]{:S(2)}, u32[]{:S(2)}) collective-permute-start(bf16[256,1024]{1,0:T(8,128)(2,1)S(1)} %copy-done.38), channel_id=1, source_target_pairs={{0,16},{4,20},{8,24},{12,28},{16,0},{20,4},{24,8},{28,12},{1,17},{... | collective-permute-start | bytes 1572872 | tf_op jit(solution)/shard_map/ppermute | solution.py:481
  332.2 21.7 %collective-permute-start.38 = (bf16[256,1024]{1,0:T(8,128)(2,1)S(1)}, bf16[256,1024]{1,0:T(8,128)(2,1)S(1)}, u32[]{:S(2)}, u32[]{:S(2)}) collective-permute-start(bf16[256,1024]{1,0:T(8,128)(2,1)S(1)} %fusion.71), channel_id=1, source_target_pairs={{0,16},{4,20},{8,24},{12,28},{16,0},{20,4},{24,8},{28,12},{1,17},{... | collective-permute-start | bytes 1572872 | tf_op jit(solution)/shard_map/ppermute | solution.py:481
  334.5 28.3 %collective-permute-start.35 = (bf16[256,1024]{1,0:T(8,128)(2,1)S(1)}, bf16[256,1024]{1,0:T(8,128)(2,1)S(1)}, u32[]{:S(2)}, u32[]{:S(2)}) collective-permute-start(bf16[256,1024]{1,0:T(8,128)(2,1)S(1)} %fusion.73), channel_id=1, source_target_pairs={{0,8},{4,12},{8,0},{12,4},{16,24},{20,28},{24,16},{28,20},{1,9},{5... | collective-permute-start | bytes 1572872 | tf_op jit(solution)/shard_map/ppermute | solution.py:481
  336.2 29.2 %collective-permute-start.49 = (bf16[128,1024]{1,0:T(8,128)(2,1)S(1)}, bf16[128,1024]{1,0:T(8,128)(2,1)S(1)}, u32[]{:S(2)}, u32[]{:S(2)}) collective-permute-start(bf16[128,1024]{1,0:T(8,128)(2,1)S(1)} %get-tuple-element.115), channel_id=1, source_target_pairs={{0,0},{2,1},{4,2},{6,3},{1,4},{3,5},{5,6},{7,7},{8,8},{10,9},{12,1... | collective-permute-start | bytes 786440 | tf_op jit(solution)/shard_map/ppermute | solution.py:575
  353.8 16.2 %collective-permute-start.50 = (bf16[128,1024]{1,0:T(8,128)(2,1)S(1)}, bf16[128,1024]{1,0:T(8,128)(2,1)S(1)}, u32[]{:S(2)}, u32[]{:S(2)}) collective-permute-start(bf16[128,1024]{1,0:T(8,128)(2,1)S(1)} %get-tuple-element.116), channel_id=1, source_target_pairs={{1,0},{3,1},{5,2},{7,3},{0,4},{2,5},{4,6},{6,7},{9,8},{11,9},{13,1... | collective-permute-start | bytes 786440 | tf_op jit(solution)/shard_map/ppermute | solution.py:575
  353.9 44.6 %collective-permute-start.9 = (bf16[544,1024]{1,0:T(8,128)(2,1)S(1)}, bf16[544,1024]{1,0:T(8,128)(2,1)S(1)}, u32[]{:S(2)}, u32[]{:S(2)}) collective-permute-start(bf16[544,1024]{1,0:T(8,128)(2,1)S(1)} %get-tuple-element.74), channel_id=1, source_target_pairs={{0,4},{4,0},{8,12},{12,8},{16,20},{20,16},{24,28},{28,24},{1,5},{5... | collective-permute-start | bytes 3342344 | tf_op jit(solution)/shard_map/ppermute | solution.py:478
  359.7 10.7 %collective-permute-start.51 = (bf16[128,1024]{1,0:T(8,128)(2,1)S(1)}, bf16[128,1024]{1,0:T(8,128)(2,1)S(1)}, u32[]{:S(2)}, u32[]{:S(2)}) collective-permute-start(bf16[128,1024]{1,0:T(8,128)(2,1)S(1)} %get-tuple-element.117), channel_id=1, source_target_pairs={{2,0},{0,1},{6,2},{4,3},{3,4},{1,5},{7,6},{5,7},{10,8},{8,9},{14,1... | collective-permute-start | bytes 786440 | tf_op jit(solution)/shard_map/ppermute | solution.py:575
  362.8 11.8 %collective-permute-start.52 = (bf16[128,1024]{1,0:T(8,128)(2,1)S(1)}, bf16[128,1024]{1,0:T(8,128)(2,1)S(1)}, u32[]{:S(2)}, u32[]{:S(2)}) collective-permute-start(bf16[128,1024]{1,0:T(8,128)(2,1)S(1)} %get-tuple-element.118), channel_id=1, source_target_pairs={{3,0},{1,1},{7,2},{5,3},{2,4},{0,5},{6,6},{4,7},{11,8},{9,9},{15,1... | collective-permute-start | bytes 786440 | tf_op jit(solution)/shard_map/ppermute | solution.py:575
  365.4 15.8 %collective-permute-start.39 = (bf16[128,1024]{1,0:T(8,128)(2,1)S(1)}, bf16[128,1024]{1,0:T(8,128)(2,1)S(1)}, u32[]{:S(2)}, u32[]{:S(2)}) collective-permute-start(bf16[128,1024]{1,0:T(8,128)(2,1)S(1)} %get-tuple-element.119), channel_id=1, source_target_pairs={{0,0},{2,1},{4,2},{6,3},{1,4},{3,5},{5,6},{7,7},{8,8},{10,9},{12,1... | collective-permute-start | bytes 786440 | tf_op jit(solution)/shard_map/ppermute | solution.py:575
  370.0 15.3 %collective-permute-start.40 = (bf16[128,1024]{1,0:T(8,128)(2,1)S(1)}, bf16[128,1024]{1,0:T(8,128)(2,1)S(1)}, u32[]{:S(2)}, u32[]{:S(2)}) collective-permute-start(bf16[128,1024]{1,0:T(8,128)(2,1)S(1)} %get-tuple-element.120), channel_id=1, source_target_pairs={{1,0},{3,1},{5,2},{7,3},{0,4},{2,5},{4,6},{6,7},{9,8},{11,9},{13,1... | collective-permute-start | bytes 786440 | tf_op jit(solution)/shard_map/ppermute | solution.py:575
  370.5 18.2 %collective-permute-start.41 = (bf16[128,1024]{1,0:T(8,128)(2,1)S(1)}, bf16[128,1024]{1,0:T(8,128)(2,1)S(1)}, u32[]{:S(2)}, u32[]{:S(2)}) collective-permute-start(bf16[128,1024]{1,0:T(8,128)(2,1)S(1)} %get-tuple-element.121), channel_id=1, source_target_pairs={{2,0},{0,1},{6,2},{4,3},{3,4},{1,5},{7,6},{5,7},{10,8},{8,9},{14,1... | collective-permute-start | bytes 786440 | tf_op jit(solution)/shard_map/ppermute | solution.py:575
  374.6 23.0 %collective-permute-start.42 = (bf16[128,1024]{1,0:T(8,128)(2,1)S(1)}, bf16[128,1024]{1,0:T(8,128)(2,1)S(1)}, u32[]{:S(2)}, u32[]{:S(2)}) collective-permute-start(bf16[128,1024]{1,0:T(8,128)(2,1)S(1)} %get-tuple-element.122), channel_id=1, source_target_pairs={{3,0},{1,1},{7,2},{5,3},{2,4},{0,5},{6,6},{4,7},{11,8},{9,9},{15,1... | collective-permute-start | bytes 786440 | tf_op jit(solution)/shard_map/ppermute | solution.py:575
  442.7 6.6 collective-permute-start.27
  443.8 7.1 %collective-permute-start.26 = (bf16[64,1024]{1,0:T(8,128)(2,1)S(1)}, bf16[64,1024]{1,0:T(8,128)(2,1)S(1)}, u32[]{:S(2)}, u32[]{:S(2)}) collective-permute-start(bf16[64,1024]{1,0:T(8,128)(2,1)S(1)} %get-tuple-element.127), channel_id=1, source_target_pairs={{0,8},{4,12},{8,0},{12,4},{16,24},{20,28},{24,16},{28,20},{1,9},{5... | collective-permute-start | bytes 393224 | tf_op jit(solution)/shard_map/ppermute | solution.py:481
  444.2 6.2 collective-permute-start.24
  445.4 9.8 %collective-permute-start.23 = (bf16[64,1024]{1,0:T(8,128)(2,1)S(1)}, bf16[64,1024]{1,0:T(8,128)(2,1)S(1)}, u32[]{:S(2)}, u32[]{:S(2)}) collective-permute-start(bf16[64,1024]{1,0:T(8,128)(2,1)S(1)} %get-tuple-element.129), channel_id=1, source_target_pairs={{0,16},{4,20},{8,24},{12,28},{16,0},{20,4},{24,8},{28,12},{1,17},{... | collective-permute-start | bytes 393224 | tf_op jit(solution)/shard_map/ppermute | solution.py:481
  449.0 63.6 %collective-permute-start.10 = (bf16[544,1024]{1,0:T(8,128)(2,1)}, bf16[544,1024]{1,0:T(8,128)(2,1)}, u32[]{:S(2)}, u32[]{:S(2)}) collective-permute-start(bf16[544,1024]{1,0:T(8,128)(2,1)} %dynamic-slice_convert_fusion), channel_id=1, source_target_pairs={{0,4},{4,0},{8,12},{12,8},{16,20},{20,16},{24,28},{28,24},{1,5},{5... | collective-permute-start | bytes 3342344 | tf_op jit(solution)/shard_map/ppermute | solution.py:478
  449.2 25.9 %collective-permute-start.17 = (bf16[256,768]{1,0:T(8,128)(2,1)S(1)}, bf16[256,768]{1,0:T(8,128)(2,1)S(1)}, u32[]{:S(2)}, u32[]{:S(2)}) collective-permute-start(bf16[256,768]{1,0:T(8,128)(2,1)S(1)} %get-tuple-element.104), channel_id=1, source_target_pairs={{0,8},{4,12},{8,0},{12,4},{16,24},{20,28},{24,16},{28,20},{1,9},{5... | collective-permute-start | bytes 1179656 | tf_op jit(solution)/shard_map/ppermute | solution.py:481
  451.0 38.8 %collective-permute-start.16 = (bf16[256,768]{1,0:T(8,128)(2,1)S(1)}, bf16[256,768]{1,0:T(8,128)(2,1)S(1)}, u32[]{:S(2)}, u32[]{:S(2)}) collective-permute-start(bf16[256,768]{1,0:T(8,128)(2,1)S(1)} %get-tuple-element.103), channel_id=1, source_target_pairs={{0,8},{4,12},{8,0},{12,4},{16,24},{20,28},{24,16},{28,20},{1,9},{5... | collective-permute-start | bytes 1179656 | tf_op jit(solution)/shard_map/ppermute | solution.py:481
  454.7 16.0 %collective-permute-start.25 = (bf16[64,1024]{1,0:T(8,128)(2,1)S(1)}, bf16[64,1024]{1,0:T(8,128)(2,1)S(1)}, u32[]{:S(2)}, u32[]{:S(2)}) collective-permute-start(bf16[64,1024]{1,0:T(8,128)(2,1)S(1)} %fusion.106), channel_id=1, source_target_pairs={{0,8},{4,12},{8,0},{12,4},{16,24},{20,28},{24,16},{28,20},{1,9},{5... | collective-permute-start | bytes 393224 | tf_op jit(solution)/shard_map/ppermute | solution.py:481
  455.2 28.3 %collective-permute-start.14 = (bf16[256,768]{1,0:T(8,128)(2,1)S(1)}, bf16[256,768]{1,0:T(8,128)(2,1)S(1)}, u32[]{:S(2)}, u32[]{:S(2)}) collective-permute-start(bf16[256,768]{1,0:T(8,128)(2,1)S(1)} %get-tuple-element.106), channel_id=1, source_target_pairs={{0,16},{4,20},{8,24},{12,28},{16,0},{20,4},{24,8},{28,12},{1,17},{... | collective-permute-start | bytes 1179656 | tf_op jit(solution)/shard_map/ppermute | solution.py:481
  470.9 7.4 %collective-permute-start.29 = (bf16[32,1024]{1,0:T(8,128)(2,1)S(1)}, bf16[32,1024]{1,0:T(8,128)(2,1)S(1)}, u32[]{:S(2)}, u32[]{:S(2)}) collective-permute-start(bf16[32,1024]{1,0:T(8,128)(2,1)S(1)} %get-tuple-element.131), channel_id=1, source_target_pairs={{0,0},{2,1},{4,2},{6,3},{1,4},{3,5},{5,6},{7,7},{8,8},{10,9},{12,1... | collective-permute-start | bytes 196616 | tf_op jit(solution)/shard_map/ppermute | solution.py:575
  475.1 6.3 collective-permute-start.30
  478.3 6.6 %collective-permute-start.31 = (bf16[32,1024]{1,0:T(8,128)(2,1)S(1)}, bf16[32,1024]{1,0:T(8,128)(2,1)S(1)}, u32[]{:S(2)}, u32[]{:S(2)}) collective-permute-start(bf16[32,1024]{1,0:T(8,128)(2,1)S(1)} %get-tuple-element.133), channel_id=1, source_target_pairs={{2,0},{0,1},{6,2},{4,3},{3,4},{1,5},{7,6},{5,7},{10,8},{8,9},{14,1... | collective-permute-start | bytes 196616 | tf_op jit(solution)/shard_map/ppermute | solution.py:575
  481.5 6.5 collective-permute-start.32
  483.5 11.2 %collective-permute-start.18 = (bf16[256,768]{1,0:T(8,128)(2,1)S(1)}, bf16[256,768]{1,0:T(8,128)(2,1)S(1)}, u32[]{:S(2)}, u32[]{:S(2)}) collective-permute-start(bf16[256,768]{1,0:T(8,128)(2,1)S(1)} %fusion.75), channel_id=1, source_target_pairs={{0,16},{4,20},{8,24},{12,28},{16,0},{20,4},{24,8},{28,12},{1,17},{... | collective-permute-start | bytes 1179656 | tf_op jit(solution)/shard_map/ppermute | solution.py:481
  484.9 17.2 %collective-permute-start.13 = (bf16[256,768]{1,0:T(8,128)(2,1)S(1)}, bf16[256,768]{1,0:T(8,128)(2,1)S(1)}, u32[]{:S(2)}, u32[]{:S(2)}) collective-permute-start(bf16[256,768]{1,0:T(8,128)(2,1)S(1)} %get-tuple-element.105), channel_id=1, source_target_pairs={{0,16},{4,20},{8,24},{12,28},{16,0},{20,4},{24,8},{28,12},{1,17},{... | collective-permute-start | bytes 1179656 | tf_op jit(solution)/shard_map/ppermute | solution.py:481
  487.9 14.2 %collective-permute-start.15 = (bf16[256,768]{1,0:T(8,128)(2,1)S(1)}, bf16[256,768]{1,0:T(8,128)(2,1)S(1)}, u32[]{:S(2)}, u32[]{:S(2)}) collective-permute-start(bf16[256,768]{1,0:T(8,128)(2,1)S(1)} %fusion.77), channel_id=1, source_target_pairs={{0,8},{4,12},{8,0},{12,4},{16,24},{20,28},{24,16},{28,20},{1,9},{5... | collective-permute-start | bytes 1179656 | tf_op jit(solution)/shard_map/ppermute | solution.py:481
  504.5 24.1 %collective-permute-start.19 = (bf16[128,768]{0,1:T(8,128)(2,1)}, bf16[128,768]{0,1:T(8,128)(2,1)}, u32[]{:S(2)}, u32[]{:S(2)}) collective-permute-start(bf16[128,768]{0,1:T(8,128)(2,1)} %get-tuple-element.123), channel_id=1, source_target_pairs={{0,0},{2,1},{4,2},{6,3},{1,4},{3,5},{5,6},{7,7},{8,8},{10,9},{12,1... | collective-permute-start | bytes 589832 | tf_op jit(solution)/shard_map/ppermute | solution.py:575
  507.4 22.3 %collective-permute-start.20 = (bf16[128,768]{0,1:T(8,128)(2,1)}, bf16[128,768]{0,1:T(8,128)(2,1)}, u32[]{:S(2)}, u32[]{:S(2)}) collective-permute-start(bf16[128,768]{0,1:T(8,128)(2,1)} %get-tuple-element.124), channel_id=1, source_target_pairs={{1,0},{3,1},{5,2},{7,3},{0,4},{2,5},{4,6},{6,7},{9,8},{11,9},{13,1... | collective-permute-start | bytes 589832 | tf_op jit(solution)/shard_map/ppermute | solution.py:575
  508.1 21.6 %collective-permute-start.21 = (bf16[128,768]{0,1:T(8,128)(2,1)}, bf16[128,768]{0,1:T(8,128)(2,1)}, u32[]{:S(2)}, u32[]{:S(2)}) collective-permute-start(bf16[128,768]{0,1:T(8,128)(2,1)} %get-tuple-element.125), channel_id=1, source_target_pairs={{2,0},{0,1},{6,2},{4,3},{3,4},{1,5},{7,6},{5,7},{10,8},{8,9},{14,1... | collective-permute-start | bytes 589832 | tf_op jit(solution)/shard_map/ppermute | solution.py:575
  510.6 19.1 %collective-permute-start.22 = (bf16[128,768]{0,1:T(8,128)(2,1)S(1)}, bf16[128,768]{0,1:T(8,128)(2,1)}, u32[]{:S(2)}, u32[]{:S(2)}) collective-permute-start(bf16[128,768]{0,1:T(8,128)(2,1)S(1)} %get-tuple-element.126), channel_id=1, source_target_pairs={{3,0},{1,1},{7,2},{5,3},{2,4},{0,5},{6,6},{4,7},{11,8},{9,9},{15,1... | collective-permute-start | bytes 589832 | tf_op jit(solution)/shard_map/ppermute | solution.py:575
  524.1 126.3 %collective-permute-start.11 = (bf16[272,1024]{1,0:T(8,128)(2,1)S(1)}, bf16[272,1024]{1,0:T(8,128)(2,1)S(1)}, u32[]{:S(2)}, u32[]{:S(2)}) collective-permute-start(bf16[272,1024]{1,0:T(8,128)(2,1)S(1)} %get-tuple-element.109), channel_id=1, source_target_pairs={{0,0},{2,1},{4,2},{6,3},{1,4},{3,5},{5,6},{7,7},{8,8},{10,9},{12,1... | collective-permute-start | bytes 1671176 | tf_op jit(solution)/shard_map/ppermute | solution.py:529
  528.6 121.8 %collective-permute-start.12 = (bf16[272,1024]{1,0:T(8,128)(2,1)S(1)}, bf16[272,1024]{1,0:T(8,128)(2,1)S(1)}, u32[]{:S(2)}, u32[]{:S(2)}) collective-permute-start(bf16[272,1024]{1,0:T(8,128)(2,1)S(1)} %get-tuple-element.110), channel_id=1, source_target_pairs={{2,0},{0,1},{6,2},{4,3},{3,4},{1,5},{7,6},{5,7},{10,8},{8,9},{14,1... | collective-permute-start | bytes 1671176 | tf_op jit(solution)/shard_map/ppermute | solution.py:529
  (71 other events, 600.5 us)
Sparse Core Ops, SparseCore 0:
  520.3 124.6 all-reduce.3

commit v3 on v2

--- a/solution.py
+++ b/solution.py
@@ -59,52 +59,20 @@
     return list(zip(cuts[:-1], cuts[1:]))
 
 
-def masks(start, stop, length, seg_c, seg_r):
+def masks(start, stop, length, count):
     rows = stop - start
+    query = lax.broadcasted_iota(jnp.int32, (rows, 1), 0)
+    own = query >= lax.broadcasted_iota(jnp.int32, (1, rows), 1)
     if stop < length:
-        causal = lax.broadcasted_iota(jnp.int32, (rows, rows), 0) >= lax.broadcasted_iota(
-            jnp.int32, (rows, rows), 1
-        )
-        return causal, None
-    own = lax.broadcasted_iota(jnp.int32, (rows, rows), 0) >= lax.broadcasted_iota(
-        jnp.int32, (rows, rows), 1
-    )
-    same = seg_c[:, 0:1] == seg_r[0:1, start:stop]
-    before = seg_c[:, 0:1] == seg_r[0:1, 0:start]
-    return own & same, before
-
-
-def attend_fwd_kernel(q_ref, k_ref, v_ref, segc_ref, segr_ref, o_ref, lse_ref):
-    length = q_ref.shape[0]
-    lane = lax.broadcasted_iota(jnp.int32, (1, 128), 1)
-    for start, stop in row_blocks(length):
-        own, before = masks(start, stop, length, segc_ref[...], segr_ref[...])
-        outs = []
-        lses = []
-        for head in range(2):
-            q = jnp.where((lane >= 64) == (head == 1), q_ref[start:stop, :], jnp.zeros((), BF))
-            s2 = jnp.where(own, dot_nt(q, k_ref[start:stop, :]), NEG)
-            top = jnp.max(s2, axis=-1, keepdims=True)
-            if start:
-                s1 = dot_nt(q, k_ref[0:start, :])
-                if before is not None:
-                    s1 = jnp.where(before, s1, NEG)
-                top = jnp.maximum(top, jnp.max(s1, axis=-1, keepdims=True))
-            e2 = jnp.exp(ALPHA * (s2 - top))
-            total = jnp.sum(e2, axis=-1, keepdims=True)
-            acc = dot_nn(e2.astype(BF), v_ref[start:stop, :])
-            if start:
-                e1 = jnp.exp(ALPHA * (s1 - top))
-                total = total + jnp.sum(e1, axis=-1, keepdims=True)
-                acc = acc + dot_nn(e1.astype(BF), v_ref[0:start, :])
-            outs.append(acc / total)
-            lses.append(ALPHA * top + jnp.log(total))
-        o_ref[start:stop, :] = jnp.where(lane < 64, outs[0], outs[1]).astype(BF)
-        lse_ref[start:stop, :] = jnp.where(lane < 64, lses[0], lses[1])
+        return own, None
+    real = query + start < count
+    same = real == (lax.broadcasted_iota(jnp.int32, (1, rows), 1) + start < count)
+    before = real == (lax.broadcasted_iota(jnp.int32, (1, start), 1) < count)
+    return jnp.logical_and(own, same), before
 
 
 def attend_bwd_kernel(
-    q_ref, k_ref, v_ref, do_ref, lse_ref, segc_ref, segr_ref, d_ref, dk_ref, dv_ref
+    q_ref, k_ref, v_ref, do_ref, lse_ref, count_ref, d_ref, dk_ref, dv_ref
 ):
     length = q_ref.shape[0]
     pair = pl.program_id(0)
@@ -114,7 +82,7 @@
     dv_ref[...] = jnp.zeros_like(dv_ref)
     zero = jnp.zeros((), BF)
     for start, stop in row_blocks(length):
-        own, before = masks(start, stop, length, segc_ref[...], segr_ref[...])
+        own, before = masks(start, stop, length, count_ref[0:1, 0:1])
         dqs = []
         for head in range(2):
             mine = (lane >= 64) == (head == 1)
@@ -146,30 +114,7 @@
     d_ref[:, pl.ds(pl.multiple_of((2 * pairs + pair) * 128, 128), 128)] = dv_ref[...].astype(BF)
 
 
-def attend_forward(qkv, seg_c, seg_r):
-    length, width = qkv.shape
-    pairs = width // 384
-    col = lambda base: pl.BlockSpec((length, 128), lambda j, base=base: (0, base + j))
-    whole = lambda a: pl.BlockSpec(a.shape, lambda j: (0, 0))
-    return pl.pallas_call(
-        attend_fwd_kernel,
-        grid=(pairs,),
-        in_specs=[col(0), col(pairs), col(2 * pairs), whole(seg_c), whole(seg_r)],
-        out_specs=[col(0), col(0)],
-        out_shape=[
-            jax.ShapeDtypeStruct((length, 128 * pairs), BF),
-            jax.ShapeDtypeStruct((length, 128 * pairs), F32),
-        ],
-        compiler_params=pltpu.CompilerParams(vmem_limit_bytes=40 << 20),
-        cost_estimate=pl.CostEstimate(
-            flops=8 * pairs * length * length * 128,
-            bytes_accessed=10 * length * 128 * pairs,
-            transcendentals=pairs * length * length,
-        ),
-    )(qkv, qkv, qkv, seg_c, seg_r)
-
-
-def attend_backward(qkv, grad_o, lse, seg_c, seg_r):
+def attend_backward(qkv, grad_o, lse, count):
     length, width = qkv.shape
     pairs = width // 384
     col = lambda base: pl.BlockSpec((length, 128), lambda j, base=base: (0, base + j))
@@ -183,8 +128,7 @@
             col(2 * pairs),
             col(0),
             col(0),
-            whole(seg_c),
-            whole(seg_r),
+            whole(count),
         ],
         out_specs=pl.BlockSpec((length, width), lambda j: (0, 0)),
         out_shape=jax.ShapeDtypeStruct((length, width), BF),
@@ -195,7 +139,7 @@
             bytes_accessed=18 * length * 128 * pairs,
             transcendentals=pairs * length * length,
         ),
-    )(qkv, qkv, qkv, grad_o, lse, seg_c, seg_r)
+    )(qkv, qkv, qkv, grad_o, lse, count)
 
 
 MESH = pl.DeviceIdType.MESH
@@ -282,6 +226,23 @@
         self.used += 1
         self.open.append((own, copy))
 
+    def send_if(self, condition, src, dst, recv_sem, dp, z):
+        copy = pltpu.make_async_remote_copy(
+            src_ref=src,
+            dst_ref=dst,
+            send_sem=self.send_sems.at[self.used],
+            recv_sem=recv_sem,
+            device_id=(dp, z),
+            device_id_type=MESH,
+        )
+
+        @pl.when(condition)
+        def _():
+            copy.start()
+
+        self.used += 1
+        self.open.append((jnp.logical_not(condition), copy))
+
     def arrived(self, src, dst, recv_sem):
         pltpu.make_async_remote_copy(
             src_ref=src,
@@ -309,70 +270,6 @@
     return pl.ds(pl.multiple_of(index * rows, rows), rows)
 
 
-class Gather:
-    def __init__(self, links, src, dst, col_sems, hop_sems):
-        self.links, self.src, self.dst = links, src, dst
-        self.rows = src.shape[0]
-        self.col_sems, self.hop_sems = col_sems, hop_sems
-        self.groups = links.n_dp // 2
-
-    def column(self):
-        k = self.links
-        i = lax.rem(k.z, 2)
-        for zz in range(k.n_mp):
-            k.send_or_keep(
-                self.src,
-                self.dst.at[i, rows_at(k.dp, self.rows), :],
-                self.col_sems.at[i, k.core],
-                2 * k.group + k.z // 2,
-                zz,
-            )
-
-    def piece(self, i, group):
-        return self.dst.at[i, rows_at(group, 2 * self.rows), :]
-
-    def column_wait(self, i):
-        for c in range(2):
-            self.links.arrived(
-                self.src,
-                self.dst.at[i, rows_at(2 * self.links.group + c, self.rows), :],
-                self.col_sems.at[i, c],
-            )
-
-    def hop(self, i, rel, bit):
-        k = self.links
-        piece = self.piece(i, k.group ^ rel)
-        k.send(piece, piece, self.hop_sems.at[i, rel ^ bit], k.dp ^ (2 * bit), k.z)
-
-    def hop_wait(self, i, rel):
-        piece = self.piece(i, self.links.group ^ rel)
-        self.links.arrived(piece, piece, self.hop_sems.at[i, rel])
-
-    def first(self):
-        for i in range(2):
-            self.column_wait(i)
-            for bit, _ in plan_hops(self.groups, i):
-                self.hop(i, 0, bit)
-
-    def second(self):
-        steps = [plan_hops(self.groups, i) for i in range(2)]
-        self.waited = [set(), set()]
-        for level in range(1, len(steps[0])):
-            for i in range(2):
-                bit, known = steps[i][level]
-                for rel in known[1:]:
-                    if rel not in self.waited[i]:
-                        self.hop_wait(i, rel)
-                        self.waited[i].add(rel)
-                    self.hop(i, rel, bit)
-
-    def last(self):
-        for i in range(2):
-            for rel in range(1, self.groups):
-                if rel not in self.waited[i]:
-                    self.hop_wait(i, rel)
-
-
 def exchange_tokens(links, src, dst, sems):
     quarter = src.shape[1]
     for m in range(2):
@@ -391,56 +288,397 @@
         links.arrived(src.at[0], dst.at[pl.ds(s * quarter, quarter), :], sems.at[s])
 
 
-def gather_kernel(n_dp, n_mp, *refs):
-    tokens, grads = refs[0:2]
-    blocks = refs[2:7]
-    x_out, g_out = refs[7:9]
-    fulls = refs[9:14]
-    send_sems, col_sems, hop_sems, tok_sems = refs[14:18]
+class Column:
+    def __init__(self, links, src, dst, col_sems, hop_sems):
+        self.links, self.src, self.dst = links, src, dst
+        self.rows = src.shape[0]
+        self.col_sems, self.hop_sems = col_sems, hop_sems
+        self.groups = links.n_dp // 2
+        self.waited = [set(), set()]
+
+    def start(self):
+        k = self.links
+        i = lax.rem(k.z, 2)
+        home = k.z // 2
+        step = 1 - 2 * home
+        dst = self.dst.at[i, rows_at(k.dp, self.rows), :]
+        sem = self.col_sems.at[i, k.core]
+        owner = 2 * k.group + home
+        k.send(self.src, dst, sem, owner, k.z + step)
+        k.send_if(jnp.logical_or(k.z == 1, k.z == 2), self.src, dst, sem, owner, k.z - step)
+        k.send_or_keep(self.src, dst, sem, owner, k.z)
+
+    def piece(self, i, group):
+        return self.dst.at[i, rows_at(group, 2 * self.rows), :]
+
+    def hop(self, i, rel, bit):
+        k = self.links
+        piece = self.piece(i, k.group ^ rel)
+        k.send(piece, piece, self.hop_sems.at[i, rel ^ bit], k.dp ^ (2 * bit), k.z)
+
+    def hop_wait(self, i, rel):
+        if rel not in self.waited[i]:
+            piece = self.piece(i, self.links.group ^ rel)
+            self.links.arrived(piece, piece, self.hop_sems.at[i, rel])
+            self.waited[i].add(rel)
+
+    def first(self):
+        k = self.links
+        for i in range(2):
+            for c in range(2):
+                block = self.dst.at[i, rows_at(2 * k.group + c, self.rows), :]
+                k.arrived(self.src, block, self.col_sems.at[i, c])
+            up = jnp.logical_and(k.core == 0, jnp.logical_and(k.z > i, k.z < k.n_mp - 1))
+            down = jnp.logical_and(k.core == 1, jnp.logical_and(k.z < 2 + i, k.z > 0))
+            onward = jnp.logical_or(up, down)
+            for c in range(2):
+                block = self.dst.at[i, rows_at(2 * k.group + c, self.rows), :]
+                k.send_if(
+                    onward, block, block, self.col_sems.at[i, c], k.dp, k.z + 1 - 2 * k.core
+                )
+            for bit, _ in plan_hops(self.groups, i):
+                self.hop(i, 0, bit)
+
+    def second(self):
+        steps = [plan_hops(self.groups, i) for i in range(2)]
+        for level in range(1, len(steps[0])):
+            for i in range(2):
+                bit, known = steps[i][level]
+                for rel in known[1:]:
+                    self.hop_wait(i, rel)
+                    self.hop(i, rel, bit)
+
+    def last(self):
+        for i in range(2):
+            for rel in range(1, self.groups):
+                self.hop_wait(i, rel)
+
+
+def sends_of_column(n_mp, hops):
+    return 3 + 4 + 2 * hops
+
+
+def forward_kernel(n_dp, n_mp, *refs):
+    (tokens, grads, seg_ref) = refs[0:3]
+    blocks = refs[3:8]
+    (x_out, g_out, h1_out, qkv_out, o_out, lse_out, a_out, mid_out, h2_out) = refs[8:17]
+    (act_out, slope_out, f_out, y_out) = refs[17:21]
+    w_outs = refs[21:25]
+    count_out, vec_ref = refs[25:27]
+    weights = refs[27:32]
+    (xb, seg_other, h1, qkv, o, lse, a_send, a_recv, a_own, mid) = refs[32:42]
+    (h2, act, slope, f_send, f_recv, f_own, y, bias_ref, upb_ref) = refs[42:51]
+    (send_sems, col_sems, hop_sems, tok_sems, swap_sems, keep_sems) = refs[51:57]
+    smalls, w_qkv, w_out, w_up, w_down = weights
     links = Links(n_dp, n_mp, send_sems)
+    half = xb.shape[0]
+    length = 2 * half
+    tile = half // 2
+    other = links.dp + 1 - 2 * links.core
+    mine0 = links.core * half
+    other0 = (1 - links.core) * half
+    kept = []
+
+    def keep(src, dst):
+        copy = pltpu.make_async_copy(src, dst, keep_sems.at[len(kept)])
+        copy.start()
+        kept.append(copy)
+
+    def at(start, rows):
+        return pl.ds(pl.multiple_of(start, 16), rows)
+
     links.barrier()
-    ways = [
-        Gather(links, blocks[a], fulls[a], col_sems.at[a], hop_sems.at[a]) for a in range(5)
+    ways = [Column(links, blocks[a], weights[a], col_sems.at[a], hop_sems.at[a]) for a in range(5)]
+    v_way, q_way, o_way, u_way, d_way = ways
+    v_way.start()
+    q_way.start()
+    o_way.start()
+    links.send(seg_ref, seg_other, swap_sems.at[0], other, links.z)
+    v_way.first()
+    u_way.start()
+    q_way.first()
+    exchange_tokens(links, tokens, xb, tok_sems.at[0])
+    v_way.second()
+    o_way.first()
+    q_way.second()
+    d_way.start()
+    u_way.first()
+    o_way.second()
+    links.arrived(seg_ref, seg_other, swap_sems.at[0])
+    pick = lax.rem(links.core + links.z, 2) == 0
+    seg_row = jnp.where(
+        pick, seg_ref[pl.ds(links.z // 2, 1), :], seg_other[pl.ds(links.z // 2, 1), :]
+    )
+    count = jnp.sum((seg_row == 0).astype(jnp.int32), axis=1, keepdims=True)
+    count_out[...] = jnp.broadcast_to(count, count_out.shape)
+    v_way.last()
+    spread_smalls(n_dp, smalls, vec_ref, bias_ref, upb_ref)
+    exchange_tokens_wait(links, tokens, xb, tok_sems.at[0])
+    keep(xb, x_out)
+
+    def first_norm(t, _):
+        rows = at(t * tile, tile)
+        unit, _ = stats(xb[rows, :].astype(F32))
+        h1[at(mine0 + t * tile, tile), :] = (unit * vec_ref[0:1, :] + vec_ref[4:5, :]).astype(BF)
+        return 0
+
+    lax.fori_loop(0, 2, first_norm, 0)
+    links.send(h1.at[at(mine0, half), :], h1.at[at(mine0, half), :], swap_sems.at[1], other, links.z)
+    q_way.last()
+    cols = qkv.shape[2] // 3
+    scale_row = jnp.where(
+        lax.broadcasted_iota(jnp.int32, (1, 3 * cols), 1) < cols, SCALE, 1.0
+    ).astype(F32)
+
+    def project(start):
+        def body(t, _):
+            rows = at(start + t * tile, tile)
+            for i in range(2):
+                value = dot_nn(h1[rows, :], w_qkv[i]) + bias_ref[i : i + 1, :]
+                qkv[i, rows, :] = (value * scale_row).astype(BF)
+            return 0
+
+        lax.fori_loop(0, 2, body, 0)
+
+    project(mine0)
+    links.arrived(
+        h1.at[at(mine0, half), :], h1.at[at(other0, half), :], swap_sems.at[1]
+    )
+    project(other0)
+    keep(h1, h1_out)
+    keep(qkv, qkv_out)
+    u_way.second()
+    d_way.first()
+    exchange_tokens(links, grads, g_out, tok_sems.at[1])
+    pairs = cols // 128
+
+    def attend(i):
+        def body(j, _):
+            attend_pair_fwd(
+                qkv.at[i, :, pl.ds(pl.multiple_of(j * 128, 128), 128)],
+                qkv.at[i, :, pl.ds(pl.multiple_of((pairs + j) * 128, 128), 128)],
+                qkv.at[i, :, pl.ds(pl.multiple_of((2 * pairs + j) * 128, 128), 128)],
+                count,
+                o.at[i, :, pl.ds(pl.multiple_of(j * 128, 128), 128)],
+                lse.at[i, :, pl.ds(pl.multiple_of(j * 128, 128), 128)],
+            )
+            return 0
+
+        lax.fori_loop(0, pairs, body, 0)
+
+    attend(0)
+    attend(1)
+    d_way.second()
+    keep(o, o_out)
+    keep(lse, lse_out)
+    o_way.last()
+
+    def out_tile(start):
+        return dot_nn(o[0, at(start, tile), :], w_out[0]) + dot_nn(
+            o[1, at(start, tile), :], w_out[1]
+        )
+
+    def out_theirs(t, _):
+        a_send[at(t * tile, tile), :] = out_tile(other0 + t * tile).astype(BF)
+        return 0
+
+    def out_ours(t, _):
+        a_own[at(t * tile, tile), :] = out_tile(mine0 + t * tile)
+        return 0
+
+    lax.fori_loop(0, 2, out_theirs, 0)
+    links.send(a_send, a_recv, swap_sems.at[2], other, links.z)
+    lax.fori_loop(0, 2, out_ours, 0)
+    links.arrived(a_send, a_recv, swap_sems.at[2])
+
+    def middle_norms(t, _):
+        rows = at(t * tile, tile)
+        branch = a_own[rows, :] + a_recv[rows, :].astype(F32) + vec_ref[8:9, :]
+        a_own[rows, :] = branch
+        unit, _ = stats(branch)
+        middle = xb[rows, :].astype(F32) + unit * vec_ref[1:2, :] + vec_ref[5:6, :]
+        mid[rows, :] = middle
+        unit, _ = stats(middle)
+        h2[at(mine0 + t * tile, tile), :] = (unit * vec_ref[2:3, :] + vec_ref[6:7, :]).astype(BF)
+        return 0
+
+    lax.fori_loop(0, 2, middle_norms, 0)
+    links.send(h2.at[at(mine0, half), :], h2.at[at(mine0, half), :], swap_sems.at[3], other, links.z)
+    keep(a_own, a_out)
+    keep(mid, mid_out)
+    u_way.last()
+
+    def up(start):
+        def body(t, _):
+            rows = at(start + t * tile, tile)
+            for i in range(2):
+                value, slant = gelu_both(dot_nn(h2[rows, :], w_up[i]) + upb_ref[i : i + 1, :])
+                act[i, rows, :] = value
+                slope[i, rows, :] = slant
+            return 0
+
+        lax.fori_loop(0, 2, body, 0)
+
+    up(mine0)
+    links.arrived(h2.at[at(mine0, half), :], h2.at[at(other0, half), :], swap_sems.at[3])
+    up(other0)
+    keep(h2, h2_out)
+    keep(act, act_out)
+    keep(slope, slope_out)
+    d_way.last()
+
+    def down_tile(start):
+        return dot_nn(act[0, at(start, tile), :], w_down[0]) + dot_nn(
+            act[1, at(start, tile), :], w_down[1]
+        )
+
+    def down_theirs(t, _):
+        f_send[at(t * tile, tile), :] = down_tile(other0 + t * tile).astype(BF)
+        return 0
+
+    def down_ours(t, _):
+        f_own[at(t * tile, tile), :] = down_tile(mine0 + t * tile)
+        return 0
+
+    lax.fori_loop(0, 2, down_theirs, 0)
+    links.send(f_send, f_recv, swap_sems.at[4], other, links.z)
+    lax.fori_loop(0, 2, down_ours, 0)
+    for weight, w_hbm in zip(weights[1:], w_outs):
+        keep(weight, w_hbm)
+    links.arrived(f_send, f_recv, swap_sems.at[4])
+
+    def last_norm(t, _):
+        rows = at(t * tile, tile)
+        value = f_own[rows, :] + f_recv[rows, :].astype(F32) + vec_ref[9:10, :]
+        f_own[rows, :] = value
+        unit, _ = stats(value)
+        y[rows, :] = (mid[rows, :] + unit * vec_ref[3:4, :] + vec_ref[7:8, :]).astype(BF)
+        return 0
+
+    lax.fori_loop(0, 2, last_norm, 0)
+    keep(f_own, f_out)
+    keep(y, y_out)
+    exchange_tokens_wait(links, grads, g_out, tok_sems.at[1])
+    for copy in kept:
+        copy.wait()
+    links.finish()
+
+
+def spread_smalls(n_dp, smalls, vec_ref, bias_ref, upb_ref):
+    width = vec_ref.shape[1]
+    slim = width // n_dp
+    per_qv = bias_ref.shape[1] // 3 // n_dp
+    per_up = upb_ref.shape[1] // n_dp
+    row = [
+        [smalls[i, 16 * dp : 16 * dp + 16, :].astype(F32) for dp in range(n_dp)] for i in range(2)
     ]
-    ways[0].column()
-    ways[1].column()
-    exchange_tokens(links, tokens, x_out, tok_sems.at[0])
-    for way in ways[2:]:
-        way.column()
-    exchange_tokens(links, grads, g_out, tok_sems.at[1])
-    ways[0].first()
-    for a in range(1, 5):
-        ways[a].first()
-        ways[a - 1].second()
-    ways[4].second()
-    exchange_tokens_wait(links, tokens, x_out, tok_sems.at[0])
-    exchange_tokens_wait(links, grads, g_out, tok_sems.at[1])
-    for way in ways:
-        way.last()
-    links.finish()
-
-
-def gather_all(n_dp, n_mp, tokens, grads, blocks):
+    wide = jnp.concatenate([row[0][dp][2:12, 0:slim] for dp in range(n_dp)], axis=1)
+    vec_ref[0:10, :] = wide
+    vec_ref[10:16, :] = jnp.zeros((6, width), F32)
+    for i in range(2):
+        queries = [row[i][dp][0:1, 0:per_qv] for dp in range(n_dp)]
+        values = [row[i][dp][0:1, per_qv : 2 * per_qv] for dp in range(n_dp)]
+        zeros = [jnp.zeros((1, n_dp * per_qv), F32)]
+        bias_ref[i : i + 1, :] = jnp.concatenate(queries + zeros + values, axis=1)
+        upb_ref[i : i + 1, :] = jnp.concatenate(
+            [row[i][dp][1:2, 0:per_up] for dp in range(n_dp)], axis=1
+        )
+
+
+def attend_pair_fwd(q_ref, k_ref, v_ref, count, o_ref, lse_ref):
+    length = q_ref.shape[0]
+    lane = lax.broadcasted_iota(jnp.int32, (1, 128), 1)
+    for start, stop in row_blocks(length):
+        own, before = masks(start, stop, length, count)
+        outs = []
+        lses = []
+        for head in range(2):
+            q = jnp.where((lane >= 64) == (head == 1), q_ref[start:stop, :], jnp.zeros((), BF))
+            s2 = jnp.where(own, dot_nt(q, k_ref[start:stop, :]), NEG)
+            top = jnp.max(s2, axis=-1, keepdims=True)
+            if start:
+                s1 = dot_nt(q, k_ref[0:start, :])
+                if before is not None:
+                    s1 = jnp.where(before, s1, NEG)
+                top = jnp.maximum(top, jnp.max(s1, axis=-1, keepdims=True))
+            e2 = jnp.exp(ALPHA * (s2 - top))
+            total = jnp.sum(e2, axis=-1, keepdims=True)
+            acc = dot_nn(e2.astype(BF), v_ref[start:stop, :])
+            if start:
+                e1 = jnp.exp(ALPHA * (s1 - top))
+                total = total + jnp.sum(e1, axis=-1, keepdims=True)
+                acc = acc + dot_nn(e1.astype(BF), v_ref[0:start, :])
+            outs.append(acc / total)
+            lses.append(ALPHA * top + jnp.log(total))
+        o_ref[start:stop, :] = jnp.where(lane < 64, outs[0], outs[1]).astype(BF)
+        lse_ref[start:stop, :] = jnp.where(lane < 64, lses[0], lses[1])
+
+
+def forward_all(n_dp, n_mp, tokens, grads, seg_ids, blocks):
     groups = n_dp // 2
     hops = groups - 1
     any_spec = pl.BlockSpec(memory_space=pl.ANY)
-    half = (2 * tokens.shape[1], tokens.shape[2])
-    shapes = [jax.ShapeDtypeStruct(half, tokens.dtype)] * 2 + [
-        jax.ShapeDtypeStruct((2, n_dp * b.shape[0], b.shape[1]), b.dtype) for b in blocks
-    ]
+    vmem = pl.BlockSpec(memory_space=pltpu.VMEM)
+    width = tokens.shape[2]
+    half = 2 * tokens.shape[1]
+    length = 2 * half
+    cols3 = blocks[1].shape[1]
+    cols = cols3 // 3
+    ff = n_dp * blocks[4].shape[0]
+    shape = jax.ShapeDtypeStruct
+    full = [(2, n_dp * b.shape[0], b.shape[1]) for b in blocks]
+    out_shape = [
+        shape((half, width), BF),
+        shape((half, width), BF),
+        shape((length, width), BF),
+        shape((2, length, cols3), BF),
+        shape((2, length, cols), BF),
+        shape((2, length, cols), F32),
+        shape((half, width), F32),
+        shape((half, width), F32),
+        shape((length, width), BF),
+        shape((2, length, ff), BF),
+        shape((2, length, ff), BF),
+        shape((half, width), F32),
+        shape((half, width), BF),
+    ] + [shape(f, BF) for f in full[1:]] + [shape((8, 128), jnp.int32), shape((16, width), F32)]
     return pl.pallas_call(
-        functools.partial(gather_kernel, n_dp, n_mp),
-        in_specs=[any_spec] * 7,
-        out_specs=[any_spec] * 7,
-        out_shape=shapes,
-        scratch_shapes=[
-            pltpu.SemaphoreType.DMA((4 + 5 * (n_mp + 2 * hops),)),
+        functools.partial(forward_kernel, n_dp, n_mp),
+        in_specs=[any_spec] * 2 + [vmem] + [any_spec] * 5,
+        out_specs=[any_spec] * 17 + [vmem] * 2,
+        out_shape=out_shape,
+        scratch_shapes=[pltpu.VMEM(f, BF) for f in full]
+        + [
+            pltpu.VMEM((half, width), BF),
+            pltpu.VMEM(seg_ids.shape, jnp.int32),
+            pltpu.VMEM((length, width), BF),
+            pltpu.VMEM((2, length, cols3), BF),
+            pltpu.VMEM((2, length, cols), BF),
+            pltpu.VMEM((2, length, cols), F32),
+            pltpu.VMEM((half, width), BF),
+            pltpu.VMEM((half, width), BF),
+            pltpu.VMEM((half, width), F32),
+            pltpu.VMEM((half, width), F32),
+            pltpu.VMEM((length, width), BF),
+            pltpu.VMEM((2, length, ff), BF),
+            pltpu.VMEM((2, length, ff), BF),
+            pltpu.VMEM((half, width), BF),
+            pltpu.VMEM((half, width), BF),
+            pltpu.VMEM((half, width), F32),
+            pltpu.VMEM((half, width), BF),
+            pltpu.VMEM((2, cols3), F32),
+            pltpu.VMEM((2, ff), F32),
+            pltpu.SemaphoreType.DMA((9 + 5 * sends_of_column(n_mp, hops),)),
             pltpu.SemaphoreType.DMA((5, 2, 2)),
             pltpu.SemaphoreType.DMA((5, 2, groups)),
             pltpu.SemaphoreType.DMA((2, 2)),
+            pltpu.SemaphoreType.DMA((5,)),
+            pltpu.SemaphoreType.DMA((17,)),
         ],
-        compiler_params=pltpu.CompilerParams(collective_id=0, has_side_effects=True),
-    )(tokens, grads, *blocks)
+        compiler_params=pltpu.CompilerParams(
+            collective_id=0, has_side_effects=True, vmem_limit_bytes=60 << 20
+        ),
+    )(tokens, grads, seg_ids, *blocks)
 
 
 def build(n_dp, n_mp):
@@ -601,65 +839,43 @@
         small = jnp.concatenate(rows, axis=0)
         small = jnp.pad(small, ((0, 16 - small.shape[0]), (0, 0)))
         small = jnp.pad(small, ((0, 0), (0, max(0, 128 - small.shape[1]))))
+        cols = qkv_weight.shape[2]
         block_qkv = qkv_weight.transpose(1, 0, 2).reshape(qkv_weight.shape[1], -1)
-        x, grad_y, every, w_qkv, w_out, w_up, w_down = gather_all(
+        (
+            x,
+            grad_y,
+            h1,
+            qkvs,
+            attended,
+            log_sums,
+            branch,
+            middle,
+            h2,
+            acts,
+            slopes,
+            ffn_out,
+            out_rows,
+            w_qkv,
+            w_out,
+            w_up,
+            w_down,
+            count,
+            vec,
+        ) = forward_all(
             n_dp,
             n_mp,
             tokens,
             out_grad,
+            seg_ids,
             [small, block_qkv, out_weight, up_weight, down_weight],
         )
         x = x.astype(F32)
         grad_y = grad_y.astype(F32)
-        every = every.reshape(2, n_dp, *small.shape).astype(F32)
-        wide = every[0, :, :, :slim].transpose(1, 0, 2).reshape(small.shape[0], width)
-        gains = wide[2:6]
-        shifts = wide[6:10]
-        branch_b = wide[10:12]
-        qv_b = every[:, :, 0, : 2 * per_qv].reshape(2, n_dp, 2, per_qv)
-        qv_b = qv_b.transpose(0, 2, 1, 3).reshape(2, 2, n_dp * per_qv)
-        up_b = every[:, :, 1, : up_bias.shape[0]].reshape(2, -1)
-
-        seg_other = swap(seg_ids)
-        seg_own = pick2((core + z) % 2, seg_ids, seg_other)
-        seg_row = lax.dynamic_index_in_dim(seg_own, z // 2, 0, keepdims=False)
-        seg_r = jnp.broadcast_to(seg_row[None, :], (8, length))
-        seg_c = jnp.broadcast_to(seg_row[length - CAPTION :, None], (CAPTION, 128))
-
+        gains = vec[0:4]
         unit0, inv0 = stats(x)
-        h1 = share((unit0 * gains[0] + shifts[0]).astype(BF))
-        cols = w_qkv[0].shape[1] // 3
-        qkvs = []
-        attended = []
-        log_sums = []
-        partial = None
-        for i in range(2):
-            bias = jnp.concatenate([qv_b[i, 0], jnp.zeros((cols,), F32), qv_b[i, 1]])
-            factor = jnp.concatenate([jnp.full((cols,), SCALE, F32), jnp.ones((2 * cols,), F32)])
-            qkv = ((dot_nn(h1, w_qkv[i]) + bias) * factor).astype(BF)
-            o, lse = attend_forward(qkv, seg_c, seg_r)
-            qkvs.append(qkv)
-            attended.append(o)
-            log_sums.append(lse)
-            term = dot_nn(o, w_out[i])
-            partial = term if partial is None else partial + term
-        branch = reduce_half(partial) + branch_b[0]
         unit1, inv1 = stats(branch)
-        middle = x + unit1 * gains[1] + shifts[1]
         unit2, inv2 = stats(middle)
-        h2 = share((unit2 * gains[2] + shifts[2]).astype(BF))
-        acts = []
-        slopes = []
-        partial = None
-        for i in range(2):
-            act, slope = gelu_both(dot_nn(h2, w_up[i]) + up_b[i])
-            acts.append(act)
-            slopes.append(slope)
-            term = dot_nn(act, w_down[i])
-            partial = term if partial is None else partial + term
-        ffn_out = reduce_half(partial) + branch_b[1]
         unit3, inv3 = stats(ffn_out)
-        out_rows = (middle + unit3 * gains[3] + shifts[3]).astype(BF)
         layer_out = jnp.stack(from_rows(out_rows))
 
         grad_f, dgain3, dshift3 = norm_back(unit3, inv3, gains[3], grad_y)
@@ -693,7 +909,7 @@
         for i in range(2):
             dw_out.append(dot_tn(attended[i], grad_a_all))
             grad_o = dot_nt(grad_a_all, w_out[i]).astype(BF)
-            grad_qkv = attend_backward(qkvs[i], grad_o, log_sums[i], seg_c, seg_r)
+            grad_qkv = attend_backward(qkvs[i], grad_o, log_sums[i], count)
             sums = jnp.sum(grad_qkv.astype(F32), axis=0)
             dqv.append(jnp.stack([sums[:cols], sums[2 * cols :]]))
             dw_qkv.append(dot_tn(h1, grad_qkv))

time: 666 us -> 589 us (0.88)
  matrix products: 68.1 us -> 37.2 us
  Pallas kernels: 180 us -> 163 us
  starting transfers between devices: 101 us -> 87.6 us
  other arithmetic: 54.6 us -> 45.5 us
    dot_general x8 -> x0, matrix products: 25.9 us -> none  [dot_nn(): lax.dot_general(a, b, (((1,), (0,)), ((), ())), preferred_element_type=F32)]
    pallas_call x3 -> x1, Pallas kernels: 150 us -> 133 us  [forward_all(): pl.pallas_call(functools.partial(forward_kernel, n_dp, n_mp), in_specs=[a...]
    ppermute x9 -> x4, starting transfers between devices: 15 us -> 1.94 us  [swap(): return lax.ppermute(value, 'dp', [(i, i ^ 1) for i in range(n_dp)])]
    ppermute x16, starting transfers between devices: 50.6 us -> 40.5 us  [scatter(): got = lax.ppermute(mine, both, weight_in[k]).astype(F32)]
    ppermute x9 -> x4, waiting for transfers between devices: 9.76 us -> 0.01 us  [swap(): return lax.ppermute(value, 'dp', [(i, i ^ 1) for i in range(n_dp)])]
    ppermute x4, waiting for transfers between devices: 18.9 us -> 9.63 us  [from_rows(): got.append(lax.ppermute(mine, both, token_in[k]))]
    ppermute x24, waiting for transfers between devices: 39 us -> 46.9 us  [hop(): return lax.ppermute(value, 'dp', [(i, i ^ 2 * bit) for i in range(n_dp)])]
    ppermute x4, starting transfers between devices: 17.4 us -> 25.1 us  [from_rows(): got.append(lax.ppermute(mine, both, token_in[k]))]
  transfers between devices with their start and end apart: 54 -> 49, of which waited for: 19 -> 13; matrix products, arithmetic and copies ran while one was open for 10% -> 12% of each run, Pallas kernels for 0% -> 0%
where the time goes in v3:
time: 589 us; the launch traced here: 579 us
  waiting for transfers between devices  195 us (33%)
  Pallas kernels  163 us (28%)
  starting transfers between devices  87.6 us (15%)
  other arithmetic  45.5 us (8%)
  matrix products  37.2 us (6%)
  local copies, waits for them, and re-layouts  35.5 us (6%)
  between operations  15.5 us (3%)
    pallas_call x1, Pallas kernels, forward_all(): pl.pallas_call(functools.partial(forward_kernel, n_dp, n_mp), in_specs=[a...  133 us
    psum x1, waiting for transfers between devices, on_device(): vectors = lax.psum(vectors, both)  114 us
    ppermute x24, waiting for transfers between devices, hop(): return lax.ppermute(value, 'dp', [(i, i ^ 2 * bit) for i in range(n_dp)])  46.9 us
    ppermute x16, starting transfers between devices, scatter(): got = lax.ppermute(mine, both, weight_in[k]).astype(F32)  40.5 us
    pallas_call x2, Pallas kernels, attend_backward(): pl.pallas_call(attend_bwd_kernel, grid=(pairs,), in_specs=[col(0), col(pa...  29.9 us
    ppermute x4, starting transfers between devices, from_rows(): got.append(lax.ppermute(mine, both, token_in[k]))  25.1 us
    ppermute x16, waiting for transfers between devices, scatter(): got = lax.ppermute(mine, both, weight_in[k]).astype(F32)  23.7 us
    dot_general x8, matrix products, dot_tn(): lax.dot_general(a, b, (((0,), (0,)), ((), ())), preferred_element_type=F32)  21.6 us
  transfers between devices with their start and end apart: 49, of which 13 were waited for; matrix products, arithmetic and copies ran while one was open for 12% of the time, Pallas kernels for 0%

profile of v3, /device:TPU:1, one launch (start us, length us, event | category | flops | bytes accessed | tf_op | source)
XLA Modules:
  0.0 578.7 jit_solution(5913734072072783260)
XLA Ops:
  9.9 2.2 concatenate.30
  12.7 132.9 %shard_map.203 = (bf16[544,1024]{1,0:T(8,128)(2,1)}, bf16[544,1024]{1,0:T(8,128)(2,1)}, bf16[1088,1024]{1,0:T(8,128)(2,1)}, bf16[2,1088,768]{2,1,0:T(8,128)(2,1)...) custom-call(bf16[2,272,1024]{2,1,0:T(8,128)(2,1)} %refs_0_.1, ...), custom_call_target="tpu_custom_call" | custom-call | tf_op jit(solution)/shard_map/pallas_call | solution.py:645
  153.8 2.3 dynamic-slice_bitcast_fusion.3
  156.2 8.9 %collective-permute-start = (bf16[272,1024]{1,0:T(8,128)(2,1)}, bf16[272,1024]{1,0:T(8,128)(2,1)}, u32[]{:S(2)}, u32[]{:S(2)}) collective-permute-start(bf16[272,1024]{1,0:T(8,128)(2,1)} %get-tuple-element.109), channel_id=1, source_target_pairs={{0,0},{2,1},{4,2},{6,3},{1,4},{3,5},{5,6},{7,7},{8,8},{10,9},{12,1... | collective-permute-start | bytes 1671176 | tf_op jit(solution)/shard_map/ppermute | solution.py:767
  165.1 10.5 %collective-permute-start.1 = (bf16[272,1024]{1,0:T(8,128)(2,1)}, bf16[272,1024]{1,0:T(8,128)(2,1)}, u32[]{:S(2)}, u32[]{:S(2)}) collective-permute-start(bf16[272,1024]{1,0:T(8,128)(2,1)} %get-tuple-element.110), channel_id=1, source_target_pairs={{2,0},{0,1},{6,2},{4,3},{3,4},{1,5},{7,6},{5,7},{10,8},{8,9},{14,1... | collective-permute-start | bytes 1671176 | tf_op jit(solution)/shard_map/ppermute | solution.py:767
  177.7 2.4 multiply_reduce_fusion.3
  182.4 3.1 slice_bitcast_fusion.2
  185.5 9.6 %collective-permute-done.1 = bf16[272,1024]{1,0:T(8,128)(2,1)} collective-permute-done((bf16[272,1024]{1,0:T(8,128)(2,1)}, bf16[272,1024]{1,0:T(8,128)(2,1)}, u32[]{:S(2)}, u32[]{:S(2)}) %collective-permute-start.1) | collective-permute-done | bytes 557088 | tf_op jit(solution)/shard_map/ppermute | solution.py:767
  199.4 5.5 fusion.40
  204.9 3.2 fusion.37
  208.2 2.6 convert_reduce_fusion
  210.8 2.6 convert_reduce_fusion.1
  217.2 3.2 convolution_convert_fusion.2
  222.8 3.3 convolution_convert_fusion.3
  229.7 2.5 fusion.30
  232.2 2.5 convolution_add_fusion.1
  234.8 2.0 copy-done.15
  246.9 14.1 %collective-permute-done.43 = bf16[256,1024]{1,0:T(8,128)(2,1)S(1)} collective-permute-done((bf16[256,1024]{1,0:T(8,128)(2,1)S(1)}, bf16[256,1024]{1,0:T(8,128)(2,1)S(1)}, u32[]{:S(2)}, u32[]{:S(2)}) %collective-permute-start.43) | collective-permute-done | bytes 524320 | tf_op jit(solution)/shard_map/ppermute | solution.py:719
  270.8 2.1 multiply_reduce_fusion.1
  274.3 3.6 collective-permute-start.45
  277.9 3.7 collective-permute-done.33
  282.0 4.0 collective-permute-start.46
  286.0 2.3 collective-permute-start.47
  289.0 4.4 collective-permute-start.34
  295.1 2.7 collective-permute-done.47
  297.8 2.8 collective-permute-start.37
  301.5 2.1 collective-permute-done.35
  303.6 8.7 %collective-permute-done.36 = bf16[128,1024]{1,0:T(8,128)(2,1)S(1)} collective-permute-done((bf16[128,1024]{1,0:T(8,128)(2,1)S(1)}, bf16[128,1024]{1,0:T(8,128)(2,1)S(1)}, u32[]{:S(2)}, u32[]{:S(2)}) %collective-permute-start.36) | collective-permute-done | bytes 262176 | tf_op jit(solution)/shard_map/ppermute | solution.py:813
  312.3 8.1 %collective-permute-done.37 = bf16[128,1024]{1,0:T(8,128)(2,1)S(1)} collective-permute-done((bf16[128,1024]{1,0:T(8,128)(2,1)S(1)}, bf16[128,1024]{1,0:T(8,128)(2,1)S(1)}, u32[]{:S(2)}, u32[]{:S(2)}) %collective-permute-start.37) | collective-permute-done | bytes 262176 | tf_op jit(solution)/shard_map/ppermute | solution.py:813
  326.8 14.7 %shard_map.205 = bf16[1088,768]{1,0:T(8,128)(2,1)S(1)} custom-call(bf16[1088,768]{1,0:T(8,128)(2,1)S(1)} %get-tuple-element.83.q_ref.k_ref.v_ref, bf16[1088,768]{1,0:T(8,128)(2,1)S(1)} %get-tuple-element.83.q_ref.k_ref.v_ref, bf16[1088,768]{1,0:T(8,128)(2,1)S(1)} %get-tuple-element.83.q_ref.k_ref.v_ref, ...), custom_call_target="tpu_custom_call" | custom-call | flops 6060769280 | bytes 5013504 | tf_op jit(solution)/shard_map/pallas_call | solution.py:122
  341.8 15.3 %shard_map.204 = bf16[1088,768]{1,0:T(8,128)(2,1)S(1)} custom-call(bf16[1088,768]{1,0:T(8,128)(2,1)S(1)} %get-tuple-element.84.q_ref.k_ref.v_ref, bf16[1088,768]{1,0:T(8,128)(2,1)S(1)} %get-tuple-element.84.q_ref.k_ref.v_ref, bf16[1088,768]{1,0:T(8,128)(2,1)S(1)} %get-tuple-element.84.q_ref.k_ref.v_ref, ...), custom_call_target="tpu_custom_call" | custom-call | flops 6060769280 | bytes 5013504 | tf_op jit(solution)/shard_map/pallas_call | solution.py:122
  357.4 2.3 convolution_convert_fusion.4
  359.7 2.3 convolution_convert_fusion.5
  374.1 3.0 collective-permute-done.23
  379.3 13.3 %collective-permute-done.20 = bf16[64,1024]{1,0:T(8,128)(2,1)S(1)} collective-permute-done((bf16[64,1024]{1,0:T(8,128)(2,1)S(1)}, bf16[64,1024]{1,0:T(8,128)(2,1)S(1)}, u32[]{:S(2)}, u32[]{:S(2)}) %collective-permute-start.20) | collective-permute-done | bytes 131104 | tf_op jit(solution)/shard_map/ppermute | solution.py:719
  392.9 2.5 collective-permute-start.24
  395.4 3.8 collective-permute-start.25
  399.4 3.2 collective-permute-start.26
  407.0 2.1 collective-permute-done.27
  410.2 5.6 collective-permute-done.13
  416.3 7.1 %collective-permute-done.8 = bf16[256,768]{1,0:T(8,128)(2,1)} collective-permute-done((bf16[256,768]{1,0:T(8,128)(2,1)S(1)}, bf16[256,768]{1,0:T(8,128)(2,1)}, u32[]{:S(2)}, u32[]{:S(2)}) %collective-permute-start.8) | collective-permute-done | bytes 393248 | tf_op jit(solution)/shard_map/ppermute | solution.py:719
  426.1 2.7 collective-permute-start.14
  429.6 2.5 collective-permute-start.16
  432.1 2.1 collective-permute-start.17
  434.3 4.3 fusion.15
  440.0 2.4 fusion.14
  442.5 4.5 collective-permute-start.6
  450.4 114.3 %all-reduce.4.cloned.1.call-done = f32[16,1024]{1,0:T(8,128)} async-done(((f32[16,1024]{1,0:T(8,128)}), f32[16,1024]{1,0:T(8,128)}) %all-reduce.4.cloned.1.call-update) | async-done | bytes 65552 | tf_op jit(solution)/shard_map/psum | solution.py:952
  (246 shorter events, 96.9 us)
Async XLA Ops:
  7.2 557.5 %all-reduce.4.cloned.1.call-start = ((), (), s32[]{:S(2)}) async-start(), calls=%async_computation | async-start | bytes 131072 | tf_op jit(solution)/shard_map/psum | solution.py:952
  152.0 45.5 %collective-permute-start.2 = (bf16[544,1024]{1,0:T(8,128)(2,1)}, bf16[544,1024]{1,0:T(8,128)(2,1)}, u32[]{:S(2)}, u32[]{:S(2)}) collective-permute-start(bf16[544,1024]{1,0:T(8,128)(2,1)} %get-tuple-element.77), channel_id=1, source_target_pairs={{0,4},{4,0},{8,12},{12,8},{16,20},{20,16},{24,28},{28,24},{1,5},{5... | collective-permute-start | bytes 3342344 | tf_op jit(solution)/shard_map/ppermute | solution.py:716
  156.2 29.3 %collective-permute-start = (bf16[272,1024]{1,0:T(8,128)(2,1)}, bf16[272,1024]{1,0:T(8,128)(2,1)}, u32[]{:S(2)}, u32[]{:S(2)}) collective-permute-start(bf16[272,1024]{1,0:T(8,128)(2,1)} %get-tuple-element.109), channel_id=1, source_target_pairs={{0,0},{2,1},{4,2},{6,3},{1,4},{3,5},{5,6},{7,7},{8,8},{10,9},{12,1... | collective-permute-start | bytes 1671176 | tf_op jit(solution)/shard_map/ppermute | solution.py:767
  165.1 30.0 %collective-permute-start.1 = (bf16[272,1024]{1,0:T(8,128)(2,1)}, bf16[272,1024]{1,0:T(8,128)(2,1)}, u32[]{:S(2)}, u32[]{:S(2)}) collective-permute-start(bf16[272,1024]{1,0:T(8,128)(2,1)} %get-tuple-element.110), channel_id=1, source_target_pairs={{2,0},{0,1},{6,2},{4,3},{3,4},{1,5},{7,6},{5,7},{10,8},{8,9},{14,1... | collective-permute-start | bytes 1671176 | tf_op jit(solution)/shard_map/ppermute | solution.py:767
  214.4 23.6 %collective-permute-start.42 = (bf16[256,1024]{1,0:T(8,128)(2,1)}, bf16[256,1024]{1,0:T(8,128)(2,1)}, u32[]{:S(2)}, u32[]{:S(2)}) collective-permute-start(bf16[256,1024]{1,0:T(8,128)(2,1)} %get-tuple-element.92), channel_id=1, source_target_pairs={{0,8},{4,12},{8,0},{12,4},{16,24},{20,28},{24,16},{28,20},{1,9},{5... | collective-permute-start | bytes 1572872 | tf_op jit(solution)/shard_map/ppermute | solution.py:719
  215.7 30.3 %collective-permute-start.41 = (bf16[256,1024]{1,0:T(8,128)(2,1)}, bf16[256,1024]{1,0:T(8,128)(2,1)}, u32[]{:S(2)}, u32[]{:S(2)}) collective-permute-start(bf16[256,1024]{1,0:T(8,128)(2,1)} %get-tuple-element.91), channel_id=1, source_target_pairs={{0,8},{4,12},{8,0},{12,4},{16,24},{20,28},{24,16},{28,20},{1,9},{5... | collective-permute-start | bytes 1572872 | tf_op jit(solution)/shard_map/ppermute | solution.py:719
  217.0 23.0 %collective-permute-start.39 = (bf16[256,1024]{1,0:T(8,128)(2,1)}, bf16[256,1024]{1,0:T(8,128)(2,1)}, u32[]{:S(2)}, u32[]{:S(2)}) collective-permute-start(bf16[256,1024]{1,0:T(8,128)(2,1)} %get-tuple-element.94), channel_id=1, source_target_pairs={{0,16},{4,20},{8,24},{12,28},{16,0},{20,4},{24,8},{28,12},{1,17},{... | collective-permute-start | bytes 1572872 | tf_op jit(solution)/shard_map/ppermute | solution.py:719
  221.6 20.9 %collective-permute-start.32 = (bf16[256,1024]{1,0:T(8,128)(2,1)}, bf16[256,1024]{1,0:T(8,128)(2,1)}, u32[]{:S(2)}, u32[]{:S(2)}) collective-permute-start(bf16[256,1024]{1,0:T(8,128)(2,1)} %get-tuple-element.96), channel_id=1, source_target_pairs={{0,8},{4,12},{8,0},{12,4},{16,24},{20,28},{24,16},{28,20},{1,9},{5... | collective-permute-start | bytes 1572872 | tf_op jit(solution)/shard_map/ppermute | solution.py:719
  228.5 14.1 %collective-permute-start.29 = (bf16[256,1024]{1,0:T(8,128)(2,1)}, bf16[256,1024]{1,0:T(8,128)(2,1)}, u32[]{:S(2)}, u32[]{:S(2)}) collective-permute-start(bf16[256,1024]{1,0:T(8,128)(2,1)} %get-tuple-element.98), channel_id=1, source_target_pairs={{0,16},{4,20},{8,24},{12,28},{16,0},{20,4},{24,8},{28,12},{1,17},{... | collective-permute-start | bytes 1572872 | tf_op jit(solution)/shard_map/ppermute | solution.py:719
  238.1 26.0 %collective-permute-start.38 = (bf16[256,1024]{1,0:T(8,128)(2,1)}, bf16[256,1024]{1,0:T(8,128)(2,1)S(1)}, u32[]{:S(2)}, u32[]{:S(2)}) collective-permute-start(bf16[256,1024]{1,0:T(8,128)(2,1)} %get-tuple-element.93), channel_id=1, source_target_pairs={{0,16},{4,20},{8,24},{12,28},{16,0},{20,4},{24,8},{28,12},{1,17},{... | collective-permute-start | bytes 1572872 | tf_op jit(solution)/shard_map/ppermute | solution.py:719
  240.0 20.9 %collective-permute-start.43 = (bf16[256,1024]{1,0:T(8,128)(2,1)S(1)}, bf16[256,1024]{1,0:T(8,128)(2,1)S(1)}, u32[]{:S(2)}, u32[]{:S(2)}) collective-permute-start(bf16[256,1024]{1,0:T(8,128)(2,1)S(1)} %fusion.48), channel_id=1, source_target_pairs={{0,16},{4,20},{8,24},{12,28},{16,0},{20,4},{24,8},{28,12},{1,17},{... | collective-permute-start | bytes 1572872 | tf_op jit(solution)/shard_map/ppermute | solution.py:719
  242.5 24.4 %collective-permute-start.3 = (bf16[544,1024]{1,0:T(8,128)(2,1)}, bf16[544,1024]{1,0:T(8,128)(2,1)S(1)}, u32[]{:S(2)}, u32[]{:S(2)}) collective-permute-start(bf16[544,1024]{1,0:T(8,128)(2,1)} %dynamic-slice_convert_fusion.1), channel_id=1, source_target_pairs={{0,4},{4,0},{8,12},{12,8},{16,20},{20,16},{24,28},{28,24},{1,5},{5... | collective-permute-start | bytes 3342344 | tf_op jit(solution)/shard_map/ppermute | solution.py:716
  242.6 21.6 %collective-permute-start.40 = (bf16[256,1024]{1,0:T(8,128)(2,1)S(1)}, bf16[256,1024]{1,0:T(8,128)(2,1)S(1)}, u32[]{:S(2)}, u32[]{:S(2)}) collective-permute-start(bf16[256,1024]{1,0:T(8,128)(2,1)S(1)} %fusion.50), channel_id=1, source_target_pairs={{0,8},{4,12},{8,0},{12,4},{16,24},{20,28},{24,16},{28,20},{1,9},{5... | collective-permute-start | bytes 1572872 | tf_op jit(solution)/shard_map/ppermute | solution.py:719
  246.0 28.3 %collective-permute-start.31 = (bf16[256,1024]{1,0:T(8,128)(2,1)S(1)}, bf16[256,1024]{1,0:T(8,128)(2,1)S(1)}, u32[]{:S(2)}, u32[]{:S(2)}) collective-permute-start(bf16[256,1024]{1,0:T(8,128)(2,1)S(1)} %copy-done.25), channel_id=1, source_target_pairs={{0,8},{4,12},{8,0},{12,4},{16,24},{20,28},{24,16},{28,20},{1,9},{5... | collective-permute-start | bytes 1572872 | tf_op jit(solution)/shard_map/ppermute | solution.py:719
  260.9 21.0 %collective-permute-start.28 = (bf16[256,1024]{1,0:T(8,128)(2,1)S(1)}, bf16[256,1024]{1,0:T(8,128)(2,1)S(1)}, u32[]{:S(2)}, u32[]{:S(2)}) collective-permute-start(bf16[256,1024]{1,0:T(8,128)(2,1)S(1)} %copy-done.24), channel_id=1, source_target_pairs={{0,16},{4,20},{8,24},{12,28},{16,0},{20,4},{24,8},{28,12},{1,17},{... | collective-permute-start | bytes 1572872 | tf_op jit(solution)/shard_map/ppermute | solution.py:719
  264.1 17.6 %collective-permute-start.33 = (bf16[256,1024]{1,0:T(8,128)(2,1)S(1)}, bf16[256,1024]{1,0:T(8,128)(2,1)S(1)}, u32[]{:S(2)}, u32[]{:S(2)}) collective-permute-start(bf16[256,1024]{1,0:T(8,128)(2,1)S(1)} %fusion.52), channel_id=1, source_target_pairs={{0,16},{4,20},{8,24},{12,28},{16,0},{20,4},{24,8},{28,12},{1,17},{... | collective-permute-start | bytes 1572872 | tf_op jit(solution)/shard_map/ppermute | solution.py:719
  264.2 21.8 %collective-permute-start.30 = (bf16[256,1024]{1,0:T(8,128)(2,1)S(1)}, bf16[256,1024]{1,0:T(8,128)(2,1)S(1)}, u32[]{:S(2)}, u32[]{:S(2)}) collective-permute-start(bf16[256,1024]{1,0:T(8,128)(2,1)S(1)} %fusion.54), channel_id=1, source_target_pairs={{0,8},{4,12},{8,0},{12,4},{16,24},{20,28},{24,16},{28,20},{1,9},{5... | collective-permute-start | bytes 1572872 | tf_op jit(solution)/shard_map/ppermute | solution.py:719
  266.9 22.0 %collective-permute-start.44 = (bf16[128,1024]{1,0:T(8,128)(2,1)S(1)}, bf16[128,1024]{1,0:T(8,128)(2,1)S(1)}, u32[]{:S(2)}, u32[]{:S(2)}) collective-permute-start(bf16[128,1024]{1,0:T(8,128)(2,1)S(1)} %get-tuple-element.111), channel_id=1, source_target_pairs={{0,0},{2,1},{4,2},{6,3},{1,4},{3,5},{5,6},{7,7},{8,8},{10,9},{12,1... | collective-permute-start | bytes 786440 | tf_op jit(solution)/shard_map/ppermute | solution.py:813
  274.3 19.1 %collective-permute-start.45 = (bf16[128,1024]{1,0:T(8,128)(2,1)S(1)}, bf16[128,1024]{1,0:T(8,128)(2,1)S(1)}, u32[]{:S(2)}, u32[]{:S(2)}) collective-permute-start(bf16[128,1024]{1,0:T(8,128)(2,1)S(1)} %get-tuple-element.112), channel_id=1, source_target_pairs={{1,0},{3,1},{5,2},{7,3},{0,4},{2,5},{4,6},{6,7},{9,8},{11,9},{13,1... | collective-permute-start | bytes 786440 | tf_op jit(solution)/shard_map/ppermute | solution.py:813
  281.7 39.7 %collective-permute-start.4 = (bf16[544,1024]{1,0:T(8,128)(2,1)S(1)}, bf16[544,1024]{1,0:T(8,128)(2,1)S(1)}, u32[]{:S(2)}, u32[]{:S(2)}) collective-permute-start(bf16[544,1024]{1,0:T(8,128)(2,1)S(1)} %get-tuple-element.79), channel_id=1, source_target_pairs={{0,4},{4,0},{8,12},{12,8},{16,20},{20,16},{24,28},{28,24},{1,5},{5... | collective-permute-start | bytes 3342344 | tf_op jit(solution)/shard_map/ppermute | solution.py:716
  282.0 11.5 %collective-permute-start.46 = (bf16[128,1024]{1,0:T(8,128)(2,1)S(1)}, bf16[128,1024]{1,0:T(8,128)(2,1)S(1)}, u32[]{:S(2)}, u32[]{:S(2)}) collective-permute-start(bf16[128,1024]{1,0:T(8,128)(2,1)S(1)} %get-tuple-element.113), channel_id=1, source_target_pairs={{2,0},{0,1},{6,2},{4,3},{3,4},{1,5},{7,6},{5,7},{10,8},{8,9},{14,1... | collective-permute-start | bytes 786440 | tf_op jit(solution)/shard_map/ppermute | solution.py:813
  286.0 11.8 %collective-permute-start.47 = (bf16[128,1024]{1,0:T(8,128)(2,1)S(1)}, bf16[128,1024]{1,0:T(8,128)(2,1)S(1)}, u32[]{:S(2)}, u32[]{:S(2)}) collective-permute-start(bf16[128,1024]{1,0:T(8,128)(2,1)S(1)} %get-tuple-element.114), channel_id=1, source_target_pairs={{3,0},{1,1},{7,2},{5,3},{2,4},{0,5},{6,6},{4,7},{11,8},{9,9},{15,1... | collective-permute-start | bytes 786440 | tf_op jit(solution)/shard_map/ppermute | solution.py:813
  289.0 12.6 %collective-permute-start.34 = (bf16[128,1024]{1,0:T(8,128)(2,1)S(1)}, bf16[128,1024]{1,0:T(8,128)(2,1)S(1)}, u32[]{:S(2)}, u32[]{:S(2)}) collective-permute-start(bf16[128,1024]{1,0:T(8,128)(2,1)S(1)} %get-tuple-element.115), channel_id=1, source_target_pairs={{0,0},{2,1},{4,2},{6,3},{1,4},{3,5},{5,6},{7,7},{8,8},{10,9},{12,1... | collective-permute-start | bytes 786440 | tf_op jit(solution)/shard_map/ppermute | solution.py:813
  293.4 10.3 %collective-permute-start.35 = (bf16[128,1024]{1,0:T(8,128)(2,1)S(1)}, bf16[128,1024]{1,0:T(8,128)(2,1)S(1)}, u32[]{:S(2)}, u32[]{:S(2)}) collective-permute-start(bf16[128,1024]{1,0:T(8,128)(2,1)S(1)} %get-tuple-element.116), channel_id=1, source_target_pairs={{1,0},{3,1},{5,2},{7,3},{0,4},{2,5},{4,6},{6,7},{9,8},{11,9},{13,1... | collective-permute-start | bytes 786440 | tf_op jit(solution)/shard_map/ppermute | solution.py:813
  293.5 18.9 %collective-permute-start.36 = (bf16[128,1024]{1,0:T(8,128)(2,1)S(1)}, bf16[128,1024]{1,0:T(8,128)(2,1)S(1)}, u32[]{:S(2)}, u32[]{:S(2)}) collective-permute-start(bf16[128,1024]{1,0:T(8,128)(2,1)S(1)} %get-tuple-element.117), channel_id=1, source_target_pairs={{2,0},{0,1},{6,2},{4,3},{3,4},{1,5},{7,6},{5,7},{10,8},{8,9},{14,1... | collective-permute-start | bytes 786440 | tf_op jit(solution)/shard_map/ppermute | solution.py:813
  297.8 22.7 %collective-permute-start.37 = (bf16[128,1024]{1,0:T(8,128)(2,1)S(1)}, bf16[128,1024]{1,0:T(8,128)(2,1)S(1)}, u32[]{:S(2)}, u32[]{:S(2)}) collective-permute-start(bf16[128,1024]{1,0:T(8,128)(2,1)S(1)} %get-tuple-element.118), channel_id=1, source_target_pairs={{3,0},{1,1},{7,2},{5,3},{2,4},{0,5},{6,6},{4,7},{11,8},{9,9},{15,1... | collective-permute-start | bytes 786440 | tf_op jit(solution)/shard_map/ppermute | solution.py:813
  362.1 9.1 %collective-permute-start.22 = (bf16[64,1024]{1,0:T(8,128)(2,1)S(1)}, bf16[64,1024]{1,0:T(8,128)(2,1)S(1)}, u32[]{:S(2)}, u32[]{:S(2)}) collective-permute-start(bf16[64,1024]{1,0:T(8,128)(2,1)S(1)} %get-tuple-element.124), channel_id=1, source_target_pairs={{0,8},{4,12},{8,0},{12,4},{16,24},{20,28},{24,16},{28,20},{1,9},{5... | collective-permute-start | bytes 393224 | tf_op jit(solution)/shard_map/ppermute | solution.py:719
  362.7 10.2 %collective-permute-start.21 = (bf16[64,1024]{1,0:T(8,128)(2,1)S(1)}, bf16[64,1024]{1,0:T(8,128)(2,1)S(1)}, u32[]{:S(2)}, u32[]{:S(2)}) collective-permute-start(bf16[64,1024]{1,0:T(8,128)(2,1)S(1)} %get-tuple-element.123), channel_id=1, source_target_pairs={{0,8},{4,12},{8,0},{12,4},{16,24},{20,28},{24,16},{28,20},{1,9},{5... | collective-permute-start | bytes 393224 | tf_op jit(solution)/shard_map/ppermute | solution.py:719
  363.6 8.1 %collective-permute-start.19 = (bf16[64,1024]{1,0:T(8,128)(2,1)S(1)}, bf16[64,1024]{1,0:T(8,128)(2,1)S(1)}, u32[]{:S(2)}, u32[]{:S(2)}) collective-permute-start(bf16[64,1024]{1,0:T(8,128)(2,1)S(1)} %get-tuple-element.126), channel_id=1, source_target_pairs={{0,16},{4,20},{8,24},{12,28},{16,0},{20,4},{24,8},{28,12},{1,17},{... | collective-permute-start | bytes 393224 | tf_op jit(solution)/shard_map/ppermute | solution.py:719
  364.9 13.1 %collective-permute-start.18 = (bf16[64,1024]{1,0:T(8,128)(2,1)S(1)}, bf16[64,1024]{1,0:T(8,128)(2,1)S(1)}, u32[]{:S(2)}, u32[]{:S(2)}) collective-permute-start(bf16[64,1024]{1,0:T(8,128)(2,1)S(1)} %get-tuple-element.125), channel_id=1, source_target_pairs={{0,16},{4,20},{8,24},{12,28},{16,0},{20,4},{24,8},{28,12},{1,17},{... | collective-permute-start | bytes 393224 | tf_op jit(solution)/shard_map/ppermute | solution.py:719
  369.3 65.0 %collective-permute-start.5 = (bf16[544,1024]{1,0:T(8,128)(2,1)S(1)}, bf16[544,1024]{1,0:T(8,128)(2,1)}, u32[]{:S(2)}, u32[]{:S(2)}) collective-permute-start(bf16[544,1024]{1,0:T(8,128)(2,1)S(1)} %dynamic-slice_convert_fusion), channel_id=1, source_target_pairs={{0,4},{4,0},{8,12},{12,8},{16,20},{20,16},{24,28},{28,24},{1,5},{5... | collective-permute-start | bytes 3342344 | tf_op jit(solution)/shard_map/ppermute | solution.py:716
  371.2 24.3 %collective-permute-start.12 = (bf16[256,768]{1,0:T(8,128)(2,1)S(1)}, bf16[256,768]{1,0:T(8,128)(2,1)S(1)}, u32[]{:S(2)}, u32[]{:S(2)}) collective-permute-start(bf16[256,768]{1,0:T(8,128)(2,1)S(1)} %get-tuple-element.100), channel_id=1, source_target_pairs={{0,8},{4,12},{8,0},{12,4},{16,24},{20,28},{24,16},{28,20},{1,9},{5... | collective-permute-start | bytes 1179656 | tf_op jit(solution)/shard_map/ppermute | solution.py:719
  372.9 37.3 %collective-permute-start.11 = (bf16[256,768]{1,0:T(8,128)(2,1)S(1)}, bf16[256,768]{1,0:T(8,128)(2,1)S(1)}, u32[]{:S(2)}, u32[]{:S(2)}) collective-permute-start(bf16[256,768]{1,0:T(8,128)(2,1)S(1)} %get-tuple-element.99), channel_id=1, source_target_pairs={{0,8},{4,12},{8,0},{12,4},{16,24},{20,28},{24,16},{28,20},{1,9},{5... | collective-permute-start | bytes 1179656 | tf_op jit(solution)/shard_map/ppermute | solution.py:719
  377.1 15.6 %collective-permute-start.20 = (bf16[64,1024]{1,0:T(8,128)(2,1)S(1)}, bf16[64,1024]{1,0:T(8,128)(2,1)S(1)}, u32[]{:S(2)}, u32[]{:S(2)}) collective-permute-start(bf16[64,1024]{1,0:T(8,128)(2,1)S(1)} %fusion.86), channel_id=1, source_target_pairs={{0,8},{4,12},{8,0},{12,4},{16,24},{20,28},{24,16},{28,20},{1,9},{5... | collective-permute-start | bytes 393224 | tf_op jit(solution)/shard_map/ppermute | solution.py:719
  378.1 26.6 %collective-permute-start.9 = (bf16[256,768]{1,0:T(8,128)(2,1)S(1)}, bf16[256,768]{1,0:T(8,128)(2,1)S(1)}, u32[]{:S(2)}, u32[]{:S(2)}) collective-permute-start(bf16[256,768]{1,0:T(8,128)(2,1)S(1)} %get-tuple-element.102), channel_id=1, source_target_pairs={{0,16},{4,20},{8,24},{12,28},{16,0},{20,4},{24,8},{28,12},{1,17},{... | collective-permute-start | bytes 1179656 | tf_op jit(solution)/shard_map/ppermute | solution.py:719
  392.9 6.5 %collective-permute-start.24 = (bf16[32,1024]{1,0:T(8,128)(2,1)S(1)}, bf16[32,1024]{1,0:T(8,128)(2,1)S(1)}, u32[]{:S(2)}, u32[]{:S(2)}) collective-permute-start(bf16[32,1024]{1,0:T(8,128)(2,1)S(1)} %get-tuple-element.127), channel_id=1, source_target_pairs={{0,0},{2,1},{4,2},{6,3},{1,4},{3,5},{5,6},{7,7},{8,8},{10,9},{12,1... | collective-permute-start | bytes 196616 | tf_op jit(solution)/shard_map/ppermute | solution.py:813
  395.4 7.1 %collective-permute-start.25 = (bf16[32,1024]{1,0:T(8,128)(2,1)S(1)}, bf16[32,1024]{1,0:T(8,128)(2,1)S(1)}, u32[]{:S(2)}, u32[]{:S(2)}) collective-permute-start(bf16[32,1024]{1,0:T(8,128)(2,1)S(1)} %get-tuple-element.128), channel_id=1, source_target_pairs={{1,0},{3,1},{5,2},{7,3},{0,4},{2,5},{4,6},{6,7},{9,8},{11,9},{13,1... | collective-permute-start | bytes 196616 | tf_op jit(solution)/shard_map/ppermute | solution.py:813
  399.4 7.4 %collective-permute-start.26 = (bf16[32,1024]{1,0:T(8,128)(2,1)S(1)}, bf16[32,1024]{1,0:T(8,128)(2,1)S(1)}, u32[]{:S(2)}, u32[]{:S(2)}) collective-permute-start(bf16[32,1024]{1,0:T(8,128)(2,1)S(1)} %get-tuple-element.129), channel_id=1, source_target_pairs={{2,0},{0,1},{6,2},{4,3},{3,4},{1,5},{7,6},{5,7},{10,8},{8,9},{14,1... | collective-permute-start | bytes 196616 | tf_op jit(solution)/shard_map/ppermute | solution.py:813
  402.6 6.5 %collective-permute-start.27 = (bf16[32,1024]{1,0:T(8,128)(2,1)S(1)}, bf16[32,1024]{1,0:T(8,128)(2,1)S(1)}, u32[]{:S(2)}, u32[]{:S(2)}) collective-permute-start(bf16[32,1024]{1,0:T(8,128)(2,1)S(1)} %get-tuple-element.130), channel_id=1, source_target_pairs={{3,0},{1,1},{7,2},{5,3},{2,4},{0,5},{6,6},{4,7},{11,8},{9,9},{15,1... | collective-permute-start | bytes 196616 | tf_op jit(solution)/shard_map/ppermute | solution.py:813
  404.6 11.3 %collective-permute-start.13 = (bf16[256,768]{1,0:T(8,128)(2,1)S(1)}, bf16[256,768]{1,0:T(8,128)(2,1)S(1)}, u32[]{:S(2)}, u32[]{:S(2)}) collective-permute-start(bf16[256,768]{1,0:T(8,128)(2,1)S(1)} %fusion.56), channel_id=1, source_target_pairs={{0,16},{4,20},{8,24},{12,28},{16,0},{20,4},{24,8},{28,12},{1,17},{... | collective-permute-start | bytes 1179656 | tf_op jit(solution)/shard_map/ppermute | solution.py:719
  406.8 16.6 %collective-permute-start.8 = (bf16[256,768]{1,0:T(8,128)(2,1)S(1)}, bf16[256,768]{1,0:T(8,128)(2,1)}, u32[]{:S(2)}, u32[]{:S(2)}) collective-permute-start(bf16[256,768]{1,0:T(8,128)(2,1)S(1)} %get-tuple-element.101), channel_id=1, source_target_pairs={{0,16},{4,20},{8,24},{12,28},{16,0},{20,4},{24,8},{28,12},{1,17},{... | collective-permute-start | bytes 1179656 | tf_op jit(solution)/shard_map/ppermute | solution.py:719
  409.1 14.3 %collective-permute-start.10 = (bf16[256,768]{1,0:T(8,128)(2,1)}, bf16[256,768]{1,0:T(8,128)(2,1)}, u32[]{:S(2)}, u32[]{:S(2)}) collective-permute-start(bf16[256,768]{1,0:T(8,128)(2,1)} %fusion.58), channel_id=1, source_target_pairs={{0,8},{4,12},{8,0},{12,4},{16,24},{20,28},{24,16},{28,20},{1,9},{5... | collective-permute-start | bytes 1179656 | tf_op jit(solution)/shard_map/ppermute | solution.py:719
  426.1 21.0 %collective-permute-start.14 = (bf16[128,768]{0,1:T(8,128)(2,1)}, bf16[128,768]{0,1:T(8,128)(2,1)}, u32[]{:S(2)}, u32[]{:S(2)}) collective-permute-start(bf16[128,768]{0,1:T(8,128)(2,1)} %get-tuple-element.119), channel_id=1, source_target_pairs={{0,0},{2,1},{4,2},{6,3},{1,4},{3,5},{5,6},{7,7},{8,8},{10,9},{12,1... | collective-permute-start | bytes 589832 | tf_op jit(solution)/shard_map/ppermute | solution.py:813
  428.8 19.3 %collective-permute-start.15 = (bf16[128,768]{0,1:T(8,128)(2,1)}, bf16[128,768]{0,1:T(8,128)(2,1)}, u32[]{:S(2)}, u32[]{:S(2)}) collective-permute-start(bf16[128,768]{0,1:T(8,128)(2,1)} %get-tuple-element.120), channel_id=1, source_target_pairs={{1,0},{3,1},{5,2},{7,3},{0,4},{2,5},{4,6},{6,7},{9,8},{11,9},{13,1... | collective-permute-start | bytes 589832 | tf_op jit(solution)/shard_map/ppermute | solution.py:813
  429.6 18.5 %collective-permute-start.16 = (bf16[128,768]{0,1:T(8,128)(2,1)}, bf16[128,768]{0,1:T(8,128)(2,1)}, u32[]{:S(2)}, u32[]{:S(2)}) collective-permute-start(bf16[128,768]{0,1:T(8,128)(2,1)} %get-tuple-element.121), channel_id=1, source_target_pairs={{2,0},{0,1},{6,2},{4,3},{3,4},{1,5},{7,6},{5,7},{10,8},{8,9},{14,1... | collective-permute-start | bytes 589832 | tf_op jit(solution)/shard_map/ppermute | solution.py:813
  432.1 16.0 %collective-permute-start.17 = (bf16[128,768]{0,1:T(8,128)(2,1)}, bf16[128,768]{0,1:T(8,128)(2,1)}, u32[]{:S(2)}, u32[]{:S(2)}) collective-permute-start(bf16[128,768]{0,1:T(8,128)(2,1)} %get-tuple-element.122), channel_id=1, source_target_pairs={{3,0},{1,1},{7,2},{5,3},{2,4},{0,5},{6,6},{4,7},{11,8},{9,9},{15,1... | collective-permute-start | bytes 589832 | tf_op jit(solution)/shard_map/ppermute | solution.py:813
  442.5 127.6 %collective-permute-start.6 = (bf16[272,1024]{1,0:T(8,128)(2,1)S(1)}, bf16[272,1024]{1,0:T(8,128)(2,1)S(1)}, u32[]{:S(2)}, u32[]{:S(2)}) collective-permute-start(bf16[272,1024]{1,0:T(8,128)(2,1)S(1)} %get-tuple-element.105), channel_id=1, source_target_pairs={{0,0},{2,1},{4,2},{6,3},{1,4},{3,5},{5,6},{7,7},{8,8},{10,9},{12,1... | collective-permute-start | bytes 1671176 | tf_op jit(solution)/shard_map/ppermute | solution.py:767
  447.1 123.0 %collective-permute-start.7 = (bf16[272,1024]{1,0:T(8,128)(2,1)S(1)}, bf16[272,1024]{1,0:T(8,128)(2,1)S(1)}, u32[]{:S(2)}, u32[]{:S(2)}) collective-permute-start(bf16[272,1024]{1,0:T(8,128)(2,1)S(1)} %get-tuple-element.106), channel_id=1, source_target_pairs={{2,0},{0,1},{6,2},{4,3},{3,4},{1,5},{7,6},{5,7},{10,8},{8,9},{14,1... | collective-permute-start | bytes 1671176 | tf_op jit(solution)/shard_map/ppermute | solution.py:767
  (38 other events, 283.3 us)
Sparse Core Ops, SparseCore 0:
  440.1 124.5 all-reduce.3

commit v4 on v3

--- a/solution.py
+++ b/solution.py
@@ -69,77 +69,6 @@
     same = real == (lax.broadcasted_iota(jnp.int32, (1, rows), 1) + start < count)
     before = real == (lax.broadcasted_iota(jnp.int32, (1, start), 1) < count)
     return jnp.logical_and(own, same), before
-
-
-def attend_bwd_kernel(
-    q_ref, k_ref, v_ref, do_ref, lse_ref, count_ref, d_ref, dk_ref, dv_ref
-):
-    length = q_ref.shape[0]
-    pair = pl.program_id(0)
-    pairs = d_ref.shape[1] // 384
-    lane = lax.broadcasted_iota(jnp.int32, (1, 128), 1)
-    dk_ref[...] = jnp.zeros_like(dk_ref)
-    dv_ref[...] = jnp.zeros_like(dv_ref)
-    zero = jnp.zeros((), BF)
-    for start, stop in row_blocks(length):
-        own, before = masks(start, stop, length, count_ref[0:1, 0:1])
-        dqs = []
-        for head in range(2):
-            mine = (lane >= 64) == (head == 1)
-            q = jnp.where(mine, q_ref[start:stop, :], zero)
-            do = jnp.where(mine, do_ref[start:stop, :], zero)
-            lse = lse_ref[start:stop, head * 64 : head * 64 + 1]
-            p2 = jnp.where(own, jnp.exp(ALPHA * dot_nt(q, k_ref[start:stop, :]) - lse), 0.0)
-            g2 = dot_nt(do, v_ref[start:stop, :])
-            delta = jnp.sum(p2 * g2, axis=-1, keepdims=True)
-            if start:
-                p1 = jnp.exp(ALPHA * dot_nt(q, k_ref[0:start, :]) - lse)
-                if before is not None:
-                    p1 = jnp.where(before, p1, 0.0)
-                g1 = dot_nt(do, v_ref[0:start, :])
-                delta = delta + jnp.sum(p1 * g1, axis=-1, keepdims=True)
-            ds2 = (ALPHA * p2 * (g2 - delta)).astype(BF)
-            dq = dot_nn(ds2, k_ref[start:stop, :])
-            dk_ref[start:stop, :] += dot_tn(ds2, q)
-            dv_ref[start:stop, :] += dot_tn(p2.astype(BF), do)
-            if start:
-                ds1 = (ALPHA * p1 * (g1 - delta)).astype(BF)
-                dq = dq + dot_nn(ds1, k_ref[0:start, :])
-                dk_ref[0:start, :] += dot_tn(ds1, q)
-                dv_ref[0:start, :] += dot_tn(p1.astype(BF), do)
-            dqs.append(dq)
-        merged = jnp.where(lane < 64, dqs[0], dqs[1]) * SCALE
-        d_ref[start:stop, pl.ds(pl.multiple_of(pair * 128, 128), 128)] = merged.astype(BF)
-    d_ref[:, pl.ds(pl.multiple_of((pairs + pair) * 128, 128), 128)] = dk_ref[...].astype(BF)
-    d_ref[:, pl.ds(pl.multiple_of((2 * pairs + pair) * 128, 128), 128)] = dv_ref[...].astype(BF)
-
-
-def attend_backward(qkv, grad_o, lse, count):
-    length, width = qkv.shape
-    pairs = width // 384
-    col = lambda base: pl.BlockSpec((length, 128), lambda j, base=base: (0, base + j))
-    whole = lambda a: pl.BlockSpec(a.shape, lambda j: (0, 0))
-    return pl.pallas_call(
-        attend_bwd_kernel,
-        grid=(pairs,),
-        in_specs=[
-            col(0),
-            col(pairs),
-            col(2 * pairs),
-            col(0),
-            col(0),
-            whole(count),
-        ],
-        out_specs=pl.BlockSpec((length, width), lambda j: (0, 0)),
-        out_shape=jax.ShapeDtypeStruct((length, width), BF),
-        scratch_shapes=[pltpu.VMEM((length, 128), F32), pltpu.VMEM((length, 128), F32)],
-        compiler_params=pltpu.CompilerParams(vmem_limit_bytes=48 << 20),
-        cost_estimate=pl.CostEstimate(
-            flops=20 * pairs * length * length * 128,
-            bytes_accessed=18 * length * 128 * pairs,
-            transcendentals=pairs * length * length,
-        ),
-    )(qkv, qkv, qkv, grad_o, lse, count)
 
 
 MESH = pl.DeviceIdType.MESH
@@ -202,6 +131,11 @@
         copy.start()
         self.used += 1
         self.open.append((None, copy))
+        return copy
+
+    def wait_sent(self, copy):
+        copy.wait_send()
+        self.open = [entry for entry in self.open if entry[1] is not copy]
 
     def send_or_keep(self, src, dst, recv_sem, dp, z):
         own = jnp.logical_and(dp == self.dp, z == self.z)
@@ -460,12 +394,14 @@
                 qkv.at[i, :, pl.ds(pl.multiple_of((2 * pairs + j) * 128, 128), 128)],
                 count,
                 o.at[i, :, pl.ds(pl.multiple_of(j * 128, 128), 128)],
-                lse.at[i, :, pl.ds(pl.multiple_of(j * 128, 128), 128)],
+                lse,
+                2 * (i * pairs + j),
             )
             return 0
 
         lax.fori_loop(0, pairs, body, 0)
 
+    lse[...] = jnp.zeros_like(lse)
     attend(0)
     attend(1)
     d_way.second()
@@ -585,7 +521,7 @@
         )
 
 
-def attend_pair_fwd(q_ref, k_ref, v_ref, count, o_ref, lse_ref):
+def attend_pair_fwd(q_ref, k_ref, v_ref, count, o_ref, lse_ref, head0):
     length = q_ref.shape[0]
     lane = lax.broadcasted_iota(jnp.int32, (1, 128), 1)
     for start, stop in row_blocks(length):
@@ -611,7 +547,8 @@
             outs.append(acc / total)
             lses.append(ALPHA * top + jnp.log(total))
         o_ref[start:stop, :] = jnp.where(lane < 64, outs[0], outs[1]).astype(BF)
-        lse_ref[start:stop, :] = jnp.where(lane < 64, lses[0], lses[1])
+        kept = jnp.where(lane == head0, lses[0], lse_ref[start:stop, :])
+        lse_ref[start:stop, :] = jnp.where(lane == head0 + 1, lses[1], kept)
 
 
 def forward_all(n_dp, n_mp, tokens, grads, seg_ids, blocks):
@@ -633,7 +570,7 @@
         shape((length, width), BF),
         shape((2, length, cols3), BF),
         shape((2, length, cols), BF),
-        shape((2, length, cols), F32),
+        shape((length, 128), F32),
         shape((half, width), F32),
         shape((half, width), F32),
         shape((length, width), BF),
@@ -654,7 +591,7 @@
             pltpu.VMEM((length, width), BF),
             pltpu.VMEM((2, length, cols3), BF),
             pltpu.VMEM((2, length, cols), BF),
-            pltpu.VMEM((2, length, cols), F32),
+            pltpu.VMEM((length, 128), F32),
             pltpu.VMEM((half, width), BF),
             pltpu.VMEM((half, width), BF),
             pltpu.VMEM((half, width), F32),
@@ -681,43 +618,536 @@
     )(tokens, grads, seg_ids, *blocks)
 
 
+def attend_pair_bwd(q_ref, k_ref, v_ref, do_ref, lse_ref, head0, count, dk_ref, dv_ref):
+    length = q_ref.shape[0]
+    lane = lax.broadcasted_iota(jnp.int32, (1, 128), 1)
+    dk_ref[...] = jnp.zeros_like(dk_ref)
+    dv_ref[...] = jnp.zeros_like(dv_ref)
+    zero = jnp.zeros((), BF)
+    for start, stop in row_blocks(length):
+        own, before = masks(start, stop, length, count)
+        dqs = []
+        for head in range(2):
+            mine = (lane >= 64) == (head == 1)
+            q = jnp.where(mine, q_ref[start:stop, :], zero)
+            do = jnp.where(mine, do_ref[start:stop, :], zero)
+            lse = jnp.sum(
+                jnp.where(lane == head0 + head, lse_ref[start:stop, :], 0.0), axis=-1, keepdims=True
+            )
+            p2 = jnp.where(own, jnp.exp(ALPHA * dot_nt(q, k_ref[start:stop, :]) - lse), 0.0)
+            g2 = dot_nt(do, v_ref[start:stop, :])
+            delta = jnp.sum(p2 * g2, axis=-1, keepdims=True)
+            if start:
+                p1 = jnp.exp(ALPHA * dot_nt(q, k_ref[0:start, :]) - lse)
+                if before is not None:
+                    p1 = jnp.where(before, p1, 0.0)
+                g1 = dot_nt(do, v_ref[0:start, :])
+                delta = delta + jnp.sum(p1 * g1, axis=-1, keepdims=True)
+            ds2 = (ALPHA * p2 * (g2 - delta)).astype(BF)
+            dq = dot_nn(ds2, k_ref[start:stop, :])
+            dk_ref[start:stop, :] += dot_tn(ds2, q)
+            dv_ref[start:stop, :] += dot_tn(p2.astype(BF), do)
+            if start:
+                ds1 = (ALPHA * p1 * (g1 - delta)).astype(BF)
+                dq = dq + dot_nn(ds1, k_ref[0:start, :])
+                dk_ref[0:start, :] += dot_tn(ds1, q)
+                dv_ref[0:start, :] += dot_tn(p1.astype(BF), do)
+            dqs.append(dq)
+        q_ref[start:stop, :] = (jnp.where(lane < 64, dqs[0], dqs[1]) * SCALE).astype(BF)
+    k_ref[...] = dk_ref[...].astype(BF)
+    v_ref[...] = dv_ref[...].astype(BF)
+
+
+FAR = (1, 3, 4)
+
+
+class Reduce:
+    def __init__(self, links, part, slots, column, slot_sems, column_sems, load):
+        self.load, self.near, self.copies = load, [], []
+        self.links, self.part, self.slots, self.column = links, part, slots, column
+        self.slot_sems, self.column_sems = slot_sems, column_sems
+        self.groups = links.n_dp // 2
+        self.rows = part.shape[1] // links.n_dp
+        self.steps = [plan_hops(self.groups, i)[::-1] for i in range(2)]
+
+    def piece(self, i, rel):
+        return self.part.at[i, rows_at(self.links.group ^ rel, 2 * self.rows), :]
+
+    def slot(self, i, rel):
+        return self.slots.at[i, pl.ds((rel - 1) * 2 * self.rows, 2 * self.rows), :]
+
+    def give(self, i, rel, bit):
+        k = self.links
+        k.send(self.piece(i, rel), self.slot(i, rel), self.slot_sems.at[i, rel], k.dp ^ (2 * bit), k.z)
+
+    def start(self, i):
+        bit, known = self.steps[i][0]
+        for rel in known[::-1]:
+            self.give(i, rel ^ bit, bit)
+
+    def add(self, i, rel, slot):
+        tile = min(32, 2 * self.rows)
+        base = (self.links.group ^ rel) * 2 * self.rows
+
+        def body(t, _):
+            rows = pl.ds(pl.multiple_of(base + t * tile, tile), tile)
+            came = self.slots[i, pl.ds(pl.multiple_of((slot - 1) * 2 * self.rows + t * tile, tile), tile), :]
+            total = self.part[i, rows, :].astype(F32) + came.astype(F32)
+            self.part[i, rows, :] = total.astype(self.part.dtype)
+            return 0
+
+        lax.fori_loop(0, 2 * self.rows // tile, body, 0)
+
+    def level(self, i, number):
+        k = self.links
+        bit, known = self.steps[i][number]
+        after = self.steps[i][number + 1][0] if number + 1 < len(self.steps[i]) else 0
+        for rel in sorted(known, key=lambda r: not r & after):
+            k.arrived(self.piece(i, rel), self.slot(i, rel ^ bit), self.slot_sems.at[i, rel ^ bit])
+            self.add(i, rel, rel ^ bit)
+            if rel & after:
+                self.give(i, rel, after)
+        if not after:
+            for c in range(2):
+                k.send_or_keep(
+                    self.part.at[i, rows_at(2 * k.group + c, self.rows), :],
+                    self.column.at[k.z],
+                    self.column_sems.at[k.z],
+                    2 * k.group + c,
+                    2 * k.core + i,
+                )
+
+    def levels(self, number):
+        for i in range(2):
+            self.level(i, number)
+
+    def collect(self):
+        if self.near:
+            return
+        for zz in range(self.links.n_mp):
+            term = self.column.at[zz]
+            self.links.arrived(term, term, self.column_sems.at[zz])
+            if self.load:
+                near = self.slots.at[0, pl.ds(zz * self.rows, self.rows), :]
+                self.copies.append(self.load(term, near))
+                term = near
+            self.near.append(term)
+
+    def total(self, out):
+        self.collect()
+        for copy in self.copies:
+            copy.wait()
+        tile = min(32, self.rows)
+
+        def body(t, _):
+            rows = pl.ds(pl.multiple_of(t * tile, tile), tile)
+            value = self.near[0][rows, :].astype(F32)
+            for ref in self.near[1:]:
+                value = value + ref[rows, :].astype(F32)
+            out[rows, :] = value
+            return 0
+
+        lax.fori_loop(0, self.rows // tile, body, 0)
+
+
+def return_tokens(links, parts, dst, sems):
+    quarter = dst.shape[1]
+    m = links.z // 2
+    for s in range(2):
+        links.send_or_keep(
+            parts.at[pl.ds(s * quarter, quarter), :],
+            dst.at[m],
+            sems.at[m],
+            2 * links.group + lax.rem(links.z, 2),
+            2 * links.core + s,
+        )
+
+
+def return_tokens_wait(links, dst, sems):
+    for m in range(2):
+        links.arrived(dst.at[m], dst.at[m], sems.at[m])
+
+
+def backward_kernel(n_dp, n_mp, *refs):
+    (y_hbm, g_hbm, x_hbm, a_hbm, mid_hbm, f_hbm, h1_hbm, qkv_hbm, o_hbm, lse_hbm) = refs[0:10]
+    (h2_hbm, act_hbm, slope_hbm, wq_hbm, wo_hbm, wu_hbm, wd_hbm, vec_ref, count_ref) = refs[10:19]
+    (layer_out, grad_out, q_out, o_out, u_out, d_out, v_out, back) = refs[19:27]
+    fars = refs[27:30]
+    refs = refs[:27] + refs[30:]
+    parts = refs[27:32]
+    slots = refs[32:37]
+    columns = list(refs[37:42])
+    for a, far in zip(FAR, fars):
+        columns[a] = far
+    (pair, take, own, own2, g_buf) = refs[42:47]
+    refs = refs[:47] + (None,) + refs[47:]
+    (act, du, h, wd, wu, lse, dk, dv, vsum, vtake, vqkv, vup) = refs[48:60]
+    (send_sems, slot_sems, column_sems, tok_sems, swap_sems, load_sems) = refs[60:66]
+    links = Links(n_dp, n_mp, send_sems)
+    half = g_buf.shape[0]
+    length = 2 * half
+    tile = half // 2
+    width = g_buf.shape[1]
+    other = links.dp + 1 - 2 * links.core
+    mine0 = links.core * half
+    other0 = (1 - links.core) * half
+    cols3 = qkv_hbm.shape[2]
+    cols = cols3 // 3
+    loads = [0]
+    parts = list(parts)
+    give = h.at[pl.ds(0, half), :]
+    parts[1] = du.at[:, pl.ds(0, width), pl.ds(cols, cols3)]
+    if parts[2].dtype == BF:
+        parts[2] = wu.at[:, pl.ds(half, cols), :]
+    else:
+        parts[2] = own2.at[:, pl.ds(0, cols), :]
+
+    def load(src, dst):
+        copy = pltpu.make_async_copy(src, dst, load_sems.at[loads[0]])
+        loads[0] += 1
+        copy.start()
+        return copy
+
+    def at(start, rows):
+        return pl.ds(pl.multiple_of(start, 16), rows)
+
+    def gain(k):
+        return vec_ref[k : k + 1, :]
+
+    f_load = load(f_hbm, own)
+    g_load = load(g_hbm, g_buf)
+    act_load = load(act_hbm, act)
+    wd_load = load(wd_hbm, wd)
+    slope_load = load(slope_hbm, du)
+    h_load = load(h2_hbm, h)
+    wu_load = load(wu_hbm, wu)
+    lse_load = load(lse_hbm, lse)
+    vsum[...] = jnp.zeros_like(vsum)
+    vqkv[...] = jnp.zeros_like(vqkv)
+    vup[...] = jnp.zeros_like(vup)
+    links.barrier()
+    ways = [
+        Reduce(
+            links,
+            parts[a],
+            slots[a],
+            columns[a],
+            slot_sems.at[a],
+            column_sems.at[a],
+            load if a in FAR else None,
+        )
+        for a in range(5)
+    ]
+    v_way, q_way, o_way, u_way, d_way = ways
+    return_tokens(links, y_hbm, layer_out, tok_sems.at[0])
+
+    def norm_grad(value, k, grad):
+        unit, inverse = stats(value)
+        back, dgain, dshift = norm_back(unit, inverse, gain(k), grad)
+        vsum[k : k + 1, :] += dgain[None]
+        vsum[4 + k : 5 + k, :] += dshift[None]
+        return back
+
+    f_load.wait()
+    g_load.wait()
+
+    def last_norm(t, _):
+        rows = at(t * tile, tile)
+        back = norm_grad(own[rows, :], 3, g_buf[rows, :].astype(F32)).astype(BF)
+        vsum[9:10, :] += jnp.sum(back.astype(F32), axis=0, keepdims=True)
+        pair[at(mine0 + t * tile, tile), :] = back
+        return 0
+
+    lax.fori_loop(0, 2, last_norm, 0)
+    ours = pair.at[at(mine0, half), :]
+    theirs = pair.at[at(other0, half), :]
+    df_send = links.send(ours, ours, swap_sems.at[0], other, links.z)
+    act_load.wait()
+    links.arrived(ours, theirs, swap_sems.at[0])
+
+    def weight_grad(left, right, part, i):
+        step = min(256, left.shape[1])
+
+        def body(t, _):
+            lanes = pl.ds(pl.multiple_of(t * step, 128), step)
+            rows = pl.ds(pl.multiple_of(t * step, 16), step)
+            part[i, rows, :] = dot_tn(left[:, lanes], right[...]).astype(part.dtype)
+            return 0
+
+        lax.fori_loop(0, left.shape[1] // step, body, 0)
+
+    for i in range(2):
+        weight_grad(act.at[i], pair, parts[4], i)
+        d_way.start(i)
+    qkv_load = load(qkv_hbm, act.at[:, :, 0:cols3])
+    wd_load.wait()
+    slope_load.wait()
+    h_load.wait()
+    for i in range(2):
+
+        def slant(t, _, i=i):
+            rows = at(t * tile, tile)
+            value = (dot_nt(pair[rows, :], wd[i]) * du[i, rows, :].astype(F32)).astype(BF)
+            du[i, rows, :] = value
+            vup[i : i + 1, :] += jnp.sum(value.astype(F32), axis=0, keepdims=True)
+            return 0
+
+        lax.fori_loop(0, 4, slant, 0)
+        weight_grad(h, du.at[i], parts[3], i)
+        u_way.start(i)
+    wq_load = load(wq_hbm, wd.at[:, :, 0:cols3])
+    a_load = load(a_hbm.at[pl.ds(0, tile), :], own2.at[0])
+    mid_load = load(mid_hbm.at[pl.ds(0, tile), :], own2.at[1])
+    wu_load.wait()
+
+    def up_tile(start):
+        return dot_nt(du[0, at(start, tile), :], wu[0]) + dot_nt(du[1, at(start, tile), :], wu[1])
+
+    def up_theirs(t, _):
+        give[at(t * tile, tile), :] = up_tile(other0 + t * tile).astype(BF)
+        return 0
+
+    def up_ours(t, _):
+        own[at(t * tile, tile), :] = up_tile(mine0 + t * tile)
+        return 0
+
+    lax.fori_loop(0, 2, up_theirs, 0)
+    up_send = links.send(give, take, swap_sems.at[1], other, links.z)
+    lax.fori_loop(0, 2, up_ours, 0)
+    o_load = load(o_hbm, du.at[:, :, 0:cols])
+    x_load = load(x_hbm, wu.at[0, pl.ds(0, half), :])
+    wo_load = [load(wo_hbm.at[i], wu.at[1, pl.ds(i * cols, cols), :]) for i in range(2)]
+    links.wait_sent(df_send)
+    links.arrived(give, take, swap_sems.at[1])
+    for t in range(2):
+        a_load.wait()
+        mid_load.wait()
+        rows = pl.ds(t * tile, tile)
+        grad = own[rows, :] + take[rows, :].astype(F32)
+        grad = g_buf[rows, :].astype(F32) + norm_grad(own2[1], 2, grad)
+        own[rows, :] = grad
+        grad = norm_grad(own2[0], 1, grad).astype(BF)
+        vsum[8:9, :] += jnp.sum(grad.astype(F32), axis=0, keepdims=True)
+        pair[at(mine0 + t * tile, tile), :] = grad
+        if t == 0:
+            a_load = load(a_hbm.at[pl.ds(tile, tile), :], own2.at[0])
+            mid_load = load(mid_hbm.at[pl.ds(tile, tile), :], own2.at[1])
+    links.send(ours, ours, swap_sems.at[2], other, links.z)
+    links.wait_sent(up_send)
+    h_load = load(h1_hbm, h)
+    o_load.wait()
+    qkv_load.wait()
+    wo_load[0].wait()
+    wo_load[1].wait()
+    links.arrived(ours, theirs, swap_sems.at[2])
+
+    def open_heads(t, _):
+        rows = at(t * tile, tile)
+        for i in range(2):
+            value = dot_nt(pair[rows, :], wu[1, i * cols : (i + 1) * cols, :])
+            act[i, rows, cols3 : cols3 + cols] = value.astype(BF)
+        return 0
+
+    lax.fori_loop(0, 4, open_heads, 0)
+    for i in range(2):
+        weight_grad(du.at[i, :, 0:cols], pair, parts[2], i)
+        o_way.start(i)
+    d_way.levels(0)
+    lse_load.wait()
+    h_load.wait()
+    wq_load.wait()
+    count = count_ref[0:1, 0:1]
+    pairs = cols // 128
+
+    for i in range(2):
+
+        def attend(j, _, i=i):
+            lanes = lambda base: pl.ds(pl.multiple_of((base + j) * 128, 128), 128)
+            attend_pair_bwd(
+                act.at[i, :, lanes(0)],
+                act.at[i, :, lanes(pairs)],
+                act.at[i, :, lanes(2 * pairs)],
+                act.at[i, :, lanes(3 * pairs)],
+                lse,
+                2 * (i * pairs + j),
+                count,
+                dk,
+                dv,
+            )
+            return 0
+
+        lax.fori_loop(0, pairs, attend, 0)
+        weight_grad(h, act.at[i, :, 0:cols3], parts[1], i)
+        q_way.start(i)
+        if i == 0:
+            u_way.levels(0)
+
+    def head_tile(start):
+        rows = at(start, tile)
+        total = None
+        for i in range(2):
+            value = act[i, rows, 0:cols3]
+            vqkv[i : i + 1, :] += jnp.sum(value.astype(F32), axis=0, keepdims=True)
+            term = dot_nt(value, wd[i, :, 0:cols3])
+            total = term if total is None else total + term
+        return total
+
+    def head_theirs(t, _):
+        give[at(t * tile, tile), :] = head_tile(other0 + t * tile).astype(BF)
+        return 0
+
+    lax.fori_loop(0, 2, head_theirs, 0)
+    head_send = links.send(give, take, swap_sems.at[3], other, links.z)
+    d_way.levels(1)
+    o_way.levels(0)
+    x_load.wait()
+    links.arrived(give, take, swap_sems.at[3])
+
+    def first_norm(t, _):
+        rows = at(t * tile, tile)
+        grad = head_tile(mine0 + t * tile) + take[rows, :].astype(F32)
+        grad = own[rows, :] + norm_grad(wu[0, rows, :].astype(F32), 0, grad)
+        g_buf[rows, :] = grad.astype(BF)
+        return 0
+
+    lax.fori_loop(0, 2, first_norm, 0)
+    return_tokens(links, g_buf, back, tok_sems.at[1])
+    links.send(vsum, vtake, swap_sems.at[4], other, links.z)
+    q_way.level(0, 0)
+    u_way.levels(1)
+    q_way.level(1, 0)
+    links.arrived(vsum, vtake, swap_sems.at[4])
+    gather_smalls(n_dp, vsum[...] + vtake[...], vqkv, vup, parts[0])
+    v_way.start(0)
+    v_way.start(1)
+    o_way.levels(1)
+    v_way.levels(0)
+    d_way.total(d_out)
+    u_way.collect()
+    q_way.levels(1)
+    v_way.levels(1)
+    o_way.total(o_out)
+    u_way.total(u_out)
+    links.wait_sent(head_send)
+    return_tokens_wait(links, back, tok_sems.at[1])
+    back_copies = [load(back.at[m], give.at[pl.ds(m * tile, tile), :]) for m in range(2)]
+    back_copies[0].wait()
+    back_copies[1].wait()
+
+    def widen(t, _):
+        rows = at(t * 32, 32)
+        own[rows, :] = give[rows, :].astype(F32)
+        return 0
+
+    lax.fori_loop(0, half // 32, widen, 0)
+    grad_copies = [load(own.at[pl.ds(m * tile, tile), :], grad_out.at[m]) for m in range(2)]
+    v_way.total(v_out)
+    q_way.total(q_out)
+    return_tokens_wait(links, layer_out, tok_sems.at[0])
+    grad_copies[0].wait()
+    grad_copies[1].wait()
+    links.finish()
+
+
+def gather_smalls(n_dp, total, vqkv, vup, part):
+    width = total.shape[1]
+    slim = width // n_dp
+    per_qv = vqkv.shape[1] // 3 // n_dp
+    per_up = vup.shape[1] // n_dp
+    lanes = part.shape[2]
+    values = 2 * per_qv * n_dp
+
+    def fill(value):
+        short = lanes - value.shape[1]
+        if not short:
+            return value
+        return jnp.concatenate([value, jnp.zeros((value.shape[0], short), F32)], axis=1)
+
+    for i in range(2):
+        qkv = vqkv[i : i + 1, :]
+        up = vup[i : i + 1, :]
+        for dp in range(n_dp):
+            first = jnp.concatenate(
+                [
+                    qkv[:, dp * per_qv : (dp + 1) * per_qv],
+                    qkv[:, values + dp * per_qv : values + (dp + 1) * per_qv],
+                ],
+                axis=1,
+            )
+            base = 16 * dp
+            part[i, base : base + 1, :] = fill(first)
+            part[i, base + 1 : base + 2, :] = fill(up[:, dp * per_up : (dp + 1) * per_up])
+            part[i, base + 2 : base + 12, :] = fill(total[0:10, dp * slim : (dp + 1) * slim])
+            part[i, base + 12 : base + 16, :] = jnp.zeros((4, lanes), F32)
+
+
+def backward_all(n_dp, n_mp, saved, weights, vec, count):
+    groups = n_dp // 2
+    any_spec = pl.BlockSpec(memory_space=pl.ANY)
+    vmem = pl.BlockSpec(memory_space=pltpu.VMEM)
+    shape = jax.ShapeDtypeStruct
+    half, width = saved[0].shape
+    length = 2 * half
+    cols3 = saved[7].shape[2]
+    cols = cols3 // 3
+    ff = saved[11].shape[2]
+    full = [(2, n_dp * 16, 128)] + [w.shape for w in weights]
+    each = [f[1] // n_dp for f in full]
+    kinds = [F32] + [BF if r % 8 == 0 else F32 for r in each[1:]]
+    out_shape = [shape((2, half // 2, width), BF), shape((2, half // 2, width), F32)] + [
+        shape((each[a], full[a][2]), F32) for a in (1, 2, 3, 4, 0)
+    ]
+    out_shape += [shape((2, half // 2, width), BF)]
+    out_shape += [shape((n_mp, each[a], full[a][2]), kinds[a]) for a in FAR]
+    sends = 4 + 5 + 5 * (2 * (groups - 1) + 4)
+    return pl.pallas_call(
+        functools.partial(backward_kernel, n_dp, n_mp),
+        in_specs=[any_spec] * 17 + [vmem] * 2,
+        out_specs=[any_spec] * 2 + [vmem] * 5 + [any_spec] * 4,
+        out_shape=out_shape,
+        scratch_shapes=[
+            pltpu.VMEM((1, 16, 128) if a in (1, 2) else f, k)
+            for a, (f, k) in enumerate(zip(full, kinds))
+        ]
+        + [
+            pltpu.VMEM((2, (groups - 1) * 2 * r, f[2]), k) for f, r, k in zip(full, each, kinds)
+        ]
+        + [
+            pltpu.VMEM((n_mp, 16 if a in FAR else r, f[2]), k)
+            for a, (f, r, k) in enumerate(zip(full, each, kinds))
+        ]
+        + [
+            pltpu.VMEM((length, width), BF),
+            pltpu.VMEM((half, width), BF),
+            pltpu.VMEM((half, width), F32),
+            pltpu.VMEM((2, half // 2, width), F32),
+            pltpu.VMEM((half, width), BF),
+            pltpu.VMEM((2, length, ff), BF),
+            pltpu.VMEM((2, length, ff), BF),
+            pltpu.VMEM((length, width), BF),
+            pltpu.VMEM((2, ff, width), BF),
+            pltpu.VMEM((2, width, ff), BF),
+            pltpu.VMEM((length, 128), F32),
+            pltpu.VMEM((length, 128), F32),
+            pltpu.VMEM((length, 128), F32),
+            pltpu.VMEM((16, width), F32),
+            pltpu.VMEM((16, width), F32),
+            pltpu.VMEM((2, cols3), F32),
+            pltpu.VMEM((2, ff), F32),
+            pltpu.SemaphoreType.DMA((sends,)),
+            pltpu.SemaphoreType.DMA((5, 2, groups)),
+            pltpu.SemaphoreType.DMA((5, n_mp)),
+            pltpu.SemaphoreType.DMA((2, 2)),
+            pltpu.SemaphoreType.DMA((5,)),
+            pltpu.SemaphoreType.DMA((23 + len(FAR) * n_mp,)),
+        ],
+        compiler_params=pltpu.CompilerParams(
+            collective_id=1, has_side_effects=True, vmem_limit_bytes=61 << 20
+        ),
+    )(*saved, *weights, vec, count)[:7]
+
+
 def build(n_dp, n_mp):
-    groups = n_dp // 2
-    bits = [1 << b for b in range(groups.bit_length() - 1)]
-    orders = (bits, bits[::-1])
-
-    def flat(dp, mp):
-        return dp * n_mp + mp
-
-    token_out = []
-    token_in = []
-    for k in range(2):
-        pairs_out = []
-        for dp in range(n_dp):
-            for z in range(n_mp):
-                m = (k + z) % 2
-                dest = flat(2 * (dp // 2) + z // 2, 2 * m + dp % 2)
-                pairs_out.append((flat(dp, z), dest))
-        token_out.append(pairs_out)
-        token_in.append([(b, a) for a, b in pairs_out])
-    weight_out = []
-    weight_in = []
-    for k in range(n_mp):
-        pairs_out = []
-        for dp in range(n_dp):
-            for z in range(n_mp):
-                s = 2 * (z % 2) + dp % 2
-                pairs_out.append((flat(dp, z), flat(2 * (dp // 2) + z // 2, s ^ k)))
-        weight_out.append(pairs_out)
-        weight_in.append([(b, a) for a, b in pairs_out])
-    both = ("dp", "mp")
-
-    def swap(value):
-        return lax.ppermute(value, "dp", [(i, i ^ 1) for i in range(n_dp)])
-
-    def hop(value, bit):
-        return lax.ppermute(value, "dp", [(i, i ^ (2 * bit)) for i in range(n_dp)])
-
     def on_device(
         tokens,
         seg_ids,
@@ -732,96 +1162,7 @@
         branch_bias,
         out_grad,
     ):
-        dp = lax.axis_index("dp")
-        z = lax.axis_index("mp")
-        core = dp % 2
-        group = dp // 2
-        length = seg_ids.shape[1]
-        half = length // 2
-        quarter = length // n_mp
         width = tokens.shape[2]
-
-        def pick2(flag, first, second):
-            return jnp.where(flag == 0, first, second)
-
-        def to_rows(value):
-            got = []
-            for k in range(2):
-                mine = lax.dynamic_index_in_dim(value, (k + z) % 2, 0, keepdims=False)
-                got.append(lax.ppermute(mine, both, token_out[k]))
-            m = z // 2
-            stack = jnp.stack(got)
-            return jnp.concatenate(
-                [
-                    lax.dynamic_index_in_dim(stack, m, 0, keepdims=False),
-                    lax.dynamic_index_in_dim(stack, 1 - m, 0, keepdims=False),
-                ]
-            )
-
-        def from_rows(value):
-            parts = value.reshape(2, quarter, width)
-            m = z // 2
-            got = []
-            for k in range(2):
-                mine = lax.dynamic_index_in_dim(parts, (m + k) % 2, 0, keepdims=False)
-                got.append(lax.ppermute(mine, both, token_in[k]))
-            first = pick2(z % 2, got[0], got[1])
-            second = pick2(z % 2, got[1], got[0])
-            return first, second
-
-        def gather(block):
-            rows, columns = block.shape
-            got = [lax.ppermute(block, both, weight_out[k]) for k in range(n_mp)]
-            local = jnp.zeros((n_mp, rows, columns), block.dtype)
-            for k in range(n_mp):
-                local = lax.dynamic_update_slice(local, got[k][None], (z ^ k, 0, 0))
-            local = local.reshape(2, 1, 2 * rows, columns)
-            result = []
-            for i in range(2):
-                pieces = [(0, local[i])]
-                for bit in orders[i]:
-                    pieces = pieces + [(rel ^ bit, hop(piece, bit)) for rel, piece in pieces]
-                full = jnp.zeros((groups, 2 * rows, columns), block.dtype)
-                for rel, piece in pieces:
-                    full = lax.dynamic_update_slice(full, piece, (group ^ rel, 0, 0))
-                result.append(full.reshape(n_dp * rows, columns))
-            return result
-
-        def scatter(grads):
-            kept = []
-            for i in range(2):
-                total, columns = grads[i].shape
-                rows = total // n_dp
-                full = grads[i].astype(BF).reshape(groups, 2 * rows, columns)
-                pieces = {
-                    rel: lax.dynamic_index_in_dim(full, group ^ rel, 0, keepdims=False)
-                    for rel in range(groups)
-                }
-                for bit in orders[i][::-1]:
-                    keep = [rel for rel in pieces if not rel & bit]
-                    pieces = {
-                        rel: (
-                            pieces[rel].astype(F32) + hop(pieces[rel ^ bit], bit).astype(F32)
-                        ).astype(BF)
-                        for rel in keep
-                    }
-                kept.append(pieces[0].reshape(2, rows, columns))
-            local = jnp.concatenate(kept)
-            summed = None
-            for k in range(n_mp):
-                mine = lax.dynamic_index_in_dim(local, z ^ k, 0, keepdims=False)
-                got = lax.ppermute(mine, both, weight_in[k]).astype(F32)
-                summed = got if summed is None else summed + got
-            return summed
-
-        def share(mine):
-            other = swap(mine)
-            return jnp.concatenate([pick2(core, mine, other), pick2(core, other, mine)])
-
-        def reduce_half(partial):
-            theirs = lax.dynamic_slice_in_dim(partial, (1 - core) * half, half, 0)
-            ours = lax.dynamic_slice_in_dim(partial, core * half, half, 0)
-            return ours.astype(F32) + swap(theirs.astype(BF)).astype(F32)
 
         per_qv = qv_bias.shape[1]
         slim = width // n_dp
@@ -869,105 +1210,36 @@
             seg_ids,
             [small, block_qkv, out_weight, up_weight, down_weight],
         )
-        x = x.astype(F32)
-        grad_y = grad_y.astype(F32)
-        gains = vec[0:4]
-        unit0, inv0 = stats(x)
-        unit1, inv1 = stats(branch)
-        unit2, inv2 = stats(middle)
-        unit3, inv3 = stats(ffn_out)
-        layer_out = jnp.stack(from_rows(out_rows))
-
-        grad_f, dgain3, dshift3 = norm_back(unit3, inv3, gains[3], grad_y)
-        grad_f = grad_f.astype(BF)
-        dbranch1 = jnp.sum(grad_f.astype(F32), axis=0)
-        grad_f_all = share(grad_f)
-        dw_down = []
-        dw_up = []
-        dup = []
-        partial = None
-        for i in range(2):
-            dw_down.append(dot_tn(acts[i], grad_f_all))
-            grad_pre = (dot_nt(grad_f_all, w_down[i]) * slopes[i].astype(F32)).astype(BF)
-            dup.append(jnp.sum(grad_pre.astype(F32), axis=0))
-            dw_up.append(dot_tn(h2, grad_pre))
-            term = dot_nt(grad_pre, w_up[i])
-            partial = term if partial is None else partial + term
-        down_grad = scatter(dw_down)
-        up_grad = scatter(dw_up)
-        grad_h2 = reduce_half(partial)
-        back2, dgain2, dshift2 = norm_back(unit2, inv2, gains[2], grad_h2)
-        grad_mid = grad_y + back2
-        grad_a, dgain1, dshift1 = norm_back(unit1, inv1, gains[1], grad_mid)
-        grad_a = grad_a.astype(BF)
-        dbranch0 = jnp.sum(grad_a.astype(F32), axis=0)
-        grad_a_all = share(grad_a)
-        dw_out = []
-        dw_qkv = []
-        dqv = []
-        partial = None
-        for i in range(2):
-            dw_out.append(dot_tn(attended[i], grad_a_all))
-            grad_o = dot_nt(grad_a_all, w_out[i]).astype(BF)
-            grad_qkv = attend_backward(qkvs[i], grad_o, log_sums[i], count)
-            sums = jnp.sum(grad_qkv.astype(F32), axis=0)
-            dqv.append(jnp.stack([sums[:cols], sums[2 * cols :]]))
-            dw_qkv.append(dot_tn(h1, grad_qkv))
-            term = dot_nt(grad_qkv, w_qkv[i])
-            partial = term if partial is None else partial + term
-        out_grad_w = scatter(dw_out)
-        qkv_grad = scatter(dw_qkv)
-        grad_h1 = reduce_half(partial)
-        back0, dgain0, dshift0 = norm_back(unit0, inv0, gains[0], grad_h1)
-        input_grad = jnp.stack(from_rows((grad_mid + back0).astype(BF))).astype(F32)
-        qkv_grad = qkv_grad.reshape(qkv_weight.shape[1], 3, cols).transpose(1, 0, 2)
-
-        n_ff = up_bias.shape[0] * n_dp * n_mp
-        placed_up = lax.dynamic_update_slice(
-            jnp.zeros((n_ff,), F32), jnp.concatenate(dup), (core * (n_ff // 2),)
-        )
-        placed_qv = lax.dynamic_update_slice(
-            jnp.zeros((2, width), F32), jnp.concatenate(dqv, axis=1), (0, core * (width // 2))
-        )
-        vectors = jnp.concatenate(
-            [
-                jnp.stack(
-                    [
-                        dgain0,
-                        dgain1,
-                        dgain2,
-                        dgain3,
-                        dshift0,
-                        dshift1,
-                        dshift2,
-                        dshift3,
-                        dbranch0,
-                        dbranch1,
-                    ]
-                ),
-                placed_qv,
-                placed_up.reshape(-1, width),
-            ]
-        )
-        vectors = lax.psum(vectors, both)
-        mine = lax.dynamic_slice_in_dim(vectors[:10], dp * slim, slim, 1)
-        where_qv = (z * n_dp + dp) * per_qv
-        qv_grad = lax.dynamic_slice_in_dim(vectors[10:12], where_qv, per_qv, 1)
-        up_bias_grad = lax.dynamic_slice_in_dim(
-            vectors[12:].reshape(-1), (z * n_dp + dp) * up_bias.shape[0], up_bias.shape[0], 0
+        saved = [
+            out_rows,
+            grad_y,
+            x,
+            branch,
+            middle,
+            ffn_out,
+            h1,
+            qkvs,
+            attended,
+            log_sums,
+            h2,
+            acts,
+            slopes,
+        ]
+        layer_out, input_grad, qkv_grad, out_weight_grad, up_grad, down_grad, mine = backward_all(
+            n_dp, n_mp, saved, [w_qkv, w_out, w_up, w_down], vec, count
         )
         return (
             layer_out,
             input_grad,
-            qkv_grad,
-            qv_grad,
-            out_grad_w,
+            qkv_grad.reshape(qkv_weight.shape[1], 3, cols).transpose(1, 0, 2),
+            mine[0, : 2 * per_qv].reshape(2, per_qv),
+            out_weight_grad,
             up_grad,
-            up_bias_grad,
+            mine[1, : up_bias.shape[0]],
             down_grad,
-            mine[0:4],
-            mine[4:8],
-            mine[8:10],
+            mine[2:6, :slim],
+            mine[6:10, :slim],
+            mine[10:12, :slim],
         )
 
     return on_device

time: 589 us -> 367 us (0.62); the launches traced: 579 us -> 365 us
  waiting for transfers between devices: 195 us -> 0 us
  Pallas kernels: 163 us -> 345 us
  starting transfers between devices: 87.6 us -> 0 us
  other arithmetic: 45.5 us -> 0 us
  matrix products: 37.2 us -> 0 us
  local copies, waits for them, and re-layouts: 35.5 us -> 18.7 us
  between operations: 15.5 us -> 0.88 us
    pallas_call x2 -> x1, Pallas kernels: 29.9 us -> 200 us  [backward_all(): pl.pallas_call(functools.partial(backward_kernel, n_dp, n_mp), in_specs=[...]
    psum x1 -> x0, waiting for transfers between devices: 114 us -> none  [on_device(): vectors = lax.psum(vectors, both)]
    ppermute x48 -> x0, starting transfers between devices: 87.5 us -> none  [the longest x16 40.5 us: scatter(): got = lax.ppermute(mine, both, weight_in[k]).astype(F32)]
    ppermute x48 -> x0, waiting for transfers between devices: 80.2 us -> none  [the longest x24 46.9 us: hop(): return lax.ppermute(value, 'dp', [(i, i ^ 2 * bit) for i in range(n_dp)])]
    dot_general x16 -> x0, matrix products: 37.2 us -> none  [the longest x8 21.6 us: dot_tn(): lax.dot_general(a, b, (((0,), (0,)), ((), ())), preferred_element_type=F32)]
    reduce_sum x15 -> x0, other arithmetic: 19.3 us -> none  [the longest x4 8.86 us: norm_back(): return (grad_in, jnp.sum(grad * unit, axis=0), jnp.sum(grad, axis=0))]
    convert_element_type x18 -> x0, other arithmetic: 15.5 us -> none  [the longest x16 11.6 us: scatter(): pieces = {rel: (pieces[rel].astype(F32) + hop(pieces[rel ^ bit], bit).ast...]
    pallas_call x1, Pallas kernels: 133 us -> 146 us  [forward_all(): pl.pallas_call(functools.partial(forward_kernel, n_dp, n_mp), in_specs=[a...]
  transfers between devices with their start and end apart: 49 -> 0, of which waited for: 13 -> 0; matrix products, arithmetic and copies ran while one was open for 12% -> 0% of each run, Pallas kernels for 0% -> 0%
where the time goes in v4:
time: 367 us; the launch traced here: 365 us
  Pallas kernels  345 us (94%)
  local copies, waits for them, and re-layouts  18.7 us (5%)
    pallas_call x1, Pallas kernels, backward_all(): pl.pallas_call(functools.partial(backward_kernel, n_dp, n_mp), in_specs=[...  200 us
    pallas_call x1, Pallas kernels, forward_all(): pl.pallas_call(functools.partial(forward_kernel, n_dp, n_mp), in_specs=[a...  146 us
    unnamed x15, local copies, waits for them, and re-layouts  7.94 us

profile of v4, /device:TPU:1, one launch (start us, length us, event | category | flops | bytes accessed | tf_op | source)
XLA Modules:
  0.0 364.8 jit_solution(10702271698111495819)
XLA Ops:
  0.6 0.7 reshape.34
  1.4 2.2 concatenate.3
  3.6 0.6 pad.9.refs_3_
  4.2 1.1 copy.25
  5.3 0.8 copy.26.refs_4_
  6.1 145.5 %shard_map.203 = (bf16[544,1024]{1,0:T(8,128)(2,1)}, bf16[544,1024]{1,0:T(8,128)(2,1)}, bf16[1088,1024]{1,0:T(8,128)(2,1)}, bf16[2,1088,768]{2,1,0:T(8,128)(2,1)...) custom-call(bf16[2,272,1024]{2,1,0:T(8,128)(2,1)} %refs_0_.1, ...), custom_call_target="tpu_custom_call" | custom-call | tf_op jit(solution)/shard_map/pallas_call | solution.py:582
  151.6 199.6 %shard_map.204 = (bf16[2,272,1024]{2,1,0:T(8,128)(2,1)}, f32[2,272,1024]{2,1,0:T(8,128)}, f32[128,768]{1,0:T(8,128)}, f32[32,1024]{1,0:T(8,128)}, f32[128,1024]{...) custom-call(bf16[544,1024]{1,0:T(8,128)(2,1)} %get-tuple-element.37., ...), custom_call_target="tpu_custom_call" | custom-call | tf_op jit(solution)/shard_map/pallas_call | solution.py:1103
  351.3 0.0 copy-start
  351.3 1.3 slice_bitcast_fusion
  352.6 0.7 slice_reduce_fusion
  353.3 0.6 reshape_squeeze.3
  354.0 1.2 slice.19
  355.2 1.3 fusion
  356.6 1.1 copy.27
  357.7 0.9 copy.28
  358.6 2.3 copy.34
  361.0 0.0 copy-done
  361.0 0.0 copy-start.3
  361.0 0.0 copy-start.2
  361.0 0.0 copy-start.1
  361.0 1.4 copy.35
  362.3 0.0 copy-done.3
  362.3 0.7 copy.36
  363.0 0.0 copy-done.2
  363.0 0.8 copy.37
  363.8 0.0 copy-done.1
  363.8 0.8 copy.38
  (1 shorter events, 0.0 us)
Async XLA Ops:
  351.3 9.7 %copy-start = (f32[2,272,1024]{2,1,0:T(8,128)S(1)}, f32[2,272,1024]{2,1,0:T(8,128)}, u32[]{:S(2)}) copy-start(f32[2,272,1024]{2,1,0:T(8,128)} %get-tuple-element.88) | copy-start | bytes 6684676
  361.0 1.4 copy-start.3
  361.0 2.0 copy-start.2
  361.0 2.8 copy-start.1
